TPU v7x, 256 devices: a whole 4x4x8 slice. The times are simulated.
256 devices in a mesh: layer: 4 (over x_lo, core), row: 64 (over y, z, x_hi).
Axes of the slice: x: 4 (x_hi: 2, x_lo: 2; x = x_hi * 2 + x_lo), y: 4, z: 8, core: 2. Of those that a mesh axis runs over, the one named last changes fastest.
Arguments:
- density: bfloat16 [40960, 2048], P('row', 'layer'), may hold values from -1 to 1, as said below
- pattern: int32 [640, 32], P('row', 'layer'), may hold values 0 or 1
Outputs:
- purified: float32 [40960, 2048], P('row', 'layer')
Inputs may be any that keep to these rules, and one draw needn't show every extreme that they name: `density`: entry (r, o * 64 + c) is P's entry in row r and column ((r // 64 + o - 16) mod 640) * 64 + c.
All inputs are finite; a program needn't handle non-finite values. No bound on the sum of `pattern` on one device may be relied on, other than what follows from the above.
Results may differ from a plain program's by a relative error of at most 0.0065.
Values may be sent and summed in bfloat16 or wider, within the bound.
A program may use at most 192 MiB of HBM per device.

v0:
```python
import jax
import jax.numpy as jnp
from jax import lax
from jax.sharding import PartitionSpec as P


def shifted(value, axis, steps):
    count = lax.axis_size(axis)
    pairs = [(source, (source + steps) % count) for source in range(count)]
    return lax.ppermute(value, axis, pairs)


def body(density, pattern):
    rows_dev, slab_cols = density.shape
    block_rows, slab_offsets = pattern.shape
    tile_size = rows_dev // block_rows
    layers = lax.axis_size("layer")
    offsets = slab_offsets * layers
    half_band = offsets // 2
    reach_dev = (half_band + block_rows - 1) // block_rows
    layer_id = lax.axis_index("layer")
    keep = pattern.astype(jnp.bfloat16)[:, None, :, None]
    masked = (density.reshape(block_rows, tile_size, slab_offsets, tile_size) * keep).reshape(
        rows_dev, slab_cols
    )
    own_band = lax.all_gather(masked, "layer", axis=1, tiled=True)
    lower_parts = [shifted(own_band, "row", distance) for distance in range(reach_dev, 0, -1)]
    upper_parts = [shifted(own_band, "row", -distance) for distance in range(1, reach_dev + 1)]
    margin = jnp.concatenate(lower_parts + [own_band] + upper_parts, axis=0)
    padded = jnp.pad(
        margin.reshape(-1, tile_size, offsets, tile_size),
        ((0, 0), (0, 0), (half_band, half_band), (0, 0)),
    )
    row_base = reach_dev * block_rows - half_band
    own_start = reach_dev * rows_dev
    own_blocks = lax.slice_in_dim(margin, own_start, own_start + rows_dev, axis=0).reshape(
        block_rows, tile_size, offsets, tile_size
    )
    pattern_f = pattern.astype(jnp.float32)[:, None, :, None]
    row_ids = jnp.arange(block_rows, dtype=jnp.int32)

    def row_product(left_row, inner_count, first_offset, row_idx):

        def piece(inner_idx):
            start_row = row_base + row_idx + inner_idx
            start_col = first_offset - inner_idx + 2 * half_band
            return lax.dynamic_slice(
                padded, (start_row, 0, start_col, 0), (1, tile_size, slab_offsets, tile_size)
            )[0]

        inner_set = jnp.arange(inner_count, dtype=jnp.int32)
        windows = jax.vmap(piece)(inner_set)
        return jnp.einsum("xay,ayoz->xoz", left_row, windows, preferred_element_type=jnp.float32)

    def products(left_blocks):
        first_offset = layer_id * slab_offsets
        return lax.map(
            lambda row_idx: row_product(left_blocks[row_idx], offsets, first_offset, row_idx),
            row_ids,
        )

    square = (products(own_blocks) * pattern_f).astype(jnp.bfloat16)
    square_full = lax.all_gather(square.reshape(rows_dev, slab_cols), "layer", axis=1, tiled=True)
    cubic = products(square_full.reshape(block_rows, tile_size, offsets, tile_size)) * pattern_f
    purified = 3.0 * square.astype(jnp.float32) - 2.0 * cubic
    return purified.reshape(rows_dev, slab_cols)


def solution(mesh):
    placed = (P("row", "layer"), P("row", "layer"))
    return jax.shard_map(
        body, mesh=mesh, in_specs=placed, out_specs=P("row", "layer"), check_vma=False
    )
```

profile of v0, /device:TPU:1, one launch (start us, length us, event | category | flops | bytes accessed | tf_op | source)
XLA Modules:
  0.0 635.8 jit_solution(86129406533818942)
XLA Ops:
  9.5 40.3 %all-gather.3.cloned.1.call-done = bf16[640,2048]{1,0:T(8,128)(2,1)} async-done(((bf16[640,512]{1,0:T(8,128)(2,1)}), bf16[640,2048]{1,0:T(8,128)(2,1)}) %all-gather.3.cloned.1.call-update) | async-done | bytes 2621456 | tf_op jit(solution)/shard_map/all_gather | solution.py:26
  53.5 4.8 collective-permute-start.2
  59.0 8.5 %reshape.90 = bf16[10,64,32,64]{3,2,1,0:T(8,128)(2,1)} reshape(bf16[640,2048]{1,0:T(8,128)(2,1)} %all-gather.3.cloned.1.call-done) | data formatting | bytes 5242880 | tf_op jit(solution)/shard_map/reshape | solution.py:36
  67.6 45.1 %collective-permute-done = bf16[640,2048]{1,0:T(8,128)(2,1)} collective-permute-done((bf16[640,2048]{1,0:T(8,128)(2,1)}, bf16[640,2048]{1,0:T(8,128)(2,1)}, u32[]{:S(2)}, u32[]{:S(2)}) %collective-permute-start) | collective-permute-done | bytes 2621472 | tf_op jit(solution)/shard_map/ppermute | solution.py:10
  112.6 3.5 constant_dynamic-update-slice_fusion.4
  116.2 54.8 %collective-permute-done.1 = bf16[640,2048]{1,0:T(8,128)(2,1)} collective-permute-done((bf16[640,2048]{1,0:T(8,128)(2,1)}, bf16[640,2048]{1,0:T(8,128)(2,1)}, u32[]{:S(2)}, u32[]{:S(2)}) %collective-permute-start.1) | collective-permute-done | bytes 2621472 | tf_op jit(solution)/shard_map/ppermute | solution.py:10
  171.0 3.6 constant_dynamic-update-slice_fusion.3
  176.4 3.5 constant_dynamic-update-slice_fusion.1
  179.9 37.8 %collective-permute-done.3 = bf16[640,2048]{1,0:T(8,128)(2,1)S(1)} collective-permute-done((bf16[640,2048]{1,0:T(8,128)(2,1)}, bf16[640,2048]{1,0:T(8,128)(2,1)S(1)}, u32[]{:S(2)}, u32[]{:S(2)}) %collective-permute-start.3) | collective-permute-done | bytes 2621472 | tf_op jit(solution)/shard_map/ppermute | solution.py:10
  219.3 37.5 %reshape.91 = bf16[50,64,32,64]{3,2,1,0:T(8,128)(2,1)} reshape(bf16[3200,2048]{1,0:T(8,128)(2,1)} %constant_dynamic-update-slice_fusion) | data formatting | bytes 26214400 | tf_op jit(solution)/shard_map/reshape | solution.py:31
  256.8 18.8 %copy.22 = bf16[50,64,32,64]{3,1,0,2:T(8,128)(2,1)} copy(bf16[50,64,32,64]{3,2,1,0:T(8,128)(2,1)} %reshape.91) | data formatting | bytes 26214400
  275.7 25.0 %pad.4.clone = bf16[50,64,64,64]{3,1,0,2:T(8,128)(2,1)} pad(bf16[50,64,32,64]{3,1,0,2:T(8,128)(2,1)} %copy.22, bf16[]{:T(256)} %constant.104.clone.1), padding=0_0x0_0x16_16x0_0 | pad | bytes 39321600 | tf_op jit(solution)/shard_map/jit(_pad)/pad | solution.py:30
  300.9 127.8 %while.24 = (s32[]{:T(128)}, f32[10,64,8,64]{3,1,2,0:T(8,128)S(1)}, s32[10]{0:T(128)S(1)}, bf16[10,64,32,64]{3,2,1,0:T(8,128)(2,1)}, s32[]{:T(128)}, /*index=5*/...) while((s32[]{:T(128)}, f32[10,64,8,64]{3,1,2,0:T(8,128)S(1)}, ...), condition=%wide.region_1.2_spmd, body=%wide.region_0.1_spmd.sunk | while | flops 134218176 | bytes 7602991 | solution.py:57
  305.5 5.1 gather_fusion
  318.3 5.1 gather_fusion
  323.3 3.2 fusion.30
  331.0 5.1 gather_fusion
  343.8 5.1 gather_fusion
  348.9 3.2 fusion.30
  356.6 5.1 gather_fusion
  369.4 5.1 gather_fusion
  382.1 5.1 gather_fusion
  394.9 5.1 gather_fusion
  407.7 5.1 gather_fusion
  420.5 5.1 gather_fusion
  433.8 44.1 %all-gather.5.cloned.1.call-done = bf16[640,2048]{1,0:T(8,128)(2,1)} async-done(((bf16[640,512]{1,0:T(8,128)(2,1)}), bf16[640,2048]{1,0:T(8,128)(2,1)}) %all-gather.5.cloned.1.call-update) | async-done | bytes 2621456 | tf_op jit(solution)/shard_map/all_gather | solution.py:63
  477.9 8.5 %reshape.93 = bf16[10,64,32,64]{3,2,1,0:T(8,128)(2,1)} reshape(bf16[640,2048]{1,0:T(8,128)(2,1)} %all-gather.5.cloned.1.call-done) | data formatting | bytes 5242880 | tf_op jit(solution)/shard_map/reshape | solution.py:64
  488.3 135.1 %while.25 = (s32[]{:T(128)}, f32[10,64,8,64]{3,1,2,0:T(8,128)}, s32[10]{0:T(128)S(1)}, bf16[10,64,32,64]{3,2,1,0:T(8,128)(2,1)}, s32[]{:T(128)}, /*index=5*/bf16...) while((s32[]{:T(128)}, f32[10,64,8,64]{3,1,2,0:T(8,128)}, s32[10]{0:T(128)S(1)}, ...), condition=%wide.region_3.4_spmd, body=%wide.region_2.3_spmd.sunk | while | flops 134218176 | bytes 9438507 | solution.py:57
  492.9 5.1 gather_fusion.1
  498.0 3.9 fusion.34
  506.4 5.1 gather_fusion.1
  511.5 3.9 fusion.34
  519.9 5.1 gather_fusion.1
  525.0 3.9 fusion.34
  533.4 5.1 gather_fusion.1
  538.5 3.9 fusion.34
  546.9 5.1 gather_fusion.1
  552.0 3.9 fusion.34
  560.4 5.1 gather_fusion.1
  565.5 3.9 fusion.34
  573.9 5.1 gather_fusion.1
  579.0 3.9 fusion.34
  587.4 5.1 gather_fusion.1
  592.5 3.9 fusion.34
  600.9 5.1 gather_fusion.1
  606.0 3.9 fusion.34
  614.4 5.1 gather_fusion.1
  619.5 3.9 fusion.34
  (98 shorter events, 84.0 us)
Async XLA Ops:
  6.5 1.9 copy-start.1
  6.5 43.3 %all-gather.3.cloned.1.call-start = ((), (), s32[]{:S(2)}) async-start(), calls=%async_computation | async-start | bytes 3276800 | tf_op jit(solution)/shard_map/all_gather | solution.py:26
  9.5 468.5 %all-gather.5.cloned.1.call-start = ((), (), s32[]{:S(2)}) async-start(), calls=%async_computation.1 | async-start | bytes 3276800 | tf_op jit(solution)/shard_map/all_gather | solution.py:63
  49.9 62.8 %collective-permute-start = (bf16[640,2048]{1,0:T(8,128)(2,1)}, bf16[640,2048]{1,0:T(8,128)(2,1)}, u32[]{:S(2)}, u32[]{:S(2)}) collective-permute-start(bf16[640,2048]{1,0:T(8,128)(2,1)} %all-gather.3.cloned.1.call-done), channel_id=1, source_target_pairs={{0,2},{1,3},{2,4},{3,5},{4,6},{5,7},{6,8},{7,9},{8,10},{9,11},{10,... | collective-permute-start | bytes 7864328 | tf_op jit(solution)/shard_map/ppermute | solution.py:10
  51.1 119.8 %collective-permute-start.1 = (bf16[640,2048]{1,0:T(8,128)(2,1)}, bf16[640,2048]{1,0:T(8,128)(2,1)}, u32[]{:S(2)}, u32[]{:S(2)}) collective-permute-start(bf16[640,2048]{1,0:T(8,128)(2,1)} %all-gather.3.cloned.1.call-done), channel_id=1, source_target_pairs={{0,1},{1,2},{2,3},{3,4},{4,5},{5,6},{6,7},{7,8},{8,9},{9,10},{10,1... | collective-permute-start | bytes 7864328 | tf_op jit(solution)/shard_map/ppermute | solution.py:10
  53.5 122.8 %collective-permute-start.2 = (bf16[640,2048]{1,0:T(8,128)(2,1)}, bf16[640,2048]{1,0:T(8,128)(2,1)}, u32[]{:S(2)}, u32[]{:S(2)}) collective-permute-start(bf16[640,2048]{1,0:T(8,128)(2,1)} %all-gather.3.cloned.1.call-done), channel_id=1, source_target_pairs={{0,63},{1,0},{2,1},{3,2},{4,3},{5,4},{6,5},{7,6},{8,7},{9,8},{10,9... | collective-permute-start | bytes 7864328 | tf_op jit(solution)/shard_map/ppermute | solution.py:10
  58.3 159.4 %collective-permute-start.3 = (bf16[640,2048]{1,0:T(8,128)(2,1)}, bf16[640,2048]{1,0:T(8,128)(2,1)S(1)}, u32[]{:S(2)}, u32[]{:S(2)}) collective-permute-start(bf16[640,2048]{1,0:T(8,128)(2,1)} %all-gather.3.cloned.1.call-done), channel_id=1, source_target_pairs={{0,62},{1,63},{2,0},{3,1},{4,2},{5,3},{6,4},{7,5},{8,6},{9,7},{10,... | collective-permute-start | bytes 7864328 | tf_op jit(solution)/shard_map/ppermute | solution.py:10
  116.2 58.4 %copy-start = (bf16[640,2048]{1,0:T(8,128)(2,1)S(1)}, bf16[640,2048]{1,0:T(8,128)(2,1)}, u32[]{:S(2)}) copy-start(bf16[640,2048]{1,0:T(8,128)(2,1)} %all-gather.3.cloned.1.call-done) | copy-start | bytes 7864324
Sparse Core Ops, SparseCore 0:
  9.6 40.2 all-gather.2
  434.0 43.9 all-gather.4
where the time goes:
time: 640 us; the launch traced here: 636 us
  local copies, waits for them, and re-layouts  260 us (41%)
  waiting for transfers between devices  222 us (35%)
  matrix products  70.5 us (11%)
  loops' own time  55.6 us (9%)
  between operations  13.5 us (2%)
  starting transfers between devices  9.13 us (1%)
    ppermute x4, waiting for transfers between devices, shifted(): return lax.ppermute(value, axis, pairs)  138 us
    gather x20, local copies, waits for them, and re-layouts, piece(): lax.dynamic_slice(padded, (start_row, 0, start_col, 0), (1, tile_size, sl...  102 us
    dot_general x20, matrix products, row_product(): jnp.einsum('xay,ayoz->xoz', left_row, windows, preferred_element_type=jnp...  70.5 us
    another operation x2, loops' own time, products(): lax.map(lambda row_idx: row_product(left_blocks[row_idx], offsets, first_...  55.6 us
    all_gather x1, waiting for transfers between devices, body(): lax.all_gather(square.reshape(rows_dev, slab_cols), 'layer', axis=1, tile...  44.1 us
    all_gather x1, waiting for transfers between devices, body(): own_band = lax.all_gather(masked, 'layer', axis=1, tiled=True)  40.3 us
    reshape x1, local copies, waits for them, and re-layouts, body(): margin.reshape(-1, tile_size, offsets, tile_size)  37.5 us
    unnamed x9, local copies, waits for them, and re-layouts  31.3 us
  transfers between devices with their start and end apart: 6, of which 5 were waited for; matrix products, arithmetic and copies ran while one was open for 3% of the time, Pallas kernels for 0%

commit v1 on v0

v1 whole, which is shorter than its diff:
```python
import jax
import jax.numpy as jnp
from jax import lax
from jax.sharding import PartitionSpec as P


def shifted(value, axis, steps):
    count = lax.axis_size(axis)
    pairs = [(source, (source + steps) % count) for source in range(count)]
    return lax.ppermute(value, axis, pairs)


def skew_rows(band, shift_total):
    n, bs, width = band.shape
    pieces = [
        jnp.pad(band[i], ((0, 0), (i * bs, (shift_total - i) * bs))) for i in range(n)
    ]
    return jnp.stack(pieces, axis=0)


def body(density, pattern):
    rows_dev, slab_cols = density.shape
    block_rows, slab_offsets = pattern.shape
    bs = rows_dev // block_rows
    layers = lax.axis_size("layer")
    offsets = slab_offsets * layers
    half = offsets // 2
    layer_id = lax.axis_index("layer")

    keep = pattern.astype(jnp.bfloat16)[:, None, :, None]
    masked = (density.reshape(block_rows, bs, slab_offsets, bs) * keep).reshape(rows_dev, slab_cols)
    own_band = lax.all_gather(masked, "layer", axis=1, tiled=True)

    total_rows = block_rows + offsets - 1
    below = half
    above = total_rows - half - block_rows
    lower_parts = []
    dist = 1
    need = below
    while need > 0:
        take = min(block_rows, need)
        lower_parts.insert(0, shifted(own_band[(block_rows - take) * bs:], "row", dist))
        need -= take
        dist += 1
    upper_parts = []
    dist = 1
    need = above
    while need > 0:
        take = min(block_rows, need)
        upper_parts.append(shifted(own_band[: take * bs], "row", -dist))
        need -= take
        dist += 1
    halo = jnp.concatenate(lower_parts + [own_band] + upper_parts, axis=0)
    halo = halo.reshape(total_rows, bs, offsets * bs)

    width = slab_offsets + block_rows - 1
    pad_l = total_rows - 1 - half
    pad_r = max(0, slab_offsets * (layers - 1) + half + width - offsets)
    halo_pad = jnp.pad(halo, ((0, 0), (0, 0), (pad_l * bs, pad_r * bs)))
    base = layer_id * slab_offsets
    right_rows = []
    for t in range(total_rows):
        start = (base + (half + pad_l - t)) * bs
        right_rows.append(lax.dynamic_slice_in_dim(halo_pad[t], start, width * bs, axis=1))
    right = jnp.stack(right_rows, axis=0).reshape(total_rows * bs, width * bs)

    pattern_f = pattern.astype(jnp.float32)[:, None, :, None]

    def product(left_band):
        left = skew_rows(left_band.reshape(block_rows, bs, offsets * bs), block_rows - 1)
        left = left.reshape(rows_dev, total_rows * bs)
        dense = jnp.dot(left, right, preferred_element_type=jnp.float32)
        dense = dense.reshape(block_rows, bs, width * bs)
        out = jnp.stack(
            [dense[i, :, i * bs: (i + slab_offsets) * bs] for i in range(block_rows)], axis=0
        )
        return out.reshape(block_rows, bs, slab_offsets, bs) * pattern_f

    square = product(own_band).astype(jnp.bfloat16)
    square_full = lax.all_gather(square.reshape(rows_dev, slab_cols), "layer", axis=1, tiled=True)
    cubic = product(square_full)
    purified = 3.0 * square.astype(jnp.float32) - 2.0 * cubic
    return purified.reshape(rows_dev, slab_cols)


def solution(mesh):
    placed = (P("row", "layer"), P("row", "layer"))
    return jax.shard_map(
        body, mesh=mesh, in_specs=placed, out_specs=P("row", "layer"), check_vma=False
    )
```

time: 640 us -> 256 us (0.40)
  local copies, waits for them, and re-layouts: 260 us -> 33.1 us
  matrix products: 70.5 us -> 12.4 us
  loops' own time: 55.6 us -> 0 us
  waiting for transfers between devices: 222 us -> 178 us
    gather x20 -> x0, local copies, waits for them, and re-layouts: 102 us -> none  [piece(): lax.dynamic_slice(padded, (start_row, 0, start_col, 0), (1, tile_size, sl...]
    reshape x5 -> x0, local copies, waits for them, and re-layouts: 59 us -> none  [the longest x1 37.5 us: body(): margin.reshape(-1, tile_size, offsets, tile_size)]
    dot_general x20 -> x2, matrix products: 70.5 us -> 12.4 us  [product(): dense = jnp.dot(left, right, preferred_element_type=jnp.float32)]
    another operation x2 -> x0, loops' own time: 55.6 us -> none  [products(): lax.map(lambda row_idx: row_product(left_blocks[row_idx], offsets, first_...]
    dynamic_slice x40 -> x0, local copies, waits for them, and re-layouts: 34.8 us -> none  [the longest x20 21.6 us: products(): left_blocks[row_idx]]
    ppermute x4, waiting for transfers between devices: 138 us -> 108 us  [shifted(): return lax.ppermute(value, axis, pairs)]
    pad x1 -> x0, local copies, waits for them, and re-layouts: 25 us -> none  [body(): jnp.pad(margin.reshape(-1, tile_size, offsets, tile_size), ((0, 0), (0, 0...]
    unnamed x9 -> x90, local copies, waits for them, and re-layouts: 31.3 us -> 17.4 us
where the time goes in v1:
time: 256 us
  waiting for transfers between devices  178 us (70%)
  local copies, waits for them, and re-layouts  33.1 us (13%)
  between operations  14.2 us (6%)
  starting transfers between devices  12.7 us (5%)
  matrix products  12.4 us (5%)
  other arithmetic  5.45 us (2%)
    ppermute x4, waiting for transfers between devices, shifted(): return lax.ppermute(value, axis, pairs)  108 us
    all_gather x1, waiting for transfers between devices, body(): own_band = lax.all_gather(masked, 'layer', axis=1, tiled=True)  36.4 us
    all_gather x1, waiting for transfers between devices, body(): lax.all_gather(square.reshape(rows_dev, slab_cols), 'layer', axis=1, tile...  34 us
    unnamed x90, local copies, waits for them, and re-layouts  17.4 us
    ppermute x4, starting transfers between devices, shifted(): return lax.ppermute(value, axis, pairs)  12.6 us
    dot_general x2, matrix products, product(): dense = jnp.dot(left, right, preferred_element_type=jnp.float32)  12.4 us
  transfers between devices with their start and end apart: 6, of which 5 were waited for; matrix products, arithmetic and copies ran while one was open for 3% of the time, Pallas kernels for 0%

profile of v1, /device:TPU:1, one launch (start us, length us, event | category | flops | bytes accessed | tf_op | source)
XLA Modules:
  0.0 255.7 jit_solution(16746198936358606509)
XLA Ops:
  6.5 0.8 fusion.5
  7.4 0.3 mul.170
  7.6 0.8 mul.171
  8.4 2.1 mul.172
  10.7 1.8 mul.215
  12.5 2.0 mul.216
  14.6 36.4 %all-gather.3.cloned.1.call-done = bf16[640,2048]{1,0:T(8,128)(2,1)} async-done(((bf16[640,512]{1,0:T(8,128)(2,1)}), bf16[640,2048]{1,0:T(8,128)(2,1)}) %all-gather.3.cloned.1.call-update) | async-done | bytes 2621456 | tf_op jit(solution)/shard_map/all_gather | solution.py:32
  50.9 1.7 slice.362
  52.6 1.4 collective-permute-start
  53.9 1.4 slice.363
  55.4 4.0 %collective-permute-start.3 = (bf16[320,2048]{1,0:T(8,128)(2,1)S(1)}, bf16[320,2048]{1,0:T(8,128)(2,1)S(1)}, u32[]{:S(2)}, u32[]{:S(2)}) collective-permute-start(bf16[320,2048]{1,0:T(8,128)(2,1)S(1)} %slice.363), channel_id=1, source_target_pairs={{0,62},{1,63},{2,0},{3,1},{4,2},{5,3},{6,4},{7,5},{8,6},{9,7},{10,... | collective-permute-start | bytes 3932168 | tf_op jit(solution)/shard_map/ppermute | solution.py:10
  59.4 0.2 fusion.4
  59.7 0.1 bitcast_dynamic-update-slice_fusion.18
  59.9 2.5 collective-permute-start.1
  62.4 4.8 %collective-permute-start.2 = (bf16[640,2048]{1,0:T(8,128)(2,1)S(1)}, bf16[640,2048]{1,0:T(8,128)(2,1)S(1)}, u32[]{:S(2)}, u32[]{:S(2)}) collective-permute-start(bf16[640,2048]{1,0:T(8,128)(2,1)S(1)} %copy-done), channel_id=1, source_target_pairs={{0,63},{1,0},{2,1},{3,2},{4,3},{5,4},{6,5},{7,6},{8,7},{9,8},{10,9... | collective-permute-start | bytes 7864328 | tf_op jit(solution)/shard_map/ppermute | solution.py:10
  67.2 0.1 bitcast_dynamic-update-slice_fusion.16
  67.3 0.1 bitcast_dynamic-update-slice_fusion.14
  67.5 0.1 bitcast_dynamic-update-slice_fusion.12
  67.7 0.1 bitcast_dynamic-update-slice_fusion.10
  67.9 1.8 copy-done.2
  69.7 23.0 %collective-permute-done = bf16[384,2048]{1,0:T(8,128)(2,1)S(1)} collective-permute-done((bf16[384,2048]{1,0:T(8,128)(2,1)S(1)}, bf16[384,2048]{1,0:T(8,128)(2,1)S(1)}, u32[]{:S(2)}, u32[]{:S(2)}) %collective-permute-start) | collective-permute-done | bytes 1572896 | tf_op jit(solution)/shard_map/ppermute | solution.py:10
  92.8 81.8 %collective-permute-done.1 = bf16[640,2048]{1,0:T(8,128)(2,1)S(1)} collective-permute-done((bf16[640,2048]{1,0:T(8,128)(2,1)S(1)}, bf16[640,2048]{1,0:T(8,128)(2,1)S(1)}, u32[]{:S(2)}, u32[]{:S(2)}) %collective-permute-start.1) | collective-permute-done | bytes 2621472 | tf_op jit(solution)/shard_map/ppermute | solution.py:10
  174.6 0.3 constant_dynamic-update-slice_fusion.3
  174.9 0.3 constant_dynamic-update-slice_fusion.2
  175.2 2.7 %collective-permute-done.2 = bf16[640,2048]{1,0:T(8,128)(2,1)S(1)} collective-permute-done((bf16[640,2048]{1,0:T(8,128)(2,1)S(1)}, bf16[640,2048]{1,0:T(8,128)(2,1)S(1)}, u32[]{:S(2)}, u32[]{:S(2)}) %collective-permute-start.2) | collective-permute-done | bytes 2621472 | tf_op jit(solution)/shard_map/ppermute | solution.py:10
  177.9 0.3 constant_dynamic-update-slice_fusion.1
  178.4 1.0 pad_slice_fusion.2
  179.4 2.4 pad_slice_fusion
  181.8 1.4 pad_slice_fusion.1
  183.2 1.2 constant_dynamic-update-slice_fusion.45
  184.4 1.0 constant_dynamic-update-slice_fusion.44
  185.4 1.0 constant_dynamic-update-slice_fusion.43
  186.5 1.0 constant_dynamic-update-slice_fusion.42
  187.5 1.0 constant_dynamic-update-slice_fusion.41
  188.6 1.0 constant_dynamic-update-slice_fusion.40
  189.6 1.0 constant_dynamic-update-slice_fusion.39
  190.6 1.0 constant_dynamic-update-slice_fusion.38
  195.9 4.8 %fusion.6 = f32[10,64,1088]{2,1,0:T(8,128)S(1)} fusion(bf16[10,64,2624]{2,1,0:T(8,128)(2,1)S(1)} %copy-done.3, bf16[2624,1088,1]{1,0,2:T(8,128)(2,1)S(1)} %bitcast.66), kind=kOutput, calls=%fused_computation.135 | convolution fusion | flops 3654287360 | bytes 11853824 | tf_op jit(solution)/shard_map/dot_general | solution.py:72
  201.3 1.2 fusion.2
  202.5 34.0 %all-gather.5.cloned.1.call-done = bf16[640,2048]{1,0:T(8,128)(2,1)} async-done(((bf16[640,512]{1,0:T(8,128)(2,1)}), bf16[640,2048]{1,0:T(8,128)(2,1)}) %all-gather.5.cloned.1.call-update) | async-done | bytes 2621456 | tf_op jit(solution)/shard_map/all_gather | solution.py:80
  236.5 1.8 fusion.3
  238.3 0.1 bitcast_dynamic-update-slice_fusion.8
  238.5 0.1 bitcast_dynamic-update-slice_fusion.6
  238.7 0.1 bitcast_dynamic-update-slice_fusion.4
  238.9 0.1 bitcast_dynamic-update-slice_fusion.2
  239.1 0.1 bitcast_dynamic-update-slice_fusion
  239.3 7.6 %fusion.7 = f32[10,64,1088]{2,1,0:T(8,128)S(1)} fusion(bf16[10,64,2624]{2,1,0:T(8,128)(2,1)S(1)} %bitcast_dynamic-update-slice_fusion, bf16[2624,1088,1]{1,0,2:T(8,128)(2,1)} %bitcast.67), kind=kOutput, calls=%fused_computation.136 | convolution fusion | flops 3654287360 | bytes 11853824 | tf_op jit(solution)/shard_map/dot_general | solution.py:72
  247.5 1.4 fusion.1
  (81 shorter events, 5.7 us)
Async XLA Ops:
  6.5 44.4 %all-gather.3.cloned.1.call-start = ((), (), s32[]{:S(2)}) async-start(), calls=%async_computation | async-start | bytes 3276800 | tf_op jit(solution)/shard_map/all_gather | solution.py:32
  10.5 225.9 %all-gather.5.cloned.1.call-start = ((), (), s32[]{:S(2)}) async-start(), calls=%async_computation.1 | async-start | bytes 3276800 | tf_op jit(solution)/shard_map/all_gather | solution.py:80
  50.9 8.5 %copy-start = (bf16[640,2048]{1,0:T(8,128)(2,1)S(1)}, bf16[640,2048]{1,0:T(8,128)(2,1)}, u32[]{:S(2)}) copy-start(bf16[640,2048]{1,0:T(8,128)(2,1)} %all-gather.3.cloned.1.call-done) | copy-start | bytes 7864324
  52.6 40.1 %collective-permute-start = (bf16[384,2048]{1,0:T(8,128)(2,1)S(1)}, bf16[384,2048]{1,0:T(8,128)(2,1)S(1)}, u32[]{:S(2)}, u32[]{:S(2)}) collective-permute-start(bf16[384,2048]{1,0:T(8,128)(2,1)S(1)} %slice.362), channel_id=1, source_target_pairs={{0,2},{1,3},{2,4},{3,5},{4,6},{5,7},{6,8},{7,9},{8,10},{9,11},{10,... | collective-permute-start | bytes 4718600 | tf_op jit(solution)/shard_map/ppermute | solution.py:10
  55.4 122.9 %collective-permute-start.3 = (bf16[320,2048]{1,0:T(8,128)(2,1)S(1)}, bf16[320,2048]{1,0:T(8,128)(2,1)S(1)}, u32[]{:S(2)}, u32[]{:S(2)}) collective-permute-start(bf16[320,2048]{1,0:T(8,128)(2,1)S(1)} %slice.363), channel_id=1, source_target_pairs={{0,62},{1,63},{2,0},{3,1},{4,2},{5,3},{6,4},{7,5},{8,6},{9,7},{10,... | collective-permute-start | bytes 3932168 | tf_op jit(solution)/shard_map/ppermute | solution.py:10
  59.9 114.7 %collective-permute-start.1 = (bf16[640,2048]{1,0:T(8,128)(2,1)S(1)}, bf16[640,2048]{1,0:T(8,128)(2,1)S(1)}, u32[]{:S(2)}, u32[]{:S(2)}) collective-permute-start(bf16[640,2048]{1,0:T(8,128)(2,1)S(1)} %copy-done), channel_id=1, source_target_pairs={{0,1},{1,2},{2,3},{3,4},{4,5},{5,6},{6,7},{7,8},{8,9},{9,10},{10,1... | collective-permute-start | bytes 7864328 | tf_op jit(solution)/shard_map/ppermute | solution.py:10
  62.4 115.6 %collective-permute-start.2 = (bf16[640,2048]{1,0:T(8,128)(2,1)S(1)}, bf16[640,2048]{1,0:T(8,128)(2,1)S(1)}, u32[]{:S(2)}, u32[]{:S(2)}) collective-permute-start(bf16[640,2048]{1,0:T(8,128)(2,1)S(1)} %copy-done), channel_id=1, source_target_pairs={{0,63},{1,0},{2,1},{3,2},{4,3},{5,4},{6,5},{7,6},{8,7},{9,8},{10,9... | collective-permute-start | bytes 7864328 | tf_op jit(solution)/shard_map/ppermute | solution.py:10
  67.9 1.8 copy-start.2
  183.2 12.7 %copy-start.3 = (bf16[10,64,2624]{2,1,0:T(8,128)(2,1)S(1)}, bf16[10,64,2624]{2,1,0:T(8,128)(2,1)}, u32[]{:S(2)}) copy-start(bf16[10,64,2624]{2,1,0:T(8,128)(2,1)} %copy-done.2) | copy-start | bytes 10076164
  195.8 4.8 %copy-start.4 = (bf16[41,64,1088]{2,1,0:T(8,128)(2,1)}, bf16[41,64,1088]{2,1,0:T(8,128)(2,1)S(1)}, u32[]{:S(2)}) copy-start(bf16[41,64,1088]{2,1,0:T(8,128)(2,1)S(1)} %constant_dynamic-update-slice_fusion.5) | copy-start | bytes 17129476
  239.2 8.2 %copy-start.1 = (bf16[640,512]{1,0:T(8,128)(2,1)S(1)}, bf16[640,512]{1,0:T(8,128)(2,1)}, u32[]{:S(2)}) copy-start(bf16[640,512]{1,0:T(8,128)(2,1)} %fusion.2) | copy-start | bytes 1966084
Sparse Core Ops, SparseCore 0:
  10.7 40.2 all-gather.2
  202.6 33.8 all-gather.4

commit v2 on v1

--- a/solution.py
+++ b/solution.py
@@ -32,6 +32,21 @@
     own_band = lax.all_gather(masked, "layer", axis=1, tiled=True)
 
     total_rows = block_rows + offsets - 1
+    width = slab_offsets + block_rows - 1
+    pad_l = total_rows - 1 - half
+    pad_r = max(0, slab_offsets * (layers - 1) + half + width - offsets)
+    band_pad = jnp.pad(
+        own_band.reshape(block_rows, bs, offsets * bs), ((0, 0), (0, 0), (pad_l * bs, pad_r * bs))
+    )
+    base = layer_id * slab_offsets
+
+    def windows(shift, first, last):
+        rows = []
+        for j in range(first, last):
+            start = (base + block_rows * shift - j + pad_l) * bs
+            rows.append(lax.dynamic_slice_in_dim(band_pad[j], start, width * bs, axis=1))
+        return jnp.stack(rows, axis=0)
+
     below = half
     above = total_rows - half - block_rows
     lower_parts = []
@@ -39,7 +54,7 @@
     need = below
     while need > 0:
         take = min(block_rows, need)
-        lower_parts.insert(0, shifted(own_band[(block_rows - take) * bs:], "row", dist))
+        lower_parts.insert(0, shifted(windows(dist, block_rows - take, block_rows), "row", dist))
         need -= take
         dist += 1
     upper_parts = []
@@ -47,22 +62,11 @@
     need = above
     while need > 0:
         take = min(block_rows, need)
-        upper_parts.append(shifted(own_band[: take * bs], "row", -dist))
+        upper_parts.append(shifted(windows(-dist, 0, take), "row", -dist))
         need -= take
         dist += 1
-    halo = jnp.concatenate(lower_parts + [own_band] + upper_parts, axis=0)
-    halo = halo.reshape(total_rows, bs, offsets * bs)
-
-    width = slab_offsets + block_rows - 1
-    pad_l = total_rows - 1 - half
-    pad_r = max(0, slab_offsets * (layers - 1) + half + width - offsets)
-    halo_pad = jnp.pad(halo, ((0, 0), (0, 0), (pad_l * bs, pad_r * bs)))
-    base = layer_id * slab_offsets
-    right_rows = []
-    for t in range(total_rows):
-        start = (base + (half + pad_l - t)) * bs
-        right_rows.append(lax.dynamic_slice_in_dim(halo_pad[t], start, width * bs, axis=1))
-    right = jnp.stack(right_rows, axis=0).reshape(total_rows * bs, width * bs)
+    right = jnp.concatenate(lower_parts + [windows(0, 0, block_rows)] + upper_parts, axis=0)
+    right = right.reshape(total_rows * bs, width * bs)
 
     pattern_f = pattern.astype(jnp.float32)[:, None, :, None]
 

time: 256 us -> 238 us (0.930)
  local copies, waits for them, and re-layouts: 33.1 us -> 16.4 us
  starting transfers between devices: 12.7 us -> 5.4 us
  waiting for transfers between devices: 178 us -> 185 us
    unnamed x90 -> x64, local copies, waits for them, and re-layouts: 17.4 us -> 6.11 us
    ppermute x4, waiting for transfers between devices: 108 us -> 115 us  [shifted(): return lax.ppermute(value, axis, pairs)]
    ppermute x4, starting transfers between devices: 12.6 us -> 5.36 us  [shifted(): return lax.ppermute(value, axis, pairs)]
    slice x5 -> x1, local copies, waits for them, and re-layouts: 7.87 us -> 2.08 us  [windows(): band_pad[j]]
  transfers between devices with their start and end apart: 6 -> 6, of which waited for: 5 -> 6; matrix products, arithmetic and copies ran while one was open for 3% -> 2% of each run, Pallas kernels for 0% -> 0%
where the time goes in v2:
time: 238 us; the launch traced here: 237 us
  waiting for transfers between devices  185 us (78%)
  local copies, waits for them, and re-layouts  16.4 us (7%)
  between operations  14 us (6%)
  matrix products  12.3 us (5%)
  starting transfers between devices  5.4 us (2%)
  other arithmetic  4.37 us (2%)
    ppermute x4, waiting for transfers between devices, shifted(): return lax.ppermute(value, axis, pairs)  115 us
    all_gather x1, waiting for transfers between devices, body(): own_band = lax.all_gather(masked, 'layer', axis=1, tiled=True)  36.3 us
    all_gather x1, waiting for transfers between devices, body(): lax.all_gather(square.reshape(rows_dev, slab_cols), 'layer', axis=1, tile...  33.5 us
    dot_general x2, matrix products, product(): dense = jnp.dot(left, right, preferred_element_type=jnp.float32)  12.3 us
    unnamed x64, local copies, waits for them, and re-layouts  6.11 us
    ppermute x4, starting transfers between devices, shifted(): return lax.ppermute(value, axis, pairs)  5.36 us
  transfers between devices with their start and end apart: 6, of which 6 were waited for; matrix products, arithmetic and copies ran while one was open for 2% of the time, Pallas kernels for 0%

profile of v2, /device:TPU:1, one launch (start us, length us, event | category | flops | bytes accessed | tf_op | source)
XLA Modules:
  0.0 237.5 jit_solution(7044838918924999557)
XLA Ops:
  6.5 0.8 fusion.5
  7.4 0.3 mul.170
  7.7 0.8 mul.171
  8.4 1.0 mul.172
  9.7 1.8 mul.215
  11.5 2.0 mul.216
  13.5 36.3 %all-gather.3.cloned.1.call-done = bf16[640,2048]{1,0:T(8,128)(2,1)} async-done(((bf16[640,512]{1,0:T(8,128)(2,1)}), bf16[640,2048]{1,0:T(8,128)(2,1)}) %all-gather.3.cloned.1.call-update) | async-done | bytes 2621456 | tf_op jit(solution)/shard_map/all_gather | solution.py:32
  49.9 2.1 pad_slice_fusion
  52.5 0.2 constant_dynamic-update-slice_fusion.11
  52.6 0.2 constant_dynamic-update-slice_fusion.10
  52.8 0.2 constant_dynamic-update-slice_fusion.9
  53.0 0.2 constant_dynamic-update-slice_fusion.8
  53.1 0.2 constant_dynamic-update-slice_fusion.7
  53.3 0.2 constant_dynamic-update-slice_fusion.6
  53.5 1.4 collective-permute-start
  54.8 2.4 %collective-permute-start.1 = (bf16[10,64,1088]{2,1,0:T(8,128)(2,1)S(1)}, bf16[10,64,1088]{2,1,0:T(8,128)(2,1)S(1)}, u32[]{:S(2)}, u32[]{:S(2)}) collective-permute-start(bf16[10,64,1088]{2,1,0:T(8,128)(2,1)S(1)} %get-tuple-element.60), channel_id=1, source_target_pairs={{0,1},{1,2},{2,3},{3,4},{4,5},{5,6},{6,7},{7,8},{8,9},{9,10},{10,1... | collective-permute-start | bytes 4177928 | tf_op jit(solution)/shard_map/ppermute | solution.py:10
  57.2 0.2 fusion.4
  57.5 0.1 bitcast_dynamic-update-slice_fusion.18
  57.7 0.1 bitcast_dynamic-update-slice_fusion.16
  57.9 20.9 %collective-permute-done = bf16[6,64,1088]{2,1,0:T(8,128)(2,1)S(1)} collective-permute-done((bf16[6,64,1088]{2,1,0:T(8,128)(2,1)S(1)}, bf16[6,64,1088]{2,1,0:T(8,128)(2,1)S(1)}, u32[]{:S(2)}, u32[]{:S(2)}) %collective-permute-start) | collective-permute-done | bytes 835616 | tf_op jit(solution)/shard_map/ppermute | solution.py:10
  78.9 33.6 %collective-permute-done.1 = bf16[10,64,1088]{2,1,0:T(8,128)(2,1)S(1)} collective-permute-done((bf16[10,64,1088]{2,1,0:T(8,128)(2,1)S(1)}, bf16[10,64,1088]{2,1,0:T(8,128)(2,1)S(1)}, u32[]{:S(2)}, u32[]{:S(2)}) %collective-permute-start.1) | collective-permute-done | bytes 1392672 | tf_op jit(solution)/shard_map/ppermute | solution.py:10
  112.5 0.2 constant_dynamic-update-slice_fusion.43
  112.8 0.2 constant_dynamic-update-slice_fusion.30
  113.0 0.2 constant_dynamic-update-slice_fusion.29
  113.2 0.2 constant_dynamic-update-slice_fusion.28
  113.4 0.2 constant_dynamic-update-slice_fusion.27
  113.6 0.2 constant_dynamic-update-slice_fusion.26
  113.9 0.2 constant_dynamic-update-slice_fusion.20
  114.0 0.2 constant_dynamic-update-slice_fusion.19
  114.2 0.2 constant_dynamic-update-slice_fusion.18
  114.4 0.2 constant_dynamic-update-slice_fusion.17
  114.5 0.2 constant_dynamic-update-slice_fusion.16
  114.8 0.1 bitcast_dynamic-update-slice_fusion.14
  115.0 0.1 bitcast_dynamic-update-slice_fusion.12
  115.1 1.5 collective-permute-start.3
  116.7 0.1 bitcast_dynamic-update-slice_fusion.10
  116.8 45.0 %collective-permute-done.2 = bf16[10,64,1088]{2,1,0:T(8,128)(2,1)S(1)} collective-permute-done((bf16[10,64,1088]{2,1,0:T(8,128)(2,1)S(1)}, bf16[10,64,1088]{2,1,0:T(8,128)(2,1)S(1)}, u32[]{:S(2)}, u32[]{:S(2)}) %collective-permute-start.2) | collective-permute-done | bytes 1392672 | tf_op jit(solution)/shard_map/ppermute | solution.py:10
  161.8 0.2 constant_dynamic-update-slice_fusion.32
  162.1 15.6 %collective-permute-done.3 = bf16[5,64,1088]{2,1,0:T(8,128)(2,1)S(1)} collective-permute-done((bf16[5,64,1088]{2,1,0:T(8,128)(2,1)S(1)}, bf16[5,64,1088]{2,1,0:T(8,128)(2,1)S(1)}, u32[]{:S(2)}, u32[]{:S(2)}) %collective-permute-start.3) | collective-permute-done | bytes 696352 | tf_op jit(solution)/shard_map/ppermute | solution.py:10
  177.7 4.8 %fusion.6 = f32[10,64,1088]{2,1,0:T(8,128)S(1)} fusion(bf16[10,64,2624]{2,1,0:T(8,128)(2,1)S(1)} %bitcast_dynamic-update-slice_fusion.10, bf16[2624,1088,1]{1,0,2:T(8,128)(2,1)S(1)} %bitcast.64), kind=kOutput, calls=%fused_computation.103 | convolution fusion | flops 3654287360 | bytes 11853824 | tf_op jit(solution)/shard_map/dot_general | solution.py:76
  183.1 1.2 fusion.2
  184.3 33.5 %all-gather.5.cloned.1.call-done = bf16[640,2048]{1,0:T(8,128)(2,1)} async-done(((bf16[640,512]{1,0:T(8,128)(2,1)}), bf16[640,2048]{1,0:T(8,128)(2,1)}) %all-gather.5.cloned.1.call-update) | async-done | bytes 2621456 | tf_op jit(solution)/shard_map/all_gather | solution.py:84
  217.8 1.8 fusion.3
  219.7 0.1 bitcast_dynamic-update-slice_fusion.8
  220.4 0.1 bitcast_dynamic-update-slice_fusion
  220.6 7.5 %fusion.7 = f32[10,64,1088]{2,1,0:T(8,128)S(1)} fusion(bf16[10,64,2624]{2,1,0:T(8,128)(2,1)S(1)} %bitcast_dynamic-update-slice_fusion, bf16[2624,1088,1]{1,0,2:T(8,128)(2,1)} %bitcast.65), kind=kOutput, calls=%fused_computation.104 | convolution fusion | flops 3654287360 | bytes 11853824 | tf_op jit(solution)/shard_map/dot_general | solution.py:76
  228.7 0.5 copy-done.1
  229.2 1.4 fusion.1
  (53 shorter events, 2.7 us)
Async XLA Ops:
  6.5 1.9 copy-start.2
  6.5 43.3 %all-gather.3.cloned.1.call-start = ((), (), s32[]{:S(2)}) async-start(), calls=%async_computation | async-start | bytes 3276800 | tf_op jit(solution)/shard_map/all_gather | solution.py:32
  9.5 208.3 %all-gather.5.cloned.1.call-start = ((), (), s32[]{:S(2)}) async-start(), calls=%async_computation.1 | async-start | bytes 3276800 | tf_op jit(solution)/shard_map/all_gather | solution.py:84
  52.0 5.3 %copy-start = (bf16[640,2048]{1,0:T(8,128)(2,1)S(1)}, bf16[640,2048]{1,0:T(8,128)(2,1)}, u32[]{:S(2)}) copy-start(bf16[640,2048]{1,0:T(8,128)(2,1)} %all-gather.3.cloned.1.call-done) | copy-start | bytes 7864324
  53.5 25.3 %collective-permute-start = (bf16[6,64,1088]{2,1,0:T(8,128)(2,1)S(1)}, bf16[6,64,1088]{2,1,0:T(8,128)(2,1)S(1)}, u32[]{:S(2)}, u32[]{:S(2)}) collective-permute-start(bf16[6,64,1088]{2,1,0:T(8,128)(2,1)S(1)} %get-tuple-element.61), channel_id=1, source_target_pairs={{0,2},{1,3},{2,4},{3,5},{4,6},{5,7},{6,8},{7,9},{8,10},{9,11},{10,... | collective-permute-start | bytes 2506760 | tf_op jit(solution)/shard_map/ppermute | solution.py:10
  54.8 57.7 %collective-permute-start.1 = (bf16[10,64,1088]{2,1,0:T(8,128)(2,1)S(1)}, bf16[10,64,1088]{2,1,0:T(8,128)(2,1)S(1)}, u32[]{:S(2)}, u32[]{:S(2)}) collective-permute-start(bf16[10,64,1088]{2,1,0:T(8,128)(2,1)S(1)} %get-tuple-element.60), channel_id=1, source_target_pairs={{0,1},{1,2},{2,3},{3,4},{4,5},{5,6},{6,7},{7,8},{8,9},{9,10},{10,1... | collective-permute-start | bytes 4177928 | tf_op jit(solution)/shard_map/ppermute | solution.py:10
  114.7 47.1 %collective-permute-start.2 = (bf16[10,64,1088]{2,1,0:T(8,128)(2,1)S(1)}, bf16[10,64,1088]{2,1,0:T(8,128)(2,1)S(1)}, u32[]{:S(2)}, u32[]{:S(2)}) collective-permute-start(bf16[10,64,1088]{2,1,0:T(8,128)(2,1)S(1)} %get-tuple-element.50), channel_id=1, source_target_pairs={{0,63},{1,0},{2,1},{3,2},{4,3},{5,4},{6,5},{7,6},{8,7},{9,8},{10,9... | collective-permute-start | bytes 4177928 | tf_op jit(solution)/shard_map/ppermute | solution.py:10
  115.1 62.5 %collective-permute-start.3 = (bf16[5,64,1088]{2,1,0:T(8,128)(2,1)S(1)}, bf16[5,64,1088]{2,1,0:T(8,128)(2,1)S(1)}, u32[]{:S(2)}, u32[]{:S(2)}) collective-permute-start(bf16[5,64,1088]{2,1,0:T(8,128)(2,1)S(1)} %get-tuple-element.35), channel_id=1, source_target_pairs={{0,62},{1,63},{2,0},{3,1},{4,2},{5,3},{6,4},{7,5},{8,6},{9,7},{10,... | collective-permute-start | bytes 2088968 | tf_op jit(solution)/shard_map/ppermute | solution.py:10
  177.7 4.8 %copy-start.3 = (bf16[41,64,1088]{2,1,0:T(8,128)(2,1)}, bf16[41,64,1088]{2,1,0:T(8,128)(2,1)S(1)}, u32[]{:S(2)}) copy-start(bf16[41,64,1088]{2,1,0:T(8,128)(2,1)S(1)} %constant_dynamic-update-slice_fusion.31) | copy-start | bytes 17129476
  228.1 1.1 copy-start.1
Sparse Core Ops, SparseCore 0:
  9.6 40.2 all-gather.2
  184.5 33.3 all-gather.4

commit v3 on v2

--- a/solution.py
+++ b/solution.py
@@ -2,6 +2,121 @@
 import jax.numpy as jnp
 from jax import lax
 from jax.sharding import PartitionSpec as P
+from jax.experimental import pallas as pl
+from jax.experimental.pallas import tpu as pltpu
+
+MESH_AXES = ("layer", "row")
+
+
+def _peer(axis, sizes, step):
+    coords = [lax.axis_index(name) for name in MESH_AXES]
+    k = MESH_AXES.index(axis)
+    coords[k] = lax.rem(coords[k] + step + sizes[k], sizes[k])
+    return tuple(coords)
+
+
+def _greet(axis, sizes, steps):
+    k = MESH_AXES.index(axis)
+    peers = sorted({(s % sizes[k]) for s in steps} | {(-s) % sizes[k] for s in steps})
+    barrier = pltpu.get_barrier_semaphore()
+    for p in peers:
+        pl.semaphore_signal(barrier, inc=1, device_id=_peer(axis, sizes, p),
+                            device_id_type=pl.DeviceIdType.MESH)
+    pl.semaphore_wait(barrier, len(peers))
+
+
+def _row_exchange_kernel(sizes, steps, row_starts, own_start, *refs):
+    n = len(steps)
+    srcs = refs[:n]
+    own_ref = refs[n]
+    out_ref = refs[n + 1]
+    send_sem, recv_sem, local_sem = refs[n + 2:]
+    _greet("row", sizes, steps)
+    copies = []
+    for k, step in enumerate(steps):
+        rows = srcs[k].shape[0]
+        copy = pltpu.make_async_remote_copy(
+            src_ref=srcs[k],
+            dst_ref=out_ref.at[pl.ds(row_starts[k], rows)],
+            send_sem=send_sem.at[k],
+            recv_sem=recv_sem.at[k],
+            device_id=_peer("row", sizes, step),
+            device_id_type=pl.DeviceIdType.MESH,
+        )
+        copy.start()
+        copies.append(copy)
+    local = pltpu.make_async_copy(
+        own_ref, out_ref.at[pl.ds(own_start, own_ref.shape[0])], local_sem.at[0]
+    )
+    local.start()
+    local.wait()
+    for copy in copies:
+        copy.wait()
+
+
+def row_exchange(sizes, steps, row_starts, own_start, total_rows, sends, own):
+    n = len(steps)
+    shape = (total_rows,) + own.shape[1:]
+    any_spec = pl.BlockSpec(memory_space=pl.ANY)
+    return pl.pallas_call(
+        lambda *refs: _row_exchange_kernel(sizes, steps, row_starts, own_start, *refs),
+        out_shape=jax.ShapeDtypeStruct(shape, own.dtype),
+        in_specs=[any_spec] * (n + 1),
+        out_specs=any_spec,
+        scratch_shapes=[
+            pltpu.SemaphoreType.DMA((n,)),
+            pltpu.SemaphoreType.DMA((n,)),
+            pltpu.SemaphoreType.DMA((1,)),
+        ],
+        compiler_params=pltpu.CompilerParams(collective_id=0, has_side_effects=True),
+        name="row_exchange",
+    )(*sends, own)
+
+
+def _layer_gather_kernel(sizes, *refs):
+    src_ref, out_ref, send_sem, recv_sem, local_sem = refs
+    k = MESH_AXES.index("layer")
+    count = sizes[k]
+    steps = list(range(1, count))
+    me = lax.axis_index("layer")
+    width = src_ref.shape[1]
+    _greet("layer", sizes, steps)
+    mine = out_ref.at[:, pl.ds(pl.multiple_of(me * width, width), width)]
+    copies = []
+    for j, step in enumerate(steps):
+        copy = pltpu.make_async_remote_copy(
+            src_ref=src_ref,
+            dst_ref=mine,
+            send_sem=send_sem.at[j],
+            recv_sem=recv_sem.at[j],
+            device_id=_peer("layer", sizes, step),
+            device_id_type=pl.DeviceIdType.MESH,
+        )
+        copy.start()
+        copies.append(copy)
+    local = pltpu.make_async_copy(src_ref, mine, local_sem.at[0])
+    local.start()
+    local.wait()
+    for copy in copies:
+        copy.wait()
+
+
+def layer_gather(sizes, slab, collective_id):
+    count = sizes[MESH_AXES.index("layer")]
+    any_spec = pl.BlockSpec(memory_space=pl.ANY)
+    return pl.pallas_call(
+        lambda *refs: _layer_gather_kernel(sizes, *refs),
+        out_shape=jax.ShapeDtypeStruct((slab.shape[0], slab.shape[1] * count), slab.dtype),
+        in_specs=[any_spec],
+        out_specs=any_spec,
+        scratch_shapes=[
+            pltpu.SemaphoreType.DMA((count - 1,)),
+            pltpu.SemaphoreType.DMA((count - 1,)),
+            pltpu.SemaphoreType.DMA((1,)),
+        ],
+        compiler_params=pltpu.CompilerParams(collective_id=collective_id, has_side_effects=True),
+        name="layer_gather",
+    )(slab)
 
 
 def shifted(value, axis, steps):
@@ -26,10 +141,11 @@
     offsets = slab_offsets * layers
     half = offsets // 2
     layer_id = lax.axis_index("layer")
+    sizes = tuple(lax.axis_size(name) for name in MESH_AXES)
 
     keep = pattern.astype(jnp.bfloat16)[:, None, :, None]
     masked = (density.reshape(block_rows, bs, slab_offsets, bs) * keep).reshape(rows_dev, slab_cols)
-    own_band = lax.all_gather(masked, "layer", axis=1, tiled=True)
+    own_band = layer_gather(sizes, masked, 1)
 
     total_rows = block_rows + offsets - 1
     width = slab_offsets + block_rows - 1
@@ -49,23 +165,24 @@
 
     below = half
     above = total_rows - half - block_rows
-    lower_parts = []
-    dist = 1
-    need = below
+    steps, sends, row_starts = [], [], []
+    dist, need = 1, below
     while need > 0:
         take = min(block_rows, need)
-        lower_parts.insert(0, shifted(windows(dist, block_rows - take, block_rows), "row", dist))
+        sends.append(windows(dist, block_rows - take, block_rows))
+        steps.append(dist)
+        row_starts.append(need - take)
         need -= take
         dist += 1
-    upper_parts = []
-    dist = 1
-    need = above
+    dist, need = 1, above
     while need > 0:
         take = min(block_rows, need)
-        upper_parts.append(shifted(windows(-dist, 0, take), "row", -dist))
+        sends.append(windows(-dist, 0, take))
+        steps.append(-dist)
+        row_starts.append(below + block_rows + (above - need))
         need -= take
         dist += 1
-    right = jnp.concatenate(lower_parts + [windows(0, 0, block_rows)] + upper_parts, axis=0)
+    right = row_exchange(sizes, steps, row_starts, below, total_rows, sends, windows(0, 0, block_rows))
     right = right.reshape(total_rows * bs, width * bs)
 
     pattern_f = pattern.astype(jnp.float32)[:, None, :, None]
@@ -81,7 +198,7 @@
         return out.reshape(block_rows, bs, slab_offsets, bs) * pattern_f
 
     square = product(own_band).astype(jnp.bfloat16)
-    square_full = lax.all_gather(square.reshape(rows_dev, slab_cols), "layer", axis=1, tiled=True)
+    square_full = layer_gather(sizes, square.reshape(rows_dev, slab_cols), 1)
     cubic = product(square_full)
     purified = 3.0 * square.astype(jnp.float32) - 2.0 * cubic
     return purified.reshape(rows_dev, slab_cols)

time: 238 us -> 204 us (0.86)
  waiting for transfers between devices: 185 us -> 0 us
  Pallas kernels: 0 us -> 156 us
  local copies, waits for them, and re-layouts: 16.4 us -> 30.7 us
  between operations: 14 us -> 0.41 us
  starting transfers between devices: 5.4 us -> 0 us
    pallas_call x0 -> x3, Pallas kernels: none -> 156 us  [the longest x1 90.5 us: row_exchange(): pl.pallas_call(lambda *refs: _row_exchange_kernel(sizes, steps, row_start...]
    ppermute x4 -> x0, waiting for transfers between devices: 115 us -> none  [shifted(): return lax.ppermute(value, axis, pairs)]
    all_gather x2 -> x0, waiting for transfers between devices: 69.8 us -> none  [the longest x1 36.3 us: body(): own_band = lax.all_gather(masked, 'layer', axis=1, tiled=True)]
    unnamed x64 -> x53, local copies, waits for them, and re-layouts: 6.11 us -> 18.9 us
    ppermute x4 -> x0, starting transfers between devices: 5.36 us -> none  [shifted(): return lax.ppermute(value, axis, pairs)]
  transfers between devices with their start and end apart: 6 -> 0, of which waited for: 6 -> 0; matrix products, arithmetic and copies ran while one was open for 2% -> 0% of each run, Pallas kernels for 0% -> 0%
where the time goes in v3:
time: 204 us
  Pallas kernels  156 us (76%)
  local copies, waits for them, and re-layouts  30.7 us (15%)
  matrix products  12.3 us (6%)
  other arithmetic  4.33 us (2%)
    pallas_call x1, Pallas kernels, row_exchange(): pl.pallas_call(lambda *refs: _row_exchange_kernel(sizes, steps, row_start...  90.5 us
    pallas_call x2, Pallas kernels, layer_gather(): pl.pallas_call(lambda *refs: _layer_gather_kernel(sizes, *refs), out_shap...  65.3 us
    unnamed x53, local copies, waits for them, and re-layouts  18.9 us
    dot_general x2, matrix products, product(): dense = jnp.dot(left, right, preferred_element_type=jnp.float32)  12.3 us

profile of v3, /device:TPU:1, one launch (start us, length us, event | category | flops | bytes accessed | tf_op | source)
XLA Modules:
  0.0 203.5 jit_solution(4630423945395043087)
XLA Ops:
  0.0 0.8 fusion.5
  0.9 0.2 mul.170
  1.1 0.8 mul.171
  2.0 1.0 mul.172.refs_0_
  3.0 34.0 %layer_gather.2 = bf16[640,2048]{1,0:T(8,128)(2,1)} custom-call(bf16[640,512]{1,0:T(8,128)(2,1)} %mul.172.refs_0_), custom_call_target="tpu_custom_call" | custom-call | tf_op jit(solution)/shard_map/layer_gather/pallas_call | solution.py:107
  37.0 3.1 %pad_slice_fusion = (bf16[1,64,5184]{2,1,0:T(8,128)(2,1)S(1)}, bf16[1,64,5184]{2,1,0:T(8,128)(2,1)}, bf16[1,64,5184]{2,1,0:T(8,128)(2,1)}, bf16[1,64,5184]{2,1,0...) fusion(bf16[10,64,2048]{2,1,0:T(8,128)(2,1)} %bitcast.63), kind=kLoop, calls=%fused_computation | loop fusion | bytes 9256960 | tf_op jit(solution)/shard_map/slice | solution.py:163
  40.1 1.1 constant_dynamic-update-slice_fusion.40
  41.2 2.2 %constant_dynamic-update-slice_fusion.39 = (bf16[10,64,1088]{2,1,0:T(8,128)(2,1)}, bf16[5,64,1088]{2,1,0:T(8,128)(2,1)}, bf16[10,64,1088]{2,1,0:T(8,128)(2,1)}, bf16[10,64,1088]{2,1,0:T(8,128)(2,1)}) fusion(bf16[10,64,1088]{2,1,0:T(8,128)(2,1)} %get-tuple-element.72, bf16[1,64,5184]{2,1,0:T(8,128)(2,1)} %get-tuple-element.16, s32[]{:T(128)S(6)} %select_n.155, ...), kind=kLoop, calls=%fused_computation.74 | loop fusion | bytes 1179664
  43.4 2.2 %constant_dynamic-update-slice_fusion.38 = (bf16[10,64,1088]{2,1,0:T(8,128)(2,1)}, bf16[5,64,1088]{2,1,0:T(8,128)(2,1)}, bf16[10,64,1088]{2,1,0:T(8,128)(2,1)}, bf16[10,64,1088]{2,1,0:T(8,128)(2,1)}) fusion(bf16[10,64,1088]{2,1,0:T(8,128)(2,1)} %get-tuple-element.68, bf16[1,64,5184]{2,1,0:T(8,128)(2,1)} %get-tuple-element.17, s32[]{:T(128)S(6)} %select_n.156, ...), kind=kLoop, calls=%fused_computation.73 | loop fusion | bytes 1179664
  45.6 2.2 %constant_dynamic-update-slice_fusion.37 = (bf16[10,64,1088]{2,1,0:T(8,128)(2,1)}, bf16[5,64,1088]{2,1,0:T(8,128)(2,1)}, bf16[10,64,1088]{2,1,0:T(8,128)(2,1)}, bf16[10,64,1088]{2,1,0:T(8,128)(2,1)}) fusion(bf16[10,64,1088]{2,1,0:T(8,128)(2,1)} %get-tuple-element.64, bf16[1,64,5184]{2,1,0:T(8,128)(2,1)} %get-tuple-element.18, s32[]{:T(128)S(6)} %select_n.157, ...), kind=kLoop, calls=%fused_computation.72 | loop fusion | bytes 1179664
  47.8 1.2 constant_dynamic-update-slice_fusion.36
  49.0 2.2 %constant_dynamic-update-slice_fusion.35 = (bf16[10,64,1088]{2,1,0:T(8,128)(2,1)}, bf16[10,64,1088]{2,1,0:T(8,128)(2,1)}, bf16[6,64,1088]{2,1,0:T(8,128)(2,1)}, bf16[10,64,1088]{2,1,0:T(8,128)(2,1)}) fusion(bf16[10,64,1088]{2,1,0:T(8,128)(2,1)} %get-tuple-element.55, bf16[1,64,5184]{2,1,0:T(8,128)(2,1)} %get-tuple-element.20, s32[]{:T(128)S(6)} %select_n.159, ...), kind=kLoop, calls=%fused_computation.70 | loop fusion | bytes 1179664
  51.2 1.1 constant_dynamic-update-slice_fusion.34
  52.3 1.1 constant_dynamic-update-slice_fusion.33
  53.3 1.1 constant_dynamic-update-slice_fusion.32
  54.4 1.1 constant_dynamic-update-slice_fusion.31
  55.4 90.5 %row_exchange.1 = bf16[41,64,1088]{2,1,0:T(8,128)(2,1)} custom-call(bf16[10,64,1088]{2,1,0:T(8,128)(2,1)} %get-tuple-element.38.refs_0_, bf16[6,64,1088]{2,1,0:T(8,128)(2,1)} %get-tuple-element.37.refs_1_, bf16[10,64,1088]{2,1,0:T(8,128)(2,1)} %get-tuple-element.36.refs_2_, bf16[5,64,1088]{2,1,0:T(8,128)(2,1)} %get-tuple-element.56.refs_3_, ...), custom_call_target="tpu_custom_call" | custom-call | tf_op jit(solution)/shard_map/row_exchange/pallas_call | solution.py:61
  145.9 0.2 fusion.4
  146.2 0.1 bitcast_dynamic-update-slice_fusion.18
  146.3 0.1 bitcast_dynamic-update-slice_fusion.16
  146.5 0.1 bitcast_dynamic-update-slice_fusion.14
  146.7 0.1 bitcast_dynamic-update-slice_fusion.12
  146.9 0.1 bitcast_dynamic-update-slice_fusion.10
  147.0 1.8 copy-done.1
  148.8 4.8 %fusion.6 = f32[10,64,1088]{2,1,0:T(8,128)S(1)} fusion(bf16[10,64,2624]{2,1,0:T(8,128)(2,1)S(1)} %bitcast_dynamic-update-slice_fusion.10, bf16[2624,1088,1]{1,0,2:T(8,128)(2,1)S(1)} %bitcast.65), kind=kOutput, calls=%fused_computation.99 | convolution fusion | flops 3654287360 | bytes 11853824 | tf_op jit(solution)/shard_map/dot_general | solution.py:193
  153.6 0.1 constant_dynamic-update-slice_fusion.49
  153.7 0.1 constant_dynamic-update-slice_fusion.47
  153.9 0.1 constant_dynamic-update-slice_fusion.45
  154.0 0.1 constant_dynamic-update-slice_fusion.43
  154.1 0.1 constant_dynamic-update-slice_fusion.41
  154.3 1.8 mul.215
  156.1 2.2 %mul.216 = f32[640,512]{1,0:T(8,128)S(1)} reshape(f32[10,64,8,64]{3,2,1,0:T(8,128)} %mul.215) | data formatting | bytes 2621440 | tf_op jit(solution)/shard_map/mul | solution.py:198
  158.3 1.1 fusion.2.refs_0_
  159.5 31.2 %layer_gather.3 = bf16[640,2048]{1,0:T(8,128)(2,1)} custom-call(bf16[640,512]{1,0:T(8,128)(2,1)} %fusion.2.refs_0_), custom_call_target="tpu_custom_call" | custom-call | tf_op jit(solution)/shard_map/layer_gather/pallas_call | solution.py:107
  190.7 1.8 fusion.3
  192.6 0.1 bitcast_dynamic-update-slice_fusion.8
  192.8 0.1 bitcast_dynamic-update-slice_fusion.6
  193.0 0.1 bitcast_dynamic-update-slice_fusion.4
  193.2 0.1 bitcast_dynamic-update-slice_fusion.2
  193.3 0.1 bitcast_dynamic-update-slice_fusion
  193.5 7.5 %fusion.7 = f32[10,64,1088]{2,1,0:T(8,128)S(1)} fusion(bf16[10,64,2624]{2,1,0:T(8,128)(2,1)S(1)} %bitcast_dynamic-update-slice_fusion, bf16[2624,1088,1]{1,0,2:T(8,128)(2,1)} %bitcast.64), kind=kOutput, calls=%fused_computation.100 | convolution fusion | flops 3654287360 | bytes 11853824 | tf_op jit(solution)/shard_map/dot_general | solution.py:193
  201.1 0.1 constant_dynamic-update-slice_fusion.59
  201.2 0.1 constant_dynamic-update-slice_fusion.57
  201.3 0.1 constant_dynamic-update-slice_fusion.55
  201.4 0.1 constant_dynamic-update-slice_fusion.53
  201.5 0.1 constant_dynamic-update-slice_fusion.51
  201.6 0.5 copy-done.2
  202.1 1.4 fusion.1
  (28 shorter events, 0.6 us)
Async XLA Ops:
  0.9 1.1 copy-start.3
  55.4 90.5 %copy-start = (bf16[640,2048]{1,0:T(8,128)(2,1)S(1)}, bf16[640,2048]{1,0:T(8,128)(2,1)}, u32[]{:S(2)}) copy-start(bf16[640,2048]{1,0:T(8,128)(2,1)} %layer_gather.2) | copy-start | bytes 7864324
  146.1 2.7 %copy-start.1 = (bf16[41,64,1088]{2,1,0:T(8,128)(2,1)S(1)}, bf16[41,64,1088]{2,1,0:T(8,128)(2,1)}, u32[]{:S(2)}) copy-start(bf16[41,64,1088]{2,1,0:T(8,128)(2,1)} %row_exchange.1) | copy-start | bytes 17129476
  201.0 1.1 copy-start.2

commit v4 on v3

--- a/solution.py
+++ b/solution.py
@@ -8,39 +8,39 @@
 MESH_AXES = ("layer", "row")
 
 
-def _peer(axis, sizes, step):
-    coords = [lax.axis_index(name) for name in MESH_AXES]
-    k = MESH_AXES.index(axis)
-    coords[k] = lax.rem(coords[k] + step + sizes[k], sizes[k])
-    return tuple(coords)
-
-
-def _greet(axis, sizes, steps):
-    k = MESH_AXES.index(axis)
-    peers = sorted({(s % sizes[k]) for s in steps} | {(-s) % sizes[k] for s in steps})
+def _peer(sizes, layer_shift, row_shift):
+    layer = lax.axis_index("layer")
+    row = lax.axis_index("row")
+    return (
+        lax.rem(layer + layer_shift + sizes[0], sizes[0]),
+        lax.rem(row + row_shift + sizes[1], sizes[1]),
+    )
+
+
+def _greet(sizes, shifts):
     barrier = pltpu.get_barrier_semaphore()
-    for p in peers:
-        pl.semaphore_signal(barrier, inc=1, device_id=_peer(axis, sizes, p),
+    for layer_shift, row_shift in shifts:
+        pl.semaphore_signal(barrier, inc=1, device_id=_peer(sizes, layer_shift, row_shift),
                             device_id_type=pl.DeviceIdType.MESH)
-    pl.semaphore_wait(barrier, len(peers))
-
-
-def _row_exchange_kernel(sizes, steps, row_starts, own_start, *refs):
-    n = len(steps)
+    pl.semaphore_wait(barrier, len(shifts))
+
+
+def _row_exchange_kernel(sizes, shifts, row_starts, own_start, *refs):
+    n = len(shifts)
     srcs = refs[:n]
     own_ref = refs[n]
     out_ref = refs[n + 1]
     send_sem, recv_sem, local_sem = refs[n + 2:]
-    _greet("row", sizes, steps)
+    _greet(sizes, shifts)
     copies = []
-    for k, step in enumerate(steps):
+    for k, (layer_shift, row_shift) in enumerate(shifts):
         rows = srcs[k].shape[0]
         copy = pltpu.make_async_remote_copy(
             src_ref=srcs[k],
             dst_ref=out_ref.at[pl.ds(row_starts[k], rows)],
             send_sem=send_sem.at[k],
             recv_sem=recv_sem.at[k],
-            device_id=_peer("row", sizes, step),
+            device_id=_peer(sizes, layer_shift, row_shift),
             device_id_type=pl.DeviceIdType.MESH,
         )
         copy.start()
@@ -54,12 +54,12 @@
         copy.wait()
 
 
-def row_exchange(sizes, steps, row_starts, own_start, total_rows, sends, own):
-    n = len(steps)
+def row_exchange(sizes, shifts, row_starts, own_start, total_rows, sends, own):
+    n = len(shifts)
     shape = (total_rows,) + own.shape[1:]
     any_spec = pl.BlockSpec(memory_space=pl.ANY)
     return pl.pallas_call(
-        lambda *refs: _row_exchange_kernel(sizes, steps, row_starts, own_start, *refs),
+        lambda *refs: _row_exchange_kernel(sizes, shifts, row_starts, own_start, *refs),
         out_shape=jax.ShapeDtypeStruct(shape, own.dtype),
         in_specs=[any_spec] * (n + 1),
         out_specs=any_spec,
@@ -75,34 +75,45 @@
 
 def _layer_gather_kernel(sizes, *refs):
     src_ref, out_ref, send_sem, recv_sem, local_sem = refs
-    k = MESH_AXES.index("layer")
-    count = sizes[k]
-    steps = list(range(1, count))
+    count = sizes[0]
     me = lax.axis_index("layer")
     width = src_ref.shape[1]
-    _greet("layer", sizes, steps)
-    mine = out_ref.at[:, pl.ds(pl.multiple_of(me * width, width), width)]
-    copies = []
-    for j, step in enumerate(steps):
-        copy = pltpu.make_async_remote_copy(
-            src_ref=src_ref,
-            dst_ref=mine,
-            send_sem=send_sem.at[j],
-            recv_sem=recv_sem.at[j],
-            device_id=_peer("layer", sizes, step),
-            device_id_type=pl.DeviceIdType.MESH,
-        )
-        copy.start()
-        copies.append(copy)
+    core_shift = 1 - 2 * lax.rem(me, 2)
+    far = count // 2
+    _greet(sizes, [(far, 0), (core_shift, 0)])
+
+    def cols(layer):
+        return out_ref.at[:, pl.ds(pl.multiple_of(layer * width, width), width)]
+
+    mine = cols(me)
+    to_far = pltpu.make_async_remote_copy(
+        src_ref=src_ref, dst_ref=mine, send_sem=send_sem.at[0], recv_sem=recv_sem.at[0],
+        device_id=_peer(sizes, far, 0), device_id_type=pl.DeviceIdType.MESH,
+    )
+    to_core = pltpu.make_async_remote_copy(
+        src_ref=src_ref, dst_ref=mine, send_sem=send_sem.at[1], recv_sem=recv_sem.at[1],
+        device_id=_peer(sizes, core_shift, 0), device_id_type=pl.DeviceIdType.MESH,
+    )
+    to_far.start()
+    to_core.start()
     local = pltpu.make_async_copy(src_ref, mine, local_sem.at[0])
     local.start()
+    far_layer = lax.rem(me + far, count)
+    to_far.wait_recv()
+    forward = pltpu.make_async_remote_copy(
+        src_ref=cols(far_layer), dst_ref=cols(far_layer), send_sem=send_sem.at[2],
+        recv_sem=recv_sem.at[2], device_id=_peer(sizes, core_shift, 0),
+        device_id_type=pl.DeviceIdType.MESH,
+    )
+    forward.start()
     local.wait()
-    for copy in copies:
-        copy.wait()
+    to_far.wait_send()
+    to_core.wait()
+    forward.wait()
 
 
 def layer_gather(sizes, slab, collective_id):
-    count = sizes[MESH_AXES.index("layer")]
+    count = sizes[0]
     any_spec = pl.BlockSpec(memory_space=pl.ANY)
     return pl.pallas_call(
         lambda *refs: _layer_gather_kernel(sizes, *refs),
@@ -110,8 +121,8 @@
         in_specs=[any_spec],
         out_specs=any_spec,
         scratch_shapes=[
-            pltpu.SemaphoreType.DMA((count - 1,)),
-            pltpu.SemaphoreType.DMA((count - 1,)),
+            pltpu.SemaphoreType.DMA((3,)),
+            pltpu.SemaphoreType.DMA((3,)),
             pltpu.SemaphoreType.DMA((1,)),
         ],
         compiler_params=pltpu.CompilerParams(collective_id=collective_id, has_side_effects=True),
@@ -156,10 +167,13 @@
     )
     base = layer_id * slab_offsets
 
-    def windows(shift, first, last):
+    far = layers // 2
+
+    def windows(shift, first, last, layer_shift=0):
         rows = []
+        target = lax.rem(layer_id + layer_shift, layers) * slab_offsets
         for j in range(first, last):
-            start = (base + block_rows * shift - j + pad_l) * bs
+            start = (target + block_rows * shift - j + pad_l) * bs
             rows.append(lax.dynamic_slice_in_dim(band_pad[j], start, width * bs, axis=1))
         return jnp.stack(rows, axis=0)
 
@@ -169,16 +183,18 @@
     dist, need = 1, below
     while need > 0:
         take = min(block_rows, need)
-        sends.append(windows(dist, block_rows - take, block_rows))
-        steps.append(dist)
+        layer_shift = far if dist == 1 else 0
+        sends.append(windows(dist, block_rows - take, block_rows, layer_shift))
+        steps.append((layer_shift, dist))
         row_starts.append(need - take)
         need -= take
         dist += 1
     dist, need = 1, above
     while need > 0:
         take = min(block_rows, need)
-        sends.append(windows(-dist, 0, take))
-        steps.append(-dist)
+        layer_shift = far if dist == 1 else 0
+        sends.append(windows(-dist, 0, take, layer_shift))
+        steps.append((layer_shift, -dist))
         row_starts.append(below + block_rows + (above - need))
         need -= take
         dist += 1

time: 204 us -> 172 us (0.84)
  the two profiles are of different devices: /device:TPU:1 before, /device:TPU:4 now
where the time goes in v4:
time: 172 us; the launch traced here: 171 us
  Pallas kernels  123 us (72%)
  local copies, waits for them, and re-layouts  30.7 us (18%)
  matrix products  12.3 us (7%)
  other arithmetic  4.33 us (3%)
    pallas_call x1, Pallas kernels, row_exchange(): pl.pallas_call(lambda *refs: _row_exchange_kernel(sizes, shifts, row_star...  79.2 us
    pallas_call x2, Pallas kernels, layer_gather(): pl.pallas_call(lambda *refs: _layer_gather_kernel(sizes, *refs), out_shap...  44.2 us
    unnamed x53, local copies, waits for them, and re-layouts  18.9 us
    dot_general x2, matrix products, product(): dense = jnp.dot(left, right, preferred_element_type=jnp.float32)  12.3 us
    mul x2, local copies, waits for them, and re-layouts, product(): return out.reshape(block_rows, bs, slab_offsets, bs) * pattern_f  4.02 us

profile of v4, /device:TPU:4, one launch (start us, length us, event | category | flops | bytes accessed | tf_op | source)
XLA Modules:
  0.0 171.2 jit_solution(7693467313894048807)
XLA Ops:
  0.0 0.8 fusion.5
  0.9 0.2 mul.176
  1.1 0.8 mul.177
  2.0 1.0 mul.178.refs_0_
  3.0 22.2 %layer_gather.2 = bf16[640,2048]{1,0:T(8,128)(2,1)} custom-call(bf16[640,512]{1,0:T(8,128)(2,1)} %mul.178.refs_0_), custom_call_target="tpu_custom_call" | custom-call | tf_op jit(solution)/shard_map/layer_gather/pallas_call | solution.py:118
  25.2 3.1 %pad_slice_fusion = (bf16[1,64,5184]{2,1,0:T(8,128)(2,1)S(1)}, bf16[1,64,5184]{2,1,0:T(8,128)(2,1)}, bf16[1,64,5184]{2,1,0:T(8,128)(2,1)}, bf16[1,64,5184]{2,1,0...) fusion(bf16[10,64,2048]{2,1,0:T(8,128)(2,1)} %bitcast.63), kind=kLoop, calls=%fused_computation | loop fusion | bytes 9256960 | tf_op jit(solution)/shard_map/slice | solution.py:177
  28.3 1.1 constant_dynamic-update-slice_fusion.40
  29.3 2.2 %constant_dynamic-update-slice_fusion.39 = (bf16[10,64,1088]{2,1,0:T(8,128)(2,1)}, bf16[5,64,1088]{2,1,0:T(8,128)(2,1)}, bf16[10,64,1088]{2,1,0:T(8,128)(2,1)}, bf16[10,64,1088]{2,1,0:T(8,128)(2,1)}) fusion(bf16[10,64,1088]{2,1,0:T(8,128)(2,1)} %get-tuple-element.72, bf16[1,64,5184]{2,1,0:T(8,128)(2,1)} %get-tuple-element.16, s32[]{:T(128)S(6)} %select_n.155, ...), kind=kLoop, calls=%fused_computation.74 | loop fusion | bytes 1179664
  31.6 2.2 %constant_dynamic-update-slice_fusion.38 = (bf16[10,64,1088]{2,1,0:T(8,128)(2,1)}, bf16[5,64,1088]{2,1,0:T(8,128)(2,1)}, bf16[10,64,1088]{2,1,0:T(8,128)(2,1)}, bf16[10,64,1088]{2,1,0:T(8,128)(2,1)}) fusion(bf16[10,64,1088]{2,1,0:T(8,128)(2,1)} %get-tuple-element.68, bf16[1,64,5184]{2,1,0:T(8,128)(2,1)} %get-tuple-element.17, s32[]{:T(128)S(6)} %select_n.156, ...), kind=kLoop, calls=%fused_computation.73 | loop fusion | bytes 1179664
  33.8 2.2 %constant_dynamic-update-slice_fusion.37 = (bf16[10,64,1088]{2,1,0:T(8,128)(2,1)}, bf16[5,64,1088]{2,1,0:T(8,128)(2,1)}, bf16[10,64,1088]{2,1,0:T(8,128)(2,1)}, bf16[10,64,1088]{2,1,0:T(8,128)(2,1)}) fusion(bf16[10,64,1088]{2,1,0:T(8,128)(2,1)} %get-tuple-element.64, bf16[1,64,5184]{2,1,0:T(8,128)(2,1)} %get-tuple-element.18, s32[]{:T(128)S(6)} %select_n.157, ...), kind=kLoop, calls=%fused_computation.72 | loop fusion | bytes 1179664
  36.0 1.2 constant_dynamic-update-slice_fusion.36
  37.2 2.2 %constant_dynamic-update-slice_fusion.35 = (bf16[10,64,1088]{2,1,0:T(8,128)(2,1)}, bf16[10,64,1088]{2,1,0:T(8,128)(2,1)}, bf16[6,64,1088]{2,1,0:T(8,128)(2,1)}, bf16[10,64,1088]{2,1,0:T(8,128)(2,1)}) fusion(bf16[10,64,1088]{2,1,0:T(8,128)(2,1)} %get-tuple-element.55, bf16[1,64,5184]{2,1,0:T(8,128)(2,1)} %get-tuple-element.20, s32[]{:T(128)S(6)} %select_n.159, ...), kind=kLoop, calls=%fused_computation.70 | loop fusion | bytes 1179664
  39.4 1.1 constant_dynamic-update-slice_fusion.34
  40.4 1.1 constant_dynamic-update-slice_fusion.33
  41.5 1.1 constant_dynamic-update-slice_fusion.32
  42.6 1.1 constant_dynamic-update-slice_fusion.31
  43.6 79.2 %row_exchange.1 = bf16[41,64,1088]{2,1,0:T(8,128)(2,1)} custom-call(bf16[10,64,1088]{2,1,0:T(8,128)(2,1)} %get-tuple-element.38.refs_0_, bf16[6,64,1088]{2,1,0:T(8,128)(2,1)} %get-tuple-element.37.refs_1_, bf16[10,64,1088]{2,1,0:T(8,128)(2,1)} %get-tuple-element.36.refs_2_, bf16[5,64,1088]{2,1,0:T(8,128)(2,1)} %get-tuple-element.56.refs_3_, ...), custom_call_target="tpu_custom_call" | custom-call | tf_op jit(solution)/shard_map/row_exchange/pallas_call | solution.py:61
  122.9 0.2 fusion.4
  123.1 0.1 bitcast_dynamic-update-slice_fusion.18
  123.3 0.1 bitcast_dynamic-update-slice_fusion.16
  123.5 0.1 bitcast_dynamic-update-slice_fusion.14
  123.7 0.1 bitcast_dynamic-update-slice_fusion.12
  123.8 0.1 bitcast_dynamic-update-slice_fusion.10
  124.0 1.8 %copy-done.1 = bf16[41,64,1088]{2,1,0:T(8,128)(2,1)S(1)} copy-done((bf16[41,64,1088]{2,1,0:T(8,128)(2,1)S(1)}, bf16[41,64,1088]{2,1,0:T(8,128)(2,1)}, u32[]{:S(2)}) %copy-start.1) | copy-done | bytes 5709848
  125.8 4.8 %fusion.6 = f32[10,64,1088]{2,1,0:T(8,128)S(1)} fusion(bf16[10,64,2624]{2,1,0:T(8,128)(2,1)S(1)} %bitcast_dynamic-update-slice_fusion.10, bf16[2624,1088,1]{1,0,2:T(8,128)(2,1)S(1)} %bitcast.65), kind=kOutput, calls=%fused_computation.99 | convolution fusion | flops 3654287360 | bytes 11853824 | tf_op jit(solution)/shard_map/dot_general | solution.py:209
  130.6 0.1 constant_dynamic-update-slice_fusion.49
  130.7 0.1 constant_dynamic-update-slice_fusion.47
  130.8 0.1 constant_dynamic-update-slice_fusion.45
  130.9 0.1 constant_dynamic-update-slice_fusion.43
  131.1 0.1 constant_dynamic-update-slice_fusion.41
  131.2 1.8 %mul.222 = f32[10,64,8,64]{3,2,1,0:T(8,128)} broadcast(f32[10,8]{1,0:T(8,128)S(1)} %copy.5), dimensions={0,2} | broadcast | bytes 1311040 | tf_op jit(solution)/shard_map/mul | solution.py:214
  133.0 2.2 %mul.223 = f32[640,512]{1,0:T(8,128)S(1)} reshape(f32[10,64,8,64]{3,2,1,0:T(8,128)} %mul.222) | data formatting | bytes 2621440 | tf_op jit(solution)/shard_map/mul | solution.py:214
  135.3 1.1 fusion.2.refs_0_
  136.4 22.0 %layer_gather.3 = bf16[640,2048]{1,0:T(8,128)(2,1)} custom-call(bf16[640,512]{1,0:T(8,128)(2,1)} %fusion.2.refs_0_), custom_call_target="tpu_custom_call" | custom-call | tf_op jit(solution)/shard_map/layer_gather/pallas_call | solution.py:118
  158.4 1.8 %fusion.3 = (bf16[64,2048]{1,0:T(8,128)(2,1)S(1)}, bf16[64,2048]{1,0:T(8,128)(2,1)S(1)}, bf16[64,2048]{1,0:T(8,128)(2,1)S(1)}, bf16[64,2048]{1,0:T(8,128)(2,1)S(...) fusion(bf16[640,2048]{1,0:T(8,128)(2,1)} %layer_gather.3), kind=kLoop, calls=%fused_computation.96 | loop fusion | bytes 5242880 | tf_op jit(solution)/shard_map/slice | solution.py:142
  160.3 0.1 bitcast_dynamic-update-slice_fusion.8
  160.5 0.1 bitcast_dynamic-update-slice_fusion.6
  160.6 0.1 bitcast_dynamic-update-slice_fusion.4
  160.8 0.1 bitcast_dynamic-update-slice_fusion.2
  161.0 0.1 bitcast_dynamic-update-slice_fusion
  161.2 7.5 %fusion.7 = f32[10,64,1088]{2,1,0:T(8,128)S(1)} fusion(bf16[10,64,2624]{2,1,0:T(8,128)(2,1)S(1)} %bitcast_dynamic-update-slice_fusion, bf16[2624,1088,1]{1,0,2:T(8,128)(2,1)} %bitcast.64), kind=kOutput, calls=%fused_computation.100 | convolution fusion | flops 3654287360 | bytes 11853824 | tf_op jit(solution)/shard_map/dot_general | solution.py:209
  168.7 0.1 constant_dynamic-update-slice_fusion.59
  168.9 0.1 constant_dynamic-update-slice_fusion.57
  169.0 0.1 constant_dynamic-update-slice_fusion.55
  169.1 0.1 constant_dynamic-update-slice_fusion.53
  169.2 0.1 constant_dynamic-update-slice_fusion.51
  169.3 0.5 copy-done.2
  169.8 1.4 fusion.1
  (28 shorter events, 0.6 us)
Async XLA Ops:
  0.9 1.1 copy-start.3
  43.6 79.3 %copy-start = (bf16[640,2048]{1,0:T(8,128)(2,1)S(1)}, bf16[640,2048]{1,0:T(8,128)(2,1)}, u32[]{:S(2)}) copy-start(bf16[640,2048]{1,0:T(8,128)(2,1)} %layer_gather.2) | copy-start | bytes 7864324
  123.1 2.7 %copy-start.1 = (bf16[41,64,1088]{2,1,0:T(8,128)(2,1)S(1)}, bf16[41,64,1088]{2,1,0:T(8,128)(2,1)}, u32[]{:S(2)}) copy-start(bf16[41,64,1088]{2,1,0:T(8,128)(2,1)} %row_exchange.1) | copy-start | bytes 17129476
  168.7 1.1 copy-start.2

commit v5 on v4

--- a/solution.py
+++ b/solution.py
@@ -25,13 +25,18 @@
     pl.semaphore_wait(barrier, len(shifts))
 
 
-def _row_exchange_kernel(sizes, shifts, row_starts, own_start, *refs):
+def _row_exchange_kernel(sizes, shifts, row_starts, own_start, pair_shifts, pair_starts, *refs):
     n = len(shifts)
+    m = len(pair_shifts)
     srcs = refs[:n]
     own_ref = refs[n]
-    out_ref = refs[n + 1]
-    send_sem, recv_sem, local_sem = refs[n + 2:]
-    _greet(sizes, shifts)
+    pair_srcs = refs[n + 1:n + 1 + m]
+    out_ref, pair_ref = refs[n + 1 + m:n + 3 + m]
+    send_sem, recv_sem, pair_send, pair_recv, fwd_send, fwd_recv, local_sem = refs[n + 3 + m:]
+    me = lax.axis_index("layer")
+    core = lax.rem(me, 2)
+    core_shift = 1 - 2 * core
+    _greet(sizes, list(shifts) + list(pair_shifts) + [(core_shift, 0)])
     copies = []
     for k, (layer_shift, row_shift) in enumerate(shifts):
         rows = srcs[k].shape[0]
@@ -45,32 +50,72 @@
         )
         copy.start()
         copies.append(copy)
+    pair_copies = []
+    for k, (layer_shift, row_shift) in enumerate(pair_shifts):
+        rows = pair_srcs[k].shape[0]
+        copy = pltpu.make_async_remote_copy(
+            src_ref=pair_srcs[k],
+            dst_ref=pair_ref.at[pl.ds(pair_starts[k] + core * rows, rows)],
+            send_sem=pair_send.at[k],
+            recv_sem=pair_recv.at[k],
+            device_id=_peer(sizes, layer_shift, row_shift),
+            device_id_type=pl.DeviceIdType.MESH,
+        )
+        copy.start()
+        pair_copies.append(copy)
     local = pltpu.make_async_copy(
         own_ref, out_ref.at[pl.ds(own_start, own_ref.shape[0])], local_sem.at[0]
     )
     local.start()
+    forwards = []
+    for k in range(m):
+        rows = pair_srcs[k].shape[0]
+        pair_copies[k].wait_recv()
+        held = pair_ref.at[pl.ds(pair_starts[k] + core * rows, rows)]
+        forward = pltpu.make_async_remote_copy(
+            src_ref=held,
+            dst_ref=held,
+            send_sem=fwd_send.at[k],
+            recv_sem=fwd_recv.at[k],
+            device_id=_peer(sizes, core_shift, 0),
+            device_id_type=pl.DeviceIdType.MESH,
+        )
+        forward.start()
+        forwards.append(forward)
     local.wait()
     for copy in copies:
         copy.wait()
-
-
-def row_exchange(sizes, shifts, row_starts, own_start, total_rows, sends, own):
+    for k in range(m):
+        pair_copies[k].wait_send()
+        forwards[k].wait()
+
+
+def row_exchange(sizes, shifts, row_starts, own_start, total_rows, sends, own,
+                 pair_shifts, pair_starts, pair_rows, pair_sends):
     n = len(shifts)
+    m = len(pair_shifts)
     shape = (total_rows,) + own.shape[1:]
+    pair_shape = (pair_rows,) + pair_sends[0].shape[1:]
     any_spec = pl.BlockSpec(memory_space=pl.ANY)
     return pl.pallas_call(
-        lambda *refs: _row_exchange_kernel(sizes, shifts, row_starts, own_start, *refs),
-        out_shape=jax.ShapeDtypeStruct(shape, own.dtype),
-        in_specs=[any_spec] * (n + 1),
-        out_specs=any_spec,
+        lambda *refs: _row_exchange_kernel(
+            sizes, shifts, row_starts, own_start, pair_shifts, pair_starts, *refs),
+        out_shape=(jax.ShapeDtypeStruct(shape, own.dtype),
+                   jax.ShapeDtypeStruct(pair_shape, own.dtype)),
+        in_specs=[any_spec] * (n + 1 + m),
+        out_specs=(any_spec, any_spec),
         scratch_shapes=[
             pltpu.SemaphoreType.DMA((n,)),
             pltpu.SemaphoreType.DMA((n,)),
+            pltpu.SemaphoreType.DMA((m,)),
+            pltpu.SemaphoreType.DMA((m,)),
+            pltpu.SemaphoreType.DMA((m,)),
+            pltpu.SemaphoreType.DMA((m,)),
             pltpu.SemaphoreType.DMA((1,)),
         ],
         compiler_params=pltpu.CompilerParams(collective_id=0, has_side_effects=True),
         name="row_exchange",
-    )(*sends, own)
+    )(*sends, own, *pair_sends)
 
 
 def _layer_gather_kernel(sizes, *refs):
@@ -177,28 +222,55 @@
             rows.append(lax.dynamic_slice_in_dim(band_pad[j], start, width * bs, axis=1))
         return jnp.stack(rows, axis=0)
 
+    core = lax.rem(layer_id, 2)
+    pair_width = width + slab_offsets
+    half_rows = block_rows // 2
+
+    def pair_windows(shift):
+        target = (lax.rem(layer_id + far, layers) - core) * slab_offsets
+        rows = []
+        for jj in range(half_rows):
+            j = core * half_rows + jj
+            row = lax.dynamic_index_in_dim(band_pad, j, 0, keepdims=False)
+            start = (target + block_rows * shift - j + pad_l) * bs
+            rows.append(lax.dynamic_slice_in_dim(row, start, pair_width * bs, axis=1))
+        return jnp.stack(rows, axis=0)
+
     below = half
     above = total_rows - half - block_rows
     steps, sends, row_starts = [], [], []
+    pair_sends = []
     dist, need = 1, below
     while need > 0:
         take = min(block_rows, need)
-        layer_shift = far if dist == 1 else 0
-        sends.append(windows(dist, block_rows - take, block_rows, layer_shift))
-        steps.append((layer_shift, dist))
-        row_starts.append(need - take)
+        if dist == 1:
+            lower_start = need - take
+            pair_sends.append(pair_windows(dist))
+        else:
+            sends.append(windows(dist, block_rows - take, block_rows))
+            steps.append((0, dist))
+            row_starts.append(need - take)
         need -= take
         dist += 1
     dist, need = 1, above
     while need > 0:
         take = min(block_rows, need)
-        layer_shift = far if dist == 1 else 0
-        sends.append(windows(-dist, 0, take, layer_shift))
-        steps.append((layer_shift, -dist))
-        row_starts.append(below + block_rows + (above - need))
+        if dist == 1:
+            upper_start = below + block_rows
+            pair_sends.append(pair_windows(-dist))
+        else:
+            sends.append(windows(-dist, 0, take))
+            steps.append((0, -dist))
+            row_starts.append(below + block_rows + (above - need))
         need -= take
         dist += 1
-    right = row_exchange(sizes, steps, row_starts, below, total_rows, sends, windows(0, 0, block_rows))
+    right, pair_buf = row_exchange(
+        sizes, steps, row_starts, below, total_rows, sends, windows(0, 0, block_rows),
+        [(far, 1), (far, -1)], [0, block_rows], 2 * block_rows, pair_sends,
+    )
+    pair_part = lax.dynamic_slice_in_dim(pair_buf, core * slab_offsets * bs, width * bs, axis=2)
+    right = lax.dynamic_update_slice_in_dim(right, pair_part[:block_rows], lower_start, axis=0)
+    right = lax.dynamic_update_slice_in_dim(right, pair_part[block_rows:], upper_start, axis=0)
     right = right.reshape(total_rows * bs, width * bs)
 
     pattern_f = pattern.astype(jnp.float32)[:, None, :, None]

time: 172 us -> 170 us (0.988)
  the two profiles are of different devices: /device:TPU:4 before, /device:TPU:1 now
where the time goes in v5:
time: 170 us; the launch traced here: 168 us
  Pallas kernels  105 us (62%)
  local copies, waits for them, and re-layouts  46.7 us (27%)
  matrix products  12.3 us (7%)
  other arithmetic  4.37 us (3%)
    pallas_call x1, Pallas kernels, row_exchange(): pl.pallas_call(lambda *refs: _row_exchange_kernel(sizes, shifts, row_star...  59 us
    pallas_call x2, Pallas kernels, layer_gather(): pl.pallas_call(lambda *refs: _layer_gather_kernel(sizes, *refs), out_shap...  45.5 us
    unnamed x62, local copies, waits for them, and re-layouts  25.2 us
    dot_general x2, matrix products, product(): dense = jnp.dot(left, right, preferred_element_type=jnp.float32)  12.3 us
    mul x2, local copies, waits for them, and re-layouts, product(): return out.reshape(block_rows, bs, slab_offsets, bs) * pattern_f  4.02 us
    slice x1, local copies, waits for them, and re-layouts, windows(): band_pad[j]  3.73 us

profile of v5, /device:TPU:1, one launch (start us, length us, event | category | flops | bytes accessed | tf_op | source)
XLA Modules:
  0.0 168.4 jit_solution(5152076879377460480)
XLA Ops:
  0.0 0.8 fusion.15
  0.9 0.3 mul.162
  1.1 0.8 mul.163
  1.9 1.0 mul.164.refs_0_
  2.9 24.3 %layer_gather.2 = bf16[640,2048]{1,0:T(8,128)(2,1)} custom-call(bf16[640,512]{1,0:T(8,128)(2,1)} %mul.164.refs_0_), custom_call_target="tpu_custom_call" | custom-call | tf_op jit(solution)/shard_map/layer_gather/pallas_call | solution.py:163
  27.2 3.7 %pad_slice_fusion = (bf16[1,64,5184]{2,1,0:T(8,128)(2,1)}, bf16[1,64,5184]{2,1,0:T(8,128)(2,1)}, bf16[1,64,5184]{2,1,0:T(8,128)(2,1)}, bf16[1,64,5184]{2,1,0:T(8...) fusion(bf16[10,64,2048]{2,1,0:T(8,128)(2,1)} %bitcast.63), kind=kLoop, calls=%fused_computation.10 | loop fusion | bytes 9256960 | tf_op jit(solution)/shard_map/slice | solution.py:222
  30.9 0.8 constant_dynamic-update-slice_fusion.20
  31.7 0.8 constant_dynamic-update-slice_fusion.19
  32.6 0.9 copy-done.2
  33.5 2.0 %constant_dynamic-update-slice_fusion.18 = (bf16[10,64,1088]{2,1,0:T(8,128)(2,1)}, bf16[5,64,1088]{2,1,0:T(8,128)(2,1)}) fusion(bf16[10,64,1088]{2,1,0:T(8,128)(2,1)} %get-tuple-element.58, bf16[1,64,5184]{2,1,0:T(8,128)(2,1)} %get-tuple-element.29, s32[]{:T(128)S(6)} %select_n.160, bf16[5,64,1088]{2,1,0:T(8,128)(2,1)} %copy-done.2, s32[]{:T(128)S(6)} %select_n.155), kind=kLoop, calls=%fused_computation.75 | loop fusion | bytes 589832
  35.5 1.9 %constant_dynamic-update-slice_fusion.17 = (bf16[10,64,1088]{2,1,0:T(8,128)(2,1)}, bf16[5,64,1088]{2,1,0:T(8,128)(2,1)}) fusion(bf16[10,64,1088]{2,1,0:T(8,128)(2,1)} %get-tuple-element.56, bf16[1,64,5184]{2,1,0:T(8,128)(2,1)} %get-tuple-element.21, s32[]{:T(128)S(6)} %select_n.161, bf16[5,64,1088]{2,1,0:T(8,128)(2,1)} %get-tuple-element.57, s32[]{:T(128)S(6)} %select_n.156), kind=kLoop, calls=%fused_computation.74 | loop fusion | bytes 589832
  37.3 1.0 constant_dynamic-update-slice_fusion.16
  38.3 1.9 %constant_dynamic-update-slice_fusion.15 = (bf16[10,64,1088]{2,1,0:T(8,128)(2,1)}, bf16[6,64,1088]{2,1,0:T(8,128)(2,1)}) fusion(bf16[10,64,1088]{2,1,0:T(8,128)(2,1)} %get-tuple-element.51, bf16[1,64,5184]{2,1,0:T(8,128)(2,1)} %get-tuple-element.22, s32[]{:T(128)S(6)} %select_n.163, bf16[6,64,1088]{2,1,0:T(8,128)(2,1)} %get-tuple-element.53, s32[]{:T(128)S(6)} %select_n.148), kind=kLoop, calls=%fused_computation.72 | loop fusion | bytes 589832
  40.1 1.9 %constant_dynamic-update-slice_fusion.14 = (bf16[10,64,1088]{2,1,0:T(8,128)(2,1)}, bf16[6,64,1088]{2,1,0:T(8,128)(2,1)}) fusion(bf16[10,64,1088]{2,1,0:T(8,128)(2,1)} %get-tuple-element.49, bf16[1,64,5184]{2,1,0:T(8,128)(2,1)} %get-tuple-element.23, s32[]{:T(128)S(6)} %select_n.164, bf16[6,64,1088]{2,1,0:T(8,128)(2,1)} %get-tuple-element.50, s32[]{:T(128)S(6)} %select_n.149), kind=kLoop, calls=%fused_computation.71 | loop fusion | bytes 589832
  42.0 1.9 %constant_dynamic-update-slice_fusion.13 = (bf16[10,64,1088]{2,1,0:T(8,128)(2,1)}, bf16[6,64,1088]{2,1,0:T(8,128)(2,1)}) fusion(bf16[10,64,1088]{2,1,0:T(8,128)(2,1)} %get-tuple-element.47, bf16[1,64,5184]{2,1,0:T(8,128)(2,1)} %get-tuple-element.24, s32[]{:T(128)S(6)} %select_n.165, bf16[6,64,1088]{2,1,0:T(8,128)(2,1)} %get-tuple-element.48, s32[]{:T(128)S(6)} %select_n.150), kind=kLoop, calls=%fused_computation.70 | loop fusion | bytes 589832
  43.9 1.9 %constant_dynamic-update-slice_fusion.12 = (bf16[10,64,1088]{2,1,0:T(8,128)(2,1)}, bf16[6,64,1088]{2,1,0:T(8,128)(2,1)}) fusion(bf16[10,64,1088]{2,1,0:T(8,128)(2,1)} %get-tuple-element.45, bf16[1,64,5184]{2,1,0:T(8,128)(2,1)} %get-tuple-element.25, s32[]{:T(128)S(6)} %select_n.166, bf16[6,64,1088]{2,1,0:T(8,128)(2,1)} %get-tuple-element.46, s32[]{:T(128)S(6)} %select_n.151), kind=kLoop, calls=%fused_computation.69 | loop fusion | bytes 589832
  45.8 1.9 %constant_dynamic-update-slice_fusion.11 = (bf16[10,64,1088]{2,1,0:T(8,128)(2,1)}, bf16[6,64,1088]{2,1,0:T(8,128)(2,1)}) fusion(bf16[10,64,1088]{2,1,0:T(8,128)(2,1)} %get-tuple-element.43, bf16[1,64,5184]{2,1,0:T(8,128)(2,1)} %get-tuple-element.26, s32[]{:T(128)S(6)} %select_n.167, bf16[6,64,1088]{2,1,0:T(8,128)(2,1)} %get-tuple-element.44, s32[]{:T(128)S(6)} %select_n.152), kind=kLoop, calls=%fused_computation.68 | loop fusion | bytes 589832 | tf_op jit(solution)/shard_map/stack | solution.py:223
  47.6 0.8 fusion.8
  48.5 0.8 fusion.9
  49.3 0.8 fusion.10
  50.1 0.8 fusion.11
  50.9 1.0 fusion.12
  51.9 0.8 fusion.4
  52.7 0.8 fusion.5
  53.6 0.8 fusion.6
  54.4 0.8 fusion.7.refs_3_
  55.2 59.0 %row_exchange.1 = (bf16[41,64,1088]{2,1,0:T(8,128)(2,1)}, bf16[20,64,1600]{2,1,0:T(8,128)(2,1)}) custom-call(bf16[6,64,1088]{2,1,0:T(8,128)(2,1)} %get-tuple-element.42.refs_0_, bf16[5,64,1088]{2,1,0:T(8,128)(2,1)} %get-tuple-element.52.refs_1_, bf16[10,64,1088]{2,1,0:T(8,128)(2,1)} %get-tuple-element.41.refs_2_, bf16[5,64,1600]{2,1,0:T(8,128)(2,1)} %fusion.7.refs_3_, ...), custom_call_target="tpu_custom_call" | custom-call | tf_op jit(solution)/shard_map/row_exchange/pallas_call | solution.py:100
  114.2 3.2 %dynamic-slice_dynamic-update-slice_fusion.1 = bf16[41,64,1088]{2,1,0:T(8,128)(2,1)} fusion(bf16[41,64,1088]{2,1,0:T(8,128)(2,1)} %get-tuple-element.7, bf16[20,64,1600]{2,1,0:T(8,128)(2,1)} %get-tuple-element.8, s32[]{:T(128)S(6)} %select_n.198), kind=kLoop, calls=%fused_computation.21 | loop fusion | bytes 2949124 | tf_op jit(solution)/shard_map/dynamic_update_slice | solution.py:272
  117.4 3.2 %dynamic-slice_dynamic-update-slice_fusion = bf16[41,64,1088]{2,1,0:T(8,128)(2,1)} fusion(bf16[41,64,1088]{2,1,0:T(8,128)(2,1)} %dynamic-slice_dynamic-update-slice_fusion.1, bf16[20,64,1600]{2,1,0:T(8,128)(2,1)} %get-tuple-element.8, s32[]{:T(128)S(6)} %add.480, s32[]{:T(128)S(6)} %select_n.198), kind=kLoop, calls=%fused_computation.20 | loop fusion | bytes 2949128 | tf_op jit(solution)/shard_map/dynamic_update_slice | solution.py:273
  120.6 0.2 fusion.14
  120.9 0.1 bitcast_dynamic-update-slice_fusion.18
  121.0 0.1 bitcast_dynamic-update-slice_fusion.16
  121.2 0.1 bitcast_dynamic-update-slice_fusion.14
  121.4 0.1 bitcast_dynamic-update-slice_fusion.12
  121.6 0.1 bitcast_dynamic-update-slice_fusion.10
  121.8 1.8 %copy-done.4 = bf16[41,64,1088]{2,1,0:T(8,128)(2,1)S(1)} copy-done((bf16[41,64,1088]{2,1,0:T(8,128)(2,1)S(1)}, bf16[41,64,1088]{2,1,0:T(8,128)(2,1)}, u32[]{:S(2)}) %copy-start.4) | copy-done | bytes 5709848
  123.5 4.8 %fusion.16 = f32[10,64,1088]{2,1,0:T(8,128)S(1)} fusion(bf16[10,64,2624]{2,1,0:T(8,128)(2,1)S(1)} %bitcast_dynamic-update-slice_fusion.10, bf16[2624,1088,1]{1,0,2:T(8,128)(2,1)S(1)} %bitcast.74), kind=kOutput, calls=%fused_computation.101 | convolution fusion | flops 3654287360 | bytes 11853824 | tf_op jit(solution)/shard_map/dot_general | solution.py:281
  129.0 1.8 %mul.200 = f32[10,64,8,64]{3,2,1,0:T(8,128)} broadcast(f32[10,8]{1,0:T(8,128)S(1)} %copy.5), dimensions={0,2} | broadcast | bytes 1311040 | tf_op jit(solution)/shard_map/mul | solution.py:286
  130.8 2.2 %mul.201 = f32[640,512]{1,0:T(8,128)S(1)} reshape(f32[10,64,8,64]{3,2,1,0:T(8,128)} %mul.200) | data formatting | bytes 2621440 | tf_op jit(solution)/shard_map/mul | solution.py:286
  133.0 1.1 fusion.2.refs_0_
  134.2 21.3 %layer_gather.3 = bf16[640,2048]{1,0:T(8,128)(2,1)} custom-call(bf16[640,512]{1,0:T(8,128)(2,1)} %fusion.2.refs_0_), custom_call_target="tpu_custom_call" | custom-call | tf_op jit(solution)/shard_map/layer_gather/pallas_call | solution.py:163
  155.5 1.9 %fusion.13 = (bf16[64,2048]{1,0:T(8,128)(2,1)S(1)}, bf16[64,2048]{1,0:T(8,128)(2,1)S(1)}, bf16[64,2048]{1,0:T(8,128)(2,1)S(1)}, bf16[64,2048]{1,0:T(8,128)(2,1)S...) fusion(bf16[640,2048]{1,0:T(8,128)(2,1)} %layer_gather.3), kind=kLoop, calls=%fused_computation.98 | loop fusion | bytes 5242880 | tf_op jit(solution)/shard_map/slice | solution.py:187
  157.4 0.1 bitcast_dynamic-update-slice_fusion.8
  157.6 0.1 bitcast_dynamic-update-slice_fusion.6
  158.1 0.1 bitcast_dynamic-update-slice_fusion
  158.3 7.5 %fusion.17 = f32[10,64,1088]{2,1,0:T(8,128)S(1)} fusion(bf16[10,64,2624]{2,1,0:T(8,128)(2,1)S(1)} %bitcast_dynamic-update-slice_fusion, bf16[2624,1088,1]{1,0,2:T(8,128)(2,1)} %bitcast.73), kind=kOutput, calls=%fused_computation.102 | convolution fusion | flops 3654287360 | bytes 11853824 | tf_op jit(solution)/shard_map/dot_general | solution.py:281
  166.4 0.5 copy-done.1
  166.9 1.4 fusion.1
  (41 shorter events, 1.8 us)
Async XLA Ops:
  0.0 1.9 %copy-start.3 = (bf16[640,512]{1,0:T(8,128)(2,1)S(1)}, bf16[640,512]{1,0:T(8,128)(2,1)}, u32[]{:S(2)}) copy-start(bf16[640,512]{1,0:T(8,128)(2,1)} %param.2) | copy-start | bytes 1966084
  32.6 0.9 copy-start.2
  33.5 14.2 %copy-start = (bf16[640,2048]{1,0:T(8,128)(2,1)S(1)}, bf16[640,2048]{1,0:T(8,128)(2,1)}, u32[]{:S(2)}) copy-start(bf16[640,2048]{1,0:T(8,128)(2,1)} %layer_gather.2) | copy-start | bytes 7864324
  120.8 2.7 %copy-start.4 = (bf16[41,64,1088]{2,1,0:T(8,128)(2,1)S(1)}, bf16[41,64,1088]{2,1,0:T(8,128)(2,1)}, u32[]{:S(2)}) copy-start(bf16[41,64,1088]{2,1,0:T(8,128)(2,1)} %dynamic-slice_dynamic-update-slice_fusion) | copy-start | bytes 17129476
  165.8 1.1 copy-start.1

commit v6 on v5

--- a/solution.py
+++ b/solution.py
@@ -206,35 +206,36 @@
     total_rows = block_rows + offsets - 1
     width = slab_offsets + block_rows - 1
     pad_l = total_rows - 1 - half
-    pad_r = max(0, slab_offsets * (layers - 1) + half + width - offsets)
-    band_pad = jnp.pad(
-        own_band.reshape(block_rows, bs, offsets * bs), ((0, 0), (0, 0), (pad_l * bs, pad_r * bs))
-    )
-    base = layer_id * slab_offsets
-
-    far = layers // 2
-
-    def windows(shift, first, last, layer_shift=0):
-        rows = []
-        target = lax.rem(layer_id + layer_shift, layers) * slab_offsets
-        for j in range(first, last):
-            start = (target + block_rows * shift - j + pad_l) * bs
-            rows.append(lax.dynamic_slice_in_dim(band_pad[j], start, width * bs, axis=1))
-        return jnp.stack(rows, axis=0)
-
     core = lax.rem(layer_id, 2)
     pair_width = width + slab_offsets
     half_rows = block_rows // 2
+    far = layers // 2
+    span = pad_l + 2 * block_rows + pair_width
+    pad_r = max(0, slab_offsets * (layers - 1) + span - offsets - pad_l)
+    band_pad = jnp.pad(
+        own_band.reshape(block_rows, bs, offsets * bs), ((0, 0), (0, 0), (pad_l * bs, pad_r * bs))
+    )
+
+    def relative(target_layer):
+        start = target_layer * slab_offsets * bs
+        return lax.dynamic_slice_in_dim(band_pad, start, span * bs, axis=2)
+
+    own_rel = relative(layer_id)
+    pair_rel = relative(lax.rem(layer_id + far, layers) - core)
+
+    def cut(rel, shift, first, last, w):
+        rows = []
+        for j in range(first, last):
+            start = (block_rows * shift - j + pad_l) * bs
+            rows.append(rel[j, :, start:start + w * bs])
+        return jnp.stack(rows, axis=0)
+
+    def windows(shift, first, last):
+        return cut(own_rel, shift, first, last, width)
 
     def pair_windows(shift):
-        target = (lax.rem(layer_id + far, layers) - core) * slab_offsets
-        rows = []
-        for jj in range(half_rows):
-            j = core * half_rows + jj
-            row = lax.dynamic_index_in_dim(band_pad, j, 0, keepdims=False)
-            start = (target + block_rows * shift - j + pad_l) * bs
-            rows.append(lax.dynamic_slice_in_dim(row, start, pair_width * bs, axis=1))
-        return jnp.stack(rows, axis=0)
+        both = cut(pair_rel, shift, 0, block_rows, pair_width)
+        return lax.dynamic_slice_in_dim(both, core * half_rows, half_rows, axis=0)
 
     below = half
     above = total_rows - half - block_rows

time: 170 us -> 175 us (1.029)
  local copies, waits for them, and re-layouts: 46.7 us -> 51.1 us
    unnamed x62 -> x78, local copies, waits for them, and re-layouts: 25.2 us -> 30.3 us
    slice x1 -> x0, local copies, waits for them, and re-layouts: 3.73 us -> none  [windows(): band_pad[j]]
    dynamic_slice x0 -> x1, local copies, waits for them, and re-layouts: none -> 3.07 us  [pair_windows(): return lax.dynamic_slice_in_dim(both, core * half_rows, half_rows, axis=0)]
    another operation x3 -> x5, local copies, waits for them, and re-layouts: 3.66 us -> 3.73 us  [cut(): return jnp.stack(rows, axis=0)]
where the time goes in v6:
time: 175 us; the launch traced here: 173 us
  Pallas kernels  105 us (60%)
  local copies, waits for them, and re-layouts  51.1 us (29%)
  matrix products  12.5 us (7%)
  other arithmetic  4.34 us (2%)
    pallas_call x1, Pallas kernels, row_exchange(): pl.pallas_call(lambda *refs: _row_exchange_kernel(sizes, shifts, row_star...  59 us
    pallas_call x2, Pallas kernels, layer_gather(): pl.pallas_call(lambda *refs: _layer_gather_kernel(sizes, *refs), out_shap...  45.5 us
    unnamed x78, local copies, waits for them, and re-layouts  30.3 us
    dot_general x2, matrix products, product(): dense = jnp.dot(left, right, preferred_element_type=jnp.float32)  12.5 us
    mul x2, local copies, waits for them, and re-layouts, product(): return out.reshape(block_rows, bs, slab_offsets, bs) * pattern_f  3.85 us
    another operation x5, local copies, waits for them, and re-layouts, cut(): return jnp.stack(rows, axis=0)  3.73 us

profile of v6, /device:TPU:1, one launch (start us, length us, event | category | flops | bytes accessed | tf_op | source)
XLA Modules:
  0.0 172.9 jit_solution(17700421024894785949)
XLA Ops:
  0.0 0.8 fusion.25
  1.1 0.8 mul.61
  1.9 1.0 mul.62.refs_0_
  2.9 24.3 %layer_gather.2 = bf16[640,2048]{1,0:T(8,128)(2,1)} custom-call(bf16[640,512]{1,0:T(8,128)(2,1)} %mul.62.refs_0_), custom_call_target="tpu_custom_call" | custom-call | tf_op jit(solution)/shard_map/layer_gather/pallas_call | solution.py:163
  27.2 1.9 %fusion.4 = bf16[10,64,1600]{2,1,0:T(8,128)(2,1)} fusion(s32[]{:T(128)S(6)} %add.121, bf16[10,64,2048]{2,1,0:T(8,128)(2,1)} %bitcast.63), kind=kLoop, calls=%fused_computation.69 | loop fusion | bytes 2834436
  29.1 0.8 fusion.15
  30.0 0.8 fusion.16
  30.8 0.8 fusion.17
  31.6 0.8 fusion.18
  32.4 0.8 fusion.19
  33.3 0.8 fusion.20
  34.1 0.8 fusion.21
  34.9 0.8 fusion.22
  35.7 1.0 fusion.5
  36.7 0.8 fusion.6
  37.5 0.8 fusion.7
  38.3 0.8 fusion.8
  39.2 0.8 fusion.9
  40.0 0.8 fusion.10
  40.8 0.8 fusion.11
  41.6 0.8 fusion.12
  42.5 0.8 fusion.13
  43.3 0.8 fusion.14
  44.1 3.1 %constant_dynamic-slice_fusion = (bf16[5,64,1600]{2,1,0:T(8,128)(2,1)}, bf16[5,64,1600]{2,1,0:T(8,128)(2,1)}) fusion(bf16[10,64,1600]{2,1,0:T(8,128)(2,1)} %get-tuple-element.19, s32[]{:T(128)S(6)} %select_n.15, bf16[10,64,1600]{2,1,0:T(8,128)(2,1)} %fusion.14), kind=kLoop, calls=%fused_computation.129 | loop fusion | bytes 4096004 | tf_op jit(solution)/shard_map/dynamic_slice | solution.py:238
  47.2 0.8 constant_dynamic-update-slice_fusion.20
  48.0 0.8 constant_dynamic-update-slice_fusion.19
  48.8 0.8 constant_dynamic-update-slice_fusion.18
  50.3 0.8 constant_dynamic-update-slice_fusion.16
  51.1 0.8 constant_dynamic-update-slice_fusion.15
  53.4 0.8 constant_dynamic-update-slice_fusion.12
  54.2 0.9 constant_dynamic-update-slice_fusion.11
  55.2 0.8 constant_dynamic-update-slice_fusion.9
  55.9 0.8 constant_dynamic-update-slice_fusion.8
  56.7 0.8 constant_dynamic-update-slice_fusion.7
  57.5 0.8 constant_dynamic-update-slice_fusion.6
  58.9 1.0 copy-done.2
  59.8 59.0 %row_exchange.1 = (bf16[41,64,1088]{2,1,0:T(8,128)(2,1)}, bf16[20,64,1600]{2,1,0:T(8,128)(2,1)}) custom-call(bf16[6,64,1088]{2,1,0:T(8,128)(2,1)} %copy-done.2, bf16[5,64,1088]{2,1,0:T(8,128)(2,1)} %get-tuple-element.24.refs_1_, bf16[10,64,1088]{2,1,0:T(8,128)(2,1)} %get-tuple-element.21.refs_2_, bf16[5,64,1600]{2,1,0:T(8,128)(2,1)} %get-tuple-element.39.refs_3_, ...), custom_call_target="tpu_custom_call" | custom-call | tf_op jit(solution)/shard_map/row_exchange/pallas_call | solution.py:100
  118.8 3.2 %dynamic-slice_dynamic-update-slice_fusion.1 = bf16[41,64,1088]{2,1,0:T(8,128)(2,1)} fusion(bf16[41,64,1088]{2,1,0:T(8,128)(2,1)} %get-tuple-element.7, bf16[20,64,1600]{2,1,0:T(8,128)(2,1)} %get-tuple-element.8, s32[]{:T(128)S(6)} %select_n.16), kind=kLoop, calls=%fused_computation.42 | loop fusion | bytes 2949124 | tf_op jit(solution)/shard_map/dynamic_update_slice | solution.py:273
  122.0 3.2 %dynamic-slice_dynamic-update-slice_fusion = bf16[41,64,1088]{2,1,0:T(8,128)(2,1)} fusion(bf16[41,64,1088]{2,1,0:T(8,128)(2,1)} %dynamic-slice_dynamic-update-slice_fusion.1, bf16[20,64,1600]{2,1,0:T(8,128)(2,1)} %get-tuple-element.8, s32[]{:T(128)S(6)} %add.140, s32[]{:T(128)S(6)} %select_n.16), kind=kLoop, calls=%fused_computation.41 | loop fusion | bytes 2949128 | tf_op jit(solution)/shard_map/dynamic_update_slice | solution.py:274
  126.3 1.8 %copy-done.4 = bf16[41,64,1088]{2,1,0:T(8,128)(2,1)S(1)} copy-done((bf16[41,64,1088]{2,1,0:T(8,128)(2,1)S(1)}, bf16[41,64,1088]{2,1,0:T(8,128)(2,1)}, u32[]{:S(2)}) %copy-start.4) | copy-done | bytes 5709848
  128.1 5.0 %fusion.26 = f32[10,64,1088]{2,1,0:T(8,128)S(1)} fusion(bf16[10,64,2624]{2,1,0:T(8,128)(2,1)S(1)} %bitcast_dynamic-update-slice_fusion.10, bf16[2624,1088,1]{1,0,2:T(8,128)(2,1)S(1)} %bitcast.101), kind=kOutput, calls=%fused_computation.134 | convolution fusion | flops 3654287360 | bytes 11853824 | tf_op jit(solution)/shard_map/dot_general | solution.py:282
  133.8 1.8 %mul.67 = f32[10,64,8,64]{3,2,1,0:T(8,128)} broadcast(f32[10,8]{1,0:T(8,128)S(1)} %copy.5), dimensions={0,2} | broadcast | bytes 1311040 | tf_op jit(solution)/shard_map/mul | solution.py:287
  135.6 2.0 %mul.68 = f32[640,512]{1,0:T(8,128)S(1)} reshape(f32[10,64,8,64]{3,2,1,0:T(8,128)} %mul.67) | data formatting | bytes 2621440 | tf_op jit(solution)/shard_map/mul | solution.py:287
  137.6 1.1 fusion.2.refs_0_
  138.8 21.3 %layer_gather.3 = bf16[640,2048]{1,0:T(8,128)(2,1)} custom-call(bf16[640,512]{1,0:T(8,128)(2,1)} %fusion.2.refs_0_), custom_call_target="tpu_custom_call" | custom-call | tf_op jit(solution)/shard_map/layer_gather/pallas_call | solution.py:163
  160.0 1.8 %fusion.23 = (bf16[64,2048]{1,0:T(8,128)(2,1)S(1)}, bf16[64,2048]{1,0:T(8,128)(2,1)S(1)}, bf16[64,2048]{1,0:T(8,128)(2,1)S(1)}, bf16[64,2048]{1,0:T(8,128)(2,1)S...) fusion(bf16[640,2048]{1,0:T(8,128)(2,1)} %layer_gather.3), kind=kLoop, calls=%fused_computation.131 | loop fusion | bytes 5242880 | tf_op jit(solution)/shard_map/slice | solution.py:187
  162.8 7.5 %fusion.27 = f32[10,64,1088]{2,1,0:T(8,128)S(1)} fusion(bf16[10,64,2624]{2,1,0:T(8,128)(2,1)S(1)} %bitcast_dynamic-update-slice_fusion, bf16[2624,1088,1]{1,0,2:T(8,128)(2,1)} %bitcast.100), kind=kOutput, calls=%fused_computation.135 | convolution fusion | flops 3654287360 | bytes 11853824 | tf_op jit(solution)/shard_map/dot_general | solution.py:282
  171.4 1.4 fusion.1
  (59 shorter events, 6.7 us)
Async XLA Ops:
  0.0 1.9 %copy-start.3 = (bf16[640,512]{1,0:T(8,128)(2,1)S(1)}, bf16[640,512]{1,0:T(8,128)(2,1)}, u32[]{:S(2)}) copy-start(bf16[640,512]{1,0:T(8,128)(2,1)} %param.2) | copy-start | bytes 1966084
  27.2 1.9 %copy-start = (bf16[640,2048]{1,0:T(8,128)(2,1)S(1)}, bf16[640,2048]{1,0:T(8,128)(2,1)}, u32[]{:S(2)}) copy-start(bf16[640,2048]{1,0:T(8,128)(2,1)} %layer_gather.2) | copy-start | bytes 7864324
  58.9 1.0 copy-start.2
  125.4 2.7 %copy-start.4 = (bf16[41,64,1088]{2,1,0:T(8,128)(2,1)S(1)}, bf16[41,64,1088]{2,1,0:T(8,128)(2,1)}, u32[]{:S(2)}) copy-start(bf16[41,64,1088]{2,1,0:T(8,128)(2,1)} %dynamic-slice_dynamic-update-slice_fusion) | copy-start | bytes 17129476
  170.4 1.1 copy-start.1

commit v7 on v4

--- a/solution.py
+++ b/solution.py
@@ -25,52 +25,98 @@
     pl.semaphore_wait(barrier, len(shifts))
 
 
-def _row_exchange_kernel(sizes, shifts, row_starts, own_start, *refs):
-    n = len(shifts)
-    srcs = refs[:n]
-    own_ref = refs[n]
-    out_ref = refs[n + 1]
-    send_sem, recv_sem, local_sem = refs[n + 2:]
-    _greet(sizes, shifts)
-    copies = []
-    for k, (layer_shift, row_shift) in enumerate(shifts):
-        rows = srcs[k].shape[0]
-        copy = pltpu.make_async_remote_copy(
-            src_ref=srcs[k],
-            dst_ref=out_ref.at[pl.ds(row_starts[k], rows)],
-            send_sem=send_sem.at[k],
-            recv_sem=recv_sem.at[k],
-            device_id=_peer(sizes, layer_shift, row_shift),
-            device_id_type=pl.DeviceIdType.MESH,
-        )
-        copy.start()
-        copies.append(copy)
-    local = pltpu.make_async_copy(
-        own_ref, out_ref.at[pl.ds(own_start, own_ref.shape[0])], local_sem.at[0]
-    )
-    local.start()
-    local.wait()
-    for copy in copies:
-        copy.wait()
-
-
-def row_exchange(sizes, shifts, row_starts, own_start, total_rows, sends, own):
-    n = len(shifts)
-    shape = (total_rows,) + own.shape[1:]
+def _row_exchange_kernel(sizes, plan, *refs):
+    (slab_offsets, block_rows, pad_l, width, pair_width, far, own_start,
+     steps, pair_steps) = plan
+    band_ref, out_ref, pair_ref = refs[:3]
+    send_sem, recv_sem, pair_send, pair_recv, fwd_send, fwd_recv, local_sem = refs[3:]
+    me = lax.axis_index("layer")
+    core = lax.rem(me, 2)
+    core_shift = 1 - 2 * core
+    half_rows = block_rows // 2
+    shifts = [(0, shift) for shift, _, _, _ in steps]
+    shifts += [(far, shift) for shift, _ in pair_steps]
+    _greet(sizes, shifts + [(core_shift, 0)])
+    mesh = pl.DeviceIdType.MESH
+
+    def row_copy(j, start, count, dst, send, recv, target):
+        return pltpu.make_async_remote_copy(
+            src_ref=band_ref.at[j, pl.ds(start, count)], dst_ref=dst,
+            send_sem=send, recv_sem=recv, device_id=target, device_id_type=mesh,
+        )
+
+    def group(dst_rows, count, send, recv, target):
+        return pltpu.make_async_remote_copy(
+            src_ref=band_ref.at[pl.ds(0, dst_rows.shape[0]), pl.ds(0, count)], dst_ref=dst_rows,
+            send_sem=send, recv_sem=recv, device_id=target, device_id_type=mesh,
+        )
+
+    waits = []
+    for k, (shift, first, last, row_start) in enumerate(steps):
+        target = _peer(sizes, 0, shift)
+        for j in range(first, last):
+            start = me * slab_offsets + block_rows * shift - j + pad_l
+            row_copy(j, start, width, out_ref.at[row_start + j - first],
+                     send_sem.at[k], recv_sem.at[k], target).start()
+        waits.append(group(out_ref.at[pl.ds(row_start, last - first)], width,
+                           send_sem.at[k], recv_sem.at[k], target))
+    pair_groups = []
+    pair_base = (lax.rem(me + far, sizes[0]) - core) * slab_offsets
+    for k, (shift, pair_start) in enumerate(pair_steps):
+        target = _peer(sizes, far, shift)
+        for jj in range(half_rows):
+            j = core * half_rows + jj
+            start = pair_base + block_rows * shift - j + pad_l
+            row_copy(j, start, pair_width, pair_ref.at[pair_start + j],
+                     pair_send.at[k], pair_recv.at[k], target).start()
+        held = pair_ref.at[pl.ds(pair_start + core * half_rows, half_rows)]
+        pair_groups.append((held, group(held, pair_width, pair_send.at[k], pair_recv.at[k], target)))
+    for j in range(block_rows):
+        start = me * slab_offsets - j + pad_l
+        pltpu.make_async_copy(band_ref.at[j, pl.ds(start, width)],
+                              out_ref.at[own_start + j], local_sem.at[0]).start()
+    forwards = []
+    for k, (held, grp) in enumerate(pair_groups):
+        grp.wait_recv()
+        forward = pltpu.make_async_remote_copy(
+            src_ref=held, dst_ref=held, send_sem=fwd_send.at[k], recv_sem=fwd_recv.at[k],
+            device_id=_peer(sizes, core_shift, 0), device_id_type=mesh,
+        )
+        forward.start()
+        forwards.append(forward)
+    pltpu.make_async_copy(band_ref.at[pl.ds(0, block_rows), pl.ds(0, width)],
+                          out_ref.at[pl.ds(own_start, block_rows)], local_sem.at[0]).wait()
+    for grp in waits:
+        grp.wait()
+    for k, (held, grp) in enumerate(pair_groups):
+        grp.wait_send()
+        forwards[k].wait()
+
+
+def row_exchange(sizes, plan, total_rows, pair_rows, band):
+    (slab_offsets, block_rows, pad_l, width, pair_width, far, own_start,
+     steps, pair_steps) = plan
+    blk = band.shape[2:]
     any_spec = pl.BlockSpec(memory_space=pl.ANY)
+    n, m = len(steps), len(pair_steps)
     return pl.pallas_call(
-        lambda *refs: _row_exchange_kernel(sizes, shifts, row_starts, own_start, *refs),
-        out_shape=jax.ShapeDtypeStruct(shape, own.dtype),
-        in_specs=[any_spec] * (n + 1),
-        out_specs=any_spec,
+        lambda *refs: _row_exchange_kernel(sizes, plan, *refs),
+        out_shape=(jax.ShapeDtypeStruct((total_rows, width) + blk, band.dtype),
+                   jax.ShapeDtypeStruct((pair_rows, pair_width) + blk, band.dtype)),
+        in_specs=[any_spec],
+        out_specs=(any_spec, any_spec),
         scratch_shapes=[
             pltpu.SemaphoreType.DMA((n,)),
             pltpu.SemaphoreType.DMA((n,)),
+            pltpu.SemaphoreType.DMA((m,)),
+            pltpu.SemaphoreType.DMA((m,)),
+            pltpu.SemaphoreType.DMA((m,)),
+            pltpu.SemaphoreType.DMA((m,)),
             pltpu.SemaphoreType.DMA((1,)),
         ],
         compiler_params=pltpu.CompilerParams(collective_id=0, has_side_effects=True),
         name="row_exchange",
-    )(*sends, own)
+    )(band)
 
 
 def _layer_gather_kernel(sizes, *refs):
@@ -161,45 +207,45 @@
     total_rows = block_rows + offsets - 1
     width = slab_offsets + block_rows - 1
     pad_l = total_rows - 1 - half
-    pad_r = max(0, slab_offsets * (layers - 1) + half + width - offsets)
-    band_pad = jnp.pad(
-        own_band.reshape(block_rows, bs, offsets * bs), ((0, 0), (0, 0), (pad_l * bs, pad_r * bs))
-    )
-    base = layer_id * slab_offsets
-
     far = layers // 2
-
-    def windows(shift, first, last, layer_shift=0):
-        rows = []
-        target = lax.rem(layer_id + layer_shift, layers) * slab_offsets
-        for j in range(first, last):
-            start = (target + block_rows * shift - j + pad_l) * bs
-            rows.append(lax.dynamic_slice_in_dim(band_pad[j], start, width * bs, axis=1))
-        return jnp.stack(rows, axis=0)
+    pair_width = width + slab_offsets
+    span = pad_l + 2 * block_rows + pair_width
+    pad_r = max(0, slab_offsets * (layers - 1) + span - offsets - pad_l)
+    band = own_band.reshape(block_rows, bs, offsets, bs).transpose(0, 2, 1, 3)
+    band = jnp.pad(band, ((0, 0), (pad_l, pad_r), (0, 0), (0, 0)))
+    core = lax.rem(layer_id, 2)
 
     below = half
     above = total_rows - half - block_rows
-    steps, sends, row_starts = [], [], []
+    steps = []
     dist, need = 1, below
     while need > 0:
         take = min(block_rows, need)
-        layer_shift = far if dist == 1 else 0
-        sends.append(windows(dist, block_rows - take, block_rows, layer_shift))
-        steps.append((layer_shift, dist))
-        row_starts.append(need - take)
+        if dist == 1:
+            lower_start = need - take
+        else:
+            steps.append((dist, block_rows - take, block_rows, need - take))
         need -= take
         dist += 1
     dist, need = 1, above
     while need > 0:
         take = min(block_rows, need)
-        layer_shift = far if dist == 1 else 0
-        sends.append(windows(-dist, 0, take, layer_shift))
-        steps.append((layer_shift, -dist))
-        row_starts.append(below + block_rows + (above - need))
+        if dist == 1:
+            upper_start = below + block_rows
+        else:
+            steps.append((-dist, 0, take, below + block_rows + (above - need)))
         need -= take
         dist += 1
-    right = row_exchange(sizes, steps, row_starts, below, total_rows, sends, windows(0, 0, block_rows))
-    right = right.reshape(total_rows * bs, width * bs)
+    pair_steps = ((1, 0), (-1, block_rows))
+    plan = (slab_offsets, block_rows, pad_l, width, pair_width, far, below,
+            tuple(steps), pair_steps)
+    right, pair_buf = row_exchange(sizes, plan, total_rows, 2 * block_rows, band)
+    pair_part = lax.dynamic_slice_in_dim(pair_buf, core * slab_offsets, width, axis=1)
+    right = jnp.concatenate([
+        right[:lower_start], pair_part[:block_rows], right[below:below + block_rows],
+        pair_part[block_rows:], right[upper_start + block_rows:],
+    ], axis=0)
+    right = right.transpose(0, 2, 1, 3).reshape(total_rows * bs, width * bs)
 
     pattern_f = pattern.astype(jnp.float32)[:, None, :, None]
 

time: 172 us -> 253 us (1.47)
  the two profiles are of different devices: /device:TPU:4 before, /device:TPU:1 now
where the time goes in v7:
time: 253 us; the launch traced here: 249 us
  Pallas kernels  148 us (58%)
  local copies, waits for them, and re-layouts  83.7 us (33%)
  matrix products  12.3 us (5%)
  other arithmetic  4.34 us (2%)
    pallas_call x1, Pallas kernels, row_exchange(): pl.pallas_call(lambda *refs: _row_exchange_kernel(sizes, plan, *refs), ou...  103 us
    pallas_call x2, Pallas kernels, layer_gather(): pl.pallas_call(lambda *refs: _layer_gather_kernel(sizes, *refs), out_shap...  45.5 us
    unnamed x48, local copies, waits for them, and re-layouts  19.1 us
    transpose x1, local copies, waits for them, and re-layouts, body(): right = right.transpose(0, 2, 1, 3).reshape(total_rows * bs, width * bs)  18.4 us
    reshape x1, local copies, waits for them, and re-layouts, body(): right = right.transpose(0, 2, 1, 3).reshape(total_rows * bs, width * bs)  17.1 us
    reshape x2, local copies, waits for them, and re-layouts, body(): band = own_band.reshape(block_rows, bs, offsets, bs).transpose(0, 2, 1, 3)  13 us
    dot_general x2, matrix products, product(): dense = jnp.dot(left, right, preferred_element_type=jnp.float32)  12.3 us
    pad x1, local copies, waits for them, and re-layouts, body(): band = jnp.pad(band, ((0, 0), (pad_l, pad_r), (0, 0), (0, 0)))  5.74 us

profile of v7, /device:TPU:1, one launch (start us, length us, event | category | flops | bytes accessed | tf_op | source)
XLA Modules:
  0.0 248.8 jit_solution(15589438903211296946)
XLA Ops:
  0.0 0.8 fusion.5
  0.8 0.1 copy.5
  0.9 0.3 mul.47
  1.1 0.8 mul.48
  1.9 1.0 mul.49.refs_0_
  2.9 24.3 %layer_gather.2 = bf16[640,2048]{1,0:T(8,128)(2,1)} custom-call(bf16[640,512]{1,0:T(8,128)(2,1)} %mul.49.refs_0_), custom_call_target="tpu_custom_call" | custom-call | tf_op jit(solution)/shard_map/layer_gather/pallas_call | solution.py:164
  27.2 8.5 %reshape.75 = bf16[10,64,32,64]{3,2,1,0:T(8,128)(2,1)} reshape(bf16[640,2048]{1,0:T(8,128)(2,1)} %layer_gather.2) | data formatting | bytes 5242880 | tf_op jit(solution)/shard_map/reshape | solution.py:214
  35.7 4.5 %copy.10 = bf16[10,64,32,64]{3,1,2,0:T(8,128)(2,1)S(1)} copy(bf16[10,64,32,64]{3,2,1,0:T(8,128)(2,1)} %reshape.75) | data formatting | bytes 5242880 | tf_op jit(solution)/shard_map/reshape | solution.py:214
  40.2 5.7 %pad.84.refs_0_ = bf16[10,93,64,64]{3,2,1,0:T(8,128)(2,1)} pad(bf16[10,32,64,64]{3,2,1,0:T(8,128)(2,1)S(1)} %bitcast.64, bf16[]{:T(256)} %constant.5.clone.1), padding=0_0x24_37x0_0x0_0 | pad | bytes 10240002 | tf_op jit(solution)/shard_map/jit(_pad)/pad | solution.py:215
  46.0 102.6 %row_exchange.1 = (bf16[41,17,64,64]{3,2,1,0:T(8,128)(2,1)}, bf16[20,25,64,64]{3,2,1,0:T(8,128)(2,1)}) custom-call(bf16[10,93,64,64]{3,2,1,0:T(8,128)(2,1)} %pad.84.refs_0_), custom_call_target="tpu_custom_call" | custom-call | tf_op jit(solution)/shard_map/row_exchange/pallas_call | solution.py:102
  148.6 2.8 %slice_dynamic-update-slice_fusion.1 = bf16[41,17,64,64]{3,2,1,0:T(8,128)(2,1)} fusion(bf16[41,17,64,64]{3,2,1,0:T(8,128)(2,1)} %get-tuple-element.7), kind=kLoop, calls=%fused_computation.4 | loop fusion | bytes 2506752
  151.4 4.0 %dynamic-slice_dynamic-update-slice_fusion.1 = bf16[41,17,64,64]{3,2,1,0:T(8,128)(2,1)} fusion(bf16[41,17,64,64]{3,2,1,0:T(8,128)(2,1)} %slice_dynamic-update-slice_fusion.1, bf16[20,25,64,64]{3,2,1,0:T(8,128)(2,1)} %get-tuple-element.8, s32[]{:T(128)S(6)} %select_n.3), kind=kLoop, calls=%fused_computation.2 | loop fusion | bytes 5570564
  155.4 3.9 %slice_dynamic-update-slice_fusion = bf16[41,17,64,64]{3,2,1,0:T(8,128)(2,1)} fusion(bf16[41,17,64,64]{3,2,1,0:T(8,128)(2,1)} %dynamic-slice_dynamic-update-slice_fusion.1, bf16[41,17,64,64]{3,2,1,0:T(8,128)(2,1)} %get-tuple-element.7), kind=kLoop, calls=%fused_computation.3 | loop fusion | bytes 5570560
  159.3 3.9 %dynamic-slice_dynamic-update-slice_fusion = bf16[41,17,64,64]{3,2,1,0:T(8,128)(2,1)} fusion(bf16[41,17,64,64]{3,2,1,0:T(8,128)(2,1)} %slice_dynamic-update-slice_fusion, bf16[20,25,64,64]{3,2,1,0:T(8,128)(2,1)} %get-tuple-element.8, s32[]{:T(128)S(6)} %add.46, s32[]{:T(128)S(6)} %select_n.3), kind=kLoop, calls=%fused_computation.1 | loop fusion | bytes 5570568
  163.2 2.6 %slice_dynamic-update-slice_fusion.2 = bf16[41,17,64,64]{3,2,1,0:T(8,128)(2,1)} fusion(bf16[41,17,64,64]{3,2,1,0:T(8,128)(2,1)} %dynamic-slice_dynamic-update-slice_fusion, bf16[41,17,64,64]{3,2,1,0:T(8,128)(2,1)} %get-tuple-element.7), kind=kLoop, calls=%fused_computation.5 | loop fusion | bytes 2785280 | tf_op jit(solution)/shard_map/concatenate | solution.py:244
  165.8 18.4 %copy.7 = bf16[41,64,17,64]{1,0,3,2:T(8,128)(2,1)} copy(bf16[41,64,17,64]{3,1,2,0:T(8,128)(2,1)} %bitcast.11) | data formatting | bytes 11419648 | tf_op jit(solution)/shard_map/transpose | solution.py:248
  184.2 17.1 %reshape.79 = bf16[2624,1088,1]{0,1,2:T(8,128)(2,1)} reshape(bf16[41,64,17,64]{1,0,3,2:T(8,128)(2,1)} %copy.7) | data formatting | bytes 11419648 | tf_op jit(solution)/shard_map/reshape | solution.py:248
  201.3 0.2 fusion.4
  201.5 0.1 bitcast_dynamic-update-slice_fusion.18
  201.7 0.1 bitcast_dynamic-update-slice_fusion.16
  201.9 0.1 bitcast_dynamic-update-slice_fusion.14
  202.1 0.1 bitcast_dynamic-update-slice_fusion.12
  202.3 0.1 bitcast_dynamic-update-slice_fusion.10
  202.4 1.7 copy-done.2
  204.1 4.8 %fusion.6 = f32[10,64,1088]{2,1,0:T(8,128)S(1)} fusion(bf16[10,64,2624]{2,1,0:T(8,128)(2,1)S(1)} %bitcast_dynamic-update-slice_fusion.10, bf16[2624,1088,1]{0,1,2:T(8,128)(2,1)S(1)} %copy-done.2), kind=kOutput, calls=%fused_computation.54 | convolution fusion | flops 3654287360 | bytes 11853824 | tf_op jit(solution)/shard_map/dot_general | solution.py:255
  209.0 0.1 slice_dynamic-update-slice_fusion.21
  209.1 0.1 slice_dynamic-update-slice_fusion.19
  209.2 0.1 slice_dynamic-update-slice_fusion.17
  209.3 0.1 slice_dynamic-update-slice_fusion.15
  209.4 0.1 slice_dynamic-update-slice_fusion.13
  209.6 1.8 mul.51
  211.4 2.3 mul.52
  213.7 1.1 fusion.2.refs_0_
  214.8 21.2 %layer_gather.3 = bf16[640,2048]{1,0:T(8,128)(2,1)} custom-call(bf16[640,512]{1,0:T(8,128)(2,1)} %fusion.2.refs_0_), custom_call_target="tpu_custom_call" | custom-call | tf_op jit(solution)/shard_map/layer_gather/pallas_call | solution.py:164
  236.1 1.8 fusion.3
  237.9 0.1 bitcast_dynamic-update-slice_fusion.8
  238.1 0.1 bitcast_dynamic-update-slice_fusion.6
  238.3 0.1 bitcast_dynamic-update-slice_fusion.4
  238.5 0.1 bitcast_dynamic-update-slice_fusion.2
  238.7 0.1 bitcast_dynamic-update-slice_fusion
  238.8 7.5 %fusion.7 = f32[10,64,1088]{2,1,0:T(8,128)S(1)} fusion(bf16[10,64,2624]{2,1,0:T(8,128)(2,1)S(1)} %bitcast_dynamic-update-slice_fusion, bf16[2624,1088,1]{0,1,2:T(8,128)(2,1)} %reshape.79), kind=kOutput, calls=%fused_computation.55 | convolution fusion | flops 3654287360 | bytes 11853824 | tf_op jit(solution)/shard_map/dot_general | solution.py:255
  246.3 0.1 slice_dynamic-update-slice_fusion.11
  246.5 0.1 slice_dynamic-update-slice_fusion.9
  246.6 0.1 slice_dynamic-update-slice_fusion.7
  246.7 0.1 slice_dynamic-update-slice_fusion.5
  246.8 0.1 slice_dynamic-update-slice_fusion.3
  246.9 0.5 copy-done.1
  247.4 1.4 fusion.1
  (27 shorter events, 0.5 us)
Async XLA Ops:
  0.0 1.9 copy-start.3
  184.2 17.1 %copy-start = (bf16[640,2048]{1,0:T(8,128)(2,1)S(1)}, bf16[640,2048]{1,0:T(8,128)(2,1)}, u32[]{:S(2)}) copy-start(bf16[640,2048]{1,0:T(8,128)(2,1)} %layer_gather.2) | copy-start | bytes 7864324
  201.5 2.7 %copy-start.2 = (bf16[2624,1088,1]{0,1,2:T(8,128)(2,1)S(1)}, bf16[2624,1088,1]{0,1,2:T(8,128)(2,1)}, u32[]{:S(2)}) copy-start(bf16[2624,1088,1]{0,1,2:T(8,128)(2,1)} %reshape.79) | copy-start | bytes 17129476
  246.3 1.1 copy-start.1

commit v8 on v7

--- a/solution.py
+++ b/solution.py
@@ -39,16 +39,24 @@
     _greet(sizes, shifts + [(core_shift, 0)])
     mesh = pl.DeviceIdType.MESH
 
+    bs = band_ref.shape[2]
+
+    def window(j, start, count):
+        odd = lax.rem(start, 2)
+        first = pl.multiple_of((start - odd) * bs, 2 * bs)
+        return band_ref.at[odd, j, :, pl.ds(first, count * bs)]
+
     def row_copy(j, start, count, dst, send, recv, target):
         return pltpu.make_async_remote_copy(
-            src_ref=band_ref.at[j, pl.ds(start, count)], dst_ref=dst,
+            src_ref=window(j, start, count), dst_ref=dst,
             send_sem=send, recv_sem=recv, device_id=target, device_id_type=mesh,
         )
 
     def group(dst_rows, count, send, recv, target):
         return pltpu.make_async_remote_copy(
-            src_ref=band_ref.at[pl.ds(0, dst_rows.shape[0]), pl.ds(0, count)], dst_ref=dst_rows,
-            send_sem=send, recv_sem=recv, device_id=target, device_id_type=mesh,
+            src_ref=band_ref.at[0, pl.ds(0, dst_rows.shape[0]), :, pl.ds(0, count * bs)],
+            dst_ref=dst_rows, send_sem=send, recv_sem=recv, device_id=target,
+            device_id_type=mesh,
         )
 
     waits = []
@@ -73,7 +81,7 @@
         pair_groups.append((held, group(held, pair_width, pair_send.at[k], pair_recv.at[k], target)))
     for j in range(block_rows):
         start = me * slab_offsets - j + pad_l
-        pltpu.make_async_copy(band_ref.at[j, pl.ds(start, width)],
+        pltpu.make_async_copy(window(j, start, width),
                               out_ref.at[own_start + j], local_sem.at[0]).start()
     forwards = []
     for k, (held, grp) in enumerate(pair_groups):
@@ -84,7 +92,7 @@
         )
         forward.start()
         forwards.append(forward)
-    pltpu.make_async_copy(band_ref.at[pl.ds(0, block_rows), pl.ds(0, width)],
+    pltpu.make_async_copy(band_ref.at[0, pl.ds(0, block_rows), :, pl.ds(0, width * bs)],
                           out_ref.at[pl.ds(own_start, block_rows)], local_sem.at[0]).wait()
     for grp in waits:
         grp.wait()
@@ -96,13 +104,13 @@
 def row_exchange(sizes, plan, total_rows, pair_rows, band):
     (slab_offsets, block_rows, pad_l, width, pair_width, far, own_start,
      steps, pair_steps) = plan
-    blk = band.shape[2:]
+    bs = band.shape[2]
     any_spec = pl.BlockSpec(memory_space=pl.ANY)
     n, m = len(steps), len(pair_steps)
     return pl.pallas_call(
         lambda *refs: _row_exchange_kernel(sizes, plan, *refs),
-        out_shape=(jax.ShapeDtypeStruct((total_rows, width) + blk, band.dtype),
-                   jax.ShapeDtypeStruct((pair_rows, pair_width) + blk, band.dtype)),
+        out_shape=(jax.ShapeDtypeStruct((total_rows, bs, width * bs), band.dtype),
+                   jax.ShapeDtypeStruct((pair_rows, bs, pair_width * bs), band.dtype)),
         in_specs=[any_spec],
         out_specs=(any_spec, any_spec),
         scratch_shapes=[
@@ -208,11 +216,16 @@
     width = slab_offsets + block_rows - 1
     pad_l = total_rows - 1 - half
     far = layers // 2
+    width = width + width % 2
     pair_width = width + slab_offsets
-    span = pad_l + 2 * block_rows + pair_width
-    pad_r = max(0, slab_offsets * (layers - 1) + span - offsets - pad_l)
-    band = own_band.reshape(block_rows, bs, offsets, bs).transpose(0, 2, 1, 3)
-    band = jnp.pad(band, ((0, 0), (pad_l, pad_r), (0, 0), (0, 0)))
+    span = pad_l + 2 * block_rows + pair_width + 2
+    total_blocks = slab_offsets * (layers - 1) + span
+    total_blocks += total_blocks % 2
+    pad_r = total_blocks - offsets - pad_l
+    band = jnp.pad(own_band.reshape(block_rows, bs, offsets * bs),
+                   ((0, 0), (0, 0), (pad_l * bs, pad_r * bs)))
+    moved = jnp.pad(band[:, :, bs:], ((0, 0), (0, 0), (0, bs)))
+    band = jnp.stack([band, moved], axis=0)
     core = lax.rem(layer_id, 2)
 
     below = half
@@ -240,12 +253,12 @@
     plan = (slab_offsets, block_rows, pad_l, width, pair_width, far, below,
             tuple(steps), pair_steps)
     right, pair_buf = row_exchange(sizes, plan, total_rows, 2 * block_rows, band)
-    pair_part = lax.dynamic_slice_in_dim(pair_buf, core * slab_offsets, width, axis=1)
+    pair_part = lax.dynamic_slice_in_dim(pair_buf, core * slab_offsets * bs, width * bs, axis=2)
     right = jnp.concatenate([
         right[:lower_start], pair_part[:block_rows], right[below:below + block_rows],
         pair_part[block_rows:], right[upper_start + block_rows:],
     ], axis=0)
-    right = right.transpose(0, 2, 1, 3).reshape(total_rows * bs, width * bs)
+    right = right.reshape(total_rows * bs, width * bs)
 
     pattern_f = pattern.astype(jnp.float32)[:, None, :, None]
 

time: 253 us -> 161 us (0.64)
  local copies, waits for them, and re-layouts: 83.7 us -> 28.2 us
  Pallas kernels: 148 us -> 105 us
  other arithmetic: 4.34 us -> 11.1 us
  matrix products: 12.3 us -> 15.1 us
    pallas_call x1, Pallas kernels: 103 us -> 59 us  [row_exchange(): pl.pallas_call(lambda *refs: _row_exchange_kernel(sizes, plan, *refs), ou...]
    reshape x3 -> x0, local copies, waits for them, and re-layouts: 30.1 us -> none  [the longest x1 17.1 us: body(): right = right.transpose(0, 2, 1, 3).reshape(total_rows * bs, width * bs)]
    transpose x1 -> x0, local copies, waits for them, and re-layouts: 18.4 us -> none  [body(): right = right.transpose(0, 2, 1, 3).reshape(total_rows * bs, width * bs)]
    another operation x0 -> x1, other arithmetic: none -> 6.8 us  [body(): band = jnp.stack([band, moved], axis=0)]
    unnamed x48 -> x46, local copies, waits for them, and re-layouts: 19.1 us -> 12.8 us
    pad x1 -> x0, local copies, waits for them, and re-layouts: 5.74 us -> none  [body(): band = jnp.pad(band, ((0, 0), (pad_l, pad_r), (0, 0), (0, 0)))]
    slice x0 -> x1, local copies, waits for them, and re-layouts: none -> 3.81 us  [body(): moved = jnp.pad(band[:, :, bs:], ((0, 0), (0, 0), (0, bs)))]
    dot_general x2, matrix products: 12.3 us -> 15.1 us  [product(): dense = jnp.dot(left, right, preferred_element_type=jnp.float32)]
where the time goes in v8:
time: 161 us; the launch traced here: 159 us
  Pallas kernels  105 us (65%)
  local copies, waits for them, and re-layouts  28.2 us (18%)
  matrix products  15.1 us (9%)
  other arithmetic  11.1 us (7%)
    pallas_call x1, Pallas kernels, row_exchange(): pl.pallas_call(lambda *refs: _row_exchange_kernel(sizes, plan, *refs), ou...  59 us
    pallas_call x2, Pallas kernels, layer_gather(): pl.pallas_call(lambda *refs: _layer_gather_kernel(sizes, *refs), out_shap...  45.5 us
    dot_general x2, matrix products, product(): dense = jnp.dot(left, right, preferred_element_type=jnp.float32)  15.1 us
    unnamed x46, local copies, waits for them, and re-layouts  12.8 us
    another operation x1, other arithmetic, body(): band = jnp.stack([band, moved], axis=0)  6.8 us
    mul x2, local copies, waits for them, and re-layouts, product(): return out.reshape(block_rows, bs, slab_offsets, bs) * pattern_f  4 us
    slice x1, local copies, waits for them, and re-layouts, body(): moved = jnp.pad(band[:, :, bs:], ((0, 0), (0, 0), (0, bs)))  3.81 us

profile of v8, /device:TPU:1, one launch (start us, length us, event | category | flops | bytes accessed | tf_op | source)
XLA Modules:
  0.0 159.3 jit_solution(8145317311635481673)
XLA Ops:
  0.0 0.8 fusion.5
  0.8 0.1 copy.3
  0.9 0.3 mul.48
  1.1 0.8 mul.49
  1.9 0.0 copy-done.2
  1.9 1.0 mul.50.refs_0_
  2.9 24.3 %layer_gather.2 = bf16[640,2048]{1,0:T(8,128)(2,1)} custom-call(bf16[640,512]{1,0:T(8,128)(2,1)} %mul.50.refs_0_), custom_call_target="tpu_custom_call" | custom-call | tf_op jit(solution)/shard_map/layer_gather/pallas_call | solution.py:172
  27.2 3.8 %pad_slice_fusion = bf16[10,64,6080]{2,1,0:T(8,128)(2,1)S(1)} fusion(bf16[10,64,2048]{2,1,0:T(8,128)(2,1)} %bitcast.66), kind=kLoop, calls=%fused_computation.1 | loop fusion | bytes 10403840 | tf_op jit(solution)/shard_map/slice | solution.py:227
  31.0 1.8 %pad_bitcast_fusion = (bf16[1,10,64,6144]{3,2,1,0:T(8,128)(2,1)S(1)}, bf16[1,10,64,6144]{3,2,1,0:T(8,128)(2,1)S(1)}) fusion(bf16[10,64,2048]{2,1,0:T(8,128)(2,1)S(1)} %bitcast.67, bf16[10,64,6080]{2,1,0:T(8,128)(2,1)S(1)} %pad_slice_fusion), kind=kLoop, calls=%fused_computation.2 | loop fusion | bytes 26132480 | tf_op jit(solution)/shard_map/stack | solution.py:228
  32.9 6.8 %pad_maximum_fusion.refs_0_ = bf16[2,10,64,6144]{3,2,1,0:T(8,128)(2,1)} fusion(bf16[1,10,64,6144]{3,2,1,0:T(8,128)(2,1)S(1)} %get-tuple-element.32, bf16[1,10,64,6144]{3,2,1,0:T(8,128)(2,1)S(1)} %get-tuple-element.31), kind=kLoop, calls=%fused_computation | loop fusion | flops 7864320 | bytes 31457280 | tf_op jit(solution)/shard_map/stack | solution.py:228
  39.7 59.0 %row_exchange.1 = (bf16[41,64,1152]{2,1,0:T(8,128)(2,1)}, bf16[20,64,1664]{2,1,0:T(8,128)(2,1)}) custom-call(bf16[2,10,64,6144]{3,2,1,0:T(8,128)(2,1)} %pad_maximum_fusion.refs_0_), custom_call_target="tpu_custom_call" | custom-call | tf_op jit(solution)/shard_map/row_exchange/pallas_call | solution.py:110
  98.7 2.2 %slice_dynamic-update-slice_fusion.1 = bf16[41,64,1152]{2,1,0:T(8,128)(2,1)} fusion(bf16[41,64,1152]{2,1,0:T(8,128)(2,1)} %get-tuple-element.7), kind=kLoop, calls=%fused_computation.12 | loop fusion | bytes 1769472
  100.9 2.6 %dynamic-slice_dynamic-update-slice_fusion.1 = bf16[41,64,1152]{2,1,0:T(8,128)(2,1)} fusion(bf16[41,64,1152]{2,1,0:T(8,128)(2,1)} %slice_dynamic-update-slice_fusion.1, bf16[20,64,1664]{2,1,0:T(8,128)(2,1)} %get-tuple-element.8, s32[]{:T(128)S(6)} %select_n.3), kind=kLoop, calls=%fused_computation.5 | loop fusion | bytes 2949124
  103.5 2.6 %slice_dynamic-update-slice_fusion = bf16[41,64,1152]{2,1,0:T(8,128)(2,1)} fusion(bf16[41,64,1152]{2,1,0:T(8,128)(2,1)} %dynamic-slice_dynamic-update-slice_fusion.1, bf16[41,64,1152]{2,1,0:T(8,128)(2,1)} %get-tuple-element.7), kind=kLoop, calls=%fused_computation.6 | loop fusion | bytes 2949120
  106.1 2.6 %dynamic-slice_dynamic-update-slice_fusion = bf16[41,64,1152]{2,1,0:T(8,128)(2,1)} fusion(bf16[41,64,1152]{2,1,0:T(8,128)(2,1)} %slice_dynamic-update-slice_fusion, bf16[20,64,1664]{2,1,0:T(8,128)(2,1)} %get-tuple-element.8, s32[]{:T(128)S(6)} %add.48, s32[]{:T(128)S(6)} %select_n.3), kind=kLoop, calls=%fused_computation.4 | loop fusion | bytes 2949128
  108.7 2.1 %slice_dynamic-update-slice_fusion.2 = bf16[41,64,1152]{2,1,0:T(8,128)(2,1)} fusion(bf16[41,64,1152]{2,1,0:T(8,128)(2,1)} %dynamic-slice_dynamic-update-slice_fusion, bf16[41,64,1152]{2,1,0:T(8,128)(2,1)} %get-tuple-element.7), kind=kLoop, calls=%fused_computation.13 | loop fusion | bytes 1474560 | tf_op jit(solution)/shard_map/concatenate | solution.py:257
  110.8 0.2 fusion.4
  111.0 0.1 bitcast_dynamic-update-slice_fusion.18
  111.2 0.1 bitcast_dynamic-update-slice_fusion.16
  111.4 0.1 bitcast_dynamic-update-slice_fusion.14
  111.6 0.1 bitcast_dynamic-update-slice_fusion.12
  111.8 0.1 bitcast_dynamic-update-slice_fusion.10
  111.9 7.5 %fusion.6 = f32[10,64,1152]{2,1,0:T(8,128)S(1)} fusion(bf16[10,64,2624]{2,1,0:T(8,128)(2,1)S(1)} %bitcast_dynamic-update-slice_fusion.10, bf16[2624,1152,1]{1,0,2:T(8,128)(2,1)} %bitcast.14), kind=kOutput, calls=%fused_computation.57 | convolution fusion | flops 3869245440 | bytes 12353536 | tf_op jit(solution)/shard_map/dot_general | solution.py:268
  119.5 0.1 slice_dynamic-update-slice_fusion.21
  119.6 0.1 slice_dynamic-update-slice_fusion.19
  119.7 0.1 slice_dynamic-update-slice_fusion.17
  119.8 0.1 slice_dynamic-update-slice_fusion.15
  119.9 0.1 slice_dynamic-update-slice_fusion.13
  120.0 0.1 copy.4
  120.1 1.8 %mul.52 = f32[10,64,8,64]{3,2,1,0:T(8,128)} broadcast(f32[10,8]{1,0:T(8,128)S(1)} %copy.4), dimensions={0,2} | broadcast | bytes 1311040 | tf_op jit(solution)/shard_map/mul | solution.py:273
  121.9 2.2 %mul.53 = f32[640,512]{1,0:T(8,128)S(1)} reshape(f32[10,64,8,64]{3,2,1,0:T(8,128)} %mul.52) | data formatting | bytes 2621440 | tf_op jit(solution)/shard_map/mul | solution.py:273
  124.1 1.1 fusion.2.refs_0_
  125.3 21.2 %layer_gather.3 = bf16[640,2048]{1,0:T(8,128)(2,1)} custom-call(bf16[640,512]{1,0:T(8,128)(2,1)} %fusion.2.refs_0_), custom_call_target="tpu_custom_call" | custom-call | tf_op jit(solution)/shard_map/layer_gather/pallas_call | solution.py:172
  146.5 1.8 %fusion.3 = (bf16[64,2048]{1,0:T(8,128)(2,1)S(1)}, bf16[64,2048]{1,0:T(8,128)(2,1)S(1)}, bf16[64,2048]{1,0:T(8,128)(2,1)S(1)}, bf16[64,2048]{1,0:T(8,128)(2,1)S(...) fusion(bf16[640,2048]{1,0:T(8,128)(2,1)} %layer_gather.3), kind=kLoop, calls=%fused_computation.54 | loop fusion | bytes 5242880 | tf_op jit(solution)/shard_map/slice | solution.py:196
  148.4 0.1 bitcast_dynamic-update-slice_fusion.8
  148.6 0.1 bitcast_dynamic-update-slice_fusion.6
  148.8 0.1 bitcast_dynamic-update-slice_fusion.4
  149.0 0.1 bitcast_dynamic-update-slice_fusion.2
  149.1 0.1 bitcast_dynamic-update-slice_fusion
  149.3 7.5 %fusion.7 = f32[10,64,1152]{2,1,0:T(8,128)S(1)} fusion(bf16[10,64,2624]{2,1,0:T(8,128)(2,1)S(1)} %bitcast_dynamic-update-slice_fusion, bf16[2624,1152,1]{1,0,2:T(8,128)(2,1)} %bitcast.14), kind=kOutput, calls=%fused_computation.58 | convolution fusion | flops 3869245440 | bytes 12353536 | tf_op jit(solution)/shard_map/dot_general | solution.py:268
  156.8 0.0 copy-start.1
  156.9 0.1 slice_dynamic-update-slice_fusion.11
  157.0 0.1 slice_dynamic-update-slice_fusion.9
  157.1 0.1 slice_dynamic-update-slice_fusion.7
  157.2 0.1 slice_dynamic-update-slice_fusion.5
  157.3 0.1 slice_dynamic-update-slice_fusion.3
  157.4 0.5 copy-done.1
  157.9 1.4 fusion.1
  (23 shorter events, 0.4 us)
Async XLA Ops:
  0.0 1.9 %copy-start.2 = (bf16[640,512]{1,0:T(8,128)(2,1)S(1)}, bf16[640,512]{1,0:T(8,128)(2,1)}, u32[]{:S(2)}) copy-start(bf16[640,512]{1,0:T(8,128)(2,1)} %param.2) | copy-start | bytes 1966084
  27.2 3.8 %copy-start = (bf16[640,2048]{1,0:T(8,128)(2,1)S(1)}, bf16[640,2048]{1,0:T(8,128)(2,1)}, u32[]{:S(2)}) copy-start(bf16[640,2048]{1,0:T(8,128)(2,1)} %layer_gather.2) | copy-start | bytes 7864324
  156.8 1.1 copy-start.1

commit v9 on v8

--- a/solution.py
+++ b/solution.py
@@ -27,7 +27,7 @@
 
 def _row_exchange_kernel(sizes, plan, *refs):
     (slab_offsets, block_rows, pad_l, width, pair_width, far, own_start,
-     steps, pair_steps) = plan
+     steps, pair_steps, pair_dest) = plan
     band_ref, out_ref, pair_ref = refs[:3]
     send_sem, recv_sem, pair_send, pair_recv, fwd_send, fwd_recv, local_sem = refs[3:]
     me = lax.axis_index("layer")
@@ -99,11 +99,19 @@
     for k, (held, grp) in enumerate(pair_groups):
         grp.wait_send()
         forwards[k].wait()
+    pair_rows = 2 * half_rows
+    cols = pl.ds(pl.multiple_of(core * slab_offsets * bs, 2 * bs), width * bs)
+    for k, (shift, pair_start) in enumerate(pair_steps):
+        pltpu.make_async_copy(pair_ref.at[pl.ds(pair_start, pair_rows), :, cols],
+                              out_ref.at[pl.ds(pair_dest[k], pair_rows)], local_sem.at[0]).start()
+    for k in range(len(pair_steps)):
+        pltpu.make_async_copy(pair_ref.at[pl.ds(0, pair_rows), :, cols],
+                              out_ref.at[pl.ds(pair_dest[k], pair_rows)], local_sem.at[0]).wait()
 
 
 def row_exchange(sizes, plan, total_rows, pair_rows, band):
     (slab_offsets, block_rows, pad_l, width, pair_width, far, own_start,
-     steps, pair_steps) = plan
+     steps, pair_steps, pair_dest) = plan
     bs = band.shape[2]
     any_spec = pl.BlockSpec(memory_space=pl.ANY)
     n, m = len(steps), len(pair_steps)
@@ -251,13 +259,8 @@
         dist += 1
     pair_steps = ((1, 0), (-1, block_rows))
     plan = (slab_offsets, block_rows, pad_l, width, pair_width, far, below,
-            tuple(steps), pair_steps)
+            tuple(steps), pair_steps, (lower_start, upper_start))
     right, pair_buf = row_exchange(sizes, plan, total_rows, 2 * block_rows, band)
-    pair_part = lax.dynamic_slice_in_dim(pair_buf, core * slab_offsets * bs, width * bs, axis=2)
-    right = jnp.concatenate([
-        right[:lower_start], pair_part[:block_rows], right[below:below + block_rows],
-        pair_part[block_rows:], right[upper_start + block_rows:],
-    ], axis=0)
     right = right.reshape(total_rows * bs, width * bs)
 
     pattern_f = pattern.astype(jnp.float32)[:, None, :, None]

time: 161 us -> 240 us (1.49)
  Pallas kernels: 105 us -> 195 us
  local copies, waits for them, and re-layouts: 28.2 us -> 16.9 us
    pallas_call x1, Pallas kernels: 59 us -> 149 us  [row_exchange(): pl.pallas_call(lambda *refs: _row_exchange_kernel(sizes, plan, *refs), ou...]
    unnamed x46 -> x42, local copies, waits for them, and re-layouts: 12.8 us -> 3.56 us
where the time goes in v9:
time: 240 us; the launch traced here: 238 us
  Pallas kernels  195 us (81%)
  local copies, waits for them, and re-layouts  16.9 us (7%)
  matrix products  15 us (6%)
  other arithmetic  11.1 us (5%)
    pallas_call x1, Pallas kernels, row_exchange(): pl.pallas_call(lambda *refs: _row_exchange_kernel(sizes, plan, *refs), ou...  149 us
    pallas_call x2, Pallas kernels, layer_gather(): pl.pallas_call(lambda *refs: _layer_gather_kernel(sizes, *refs), out_shap...  45.5 us
    dot_general x2, matrix products, product(): dense = jnp.dot(left, right, preferred_element_type=jnp.float32)  15 us
    another operation x1, other arithmetic, body(): band = jnp.stack([band, moved], axis=0)  6.8 us

profile of v9, /device:TPU:1, one launch (start us, length us, event | category | flops | bytes accessed | tf_op | source)
XLA Modules:
  0.0 238.5 jit_solution(5098245018722950916)
XLA Ops:
  0.0 0.0 copy-start.2
  0.0 0.8 fusion.5
  0.8 0.1 copy.3
  0.9 0.3 mul.44
  1.1 0.8 mul.45
  1.9 0.0 copy-done.2
  1.9 1.0 mul.46.refs_0_
  2.9 24.3 %layer_gather.2 = bf16[640,2048]{1,0:T(8,128)(2,1)} custom-call(bf16[640,512]{1,0:T(8,128)(2,1)} %mul.46.refs_0_), custom_call_target="tpu_custom_call" | custom-call | tf_op jit(solution)/shard_map/layer_gather/pallas_call | solution.py:180
  27.2 1.8 fusion.4
  29.0 0.0 copy-start
  29.1 0.1 bitcast_dynamic-update-slice_fusion.18
  29.3 0.1 bitcast_dynamic-update-slice_fusion.16
  29.5 0.1 bitcast_dynamic-update-slice_fusion.14
  29.6 0.1 bitcast_dynamic-update-slice_fusion.12
  29.8 0.1 bitcast_dynamic-update-slice_fusion.10
  30.0 0.8 copy-done
  30.8 2.3 pad_slice_fusion
  33.0 1.9 pad_bitcast_fusion
  35.0 6.8 %pad_maximum_fusion.refs_0_ = bf16[2,10,64,6144]{3,2,1,0:T(8,128)(2,1)} fusion(bf16[1,10,64,6144]{3,2,1,0:T(8,128)(2,1)S(1)} %get-tuple-element.30, bf16[1,10,64,6144]{3,2,1,0:T(8,128)(2,1)S(1)} %get-tuple-element.29), kind=kLoop, calls=%fused_computation | loop fusion | flops 7864320 | bytes 31457280 | tf_op jit(solution)/shard_map/stack | solution.py:236
  41.8 149.5 %row_exchange.1 = (bf16[41,64,1152]{2,1,0:T(8,128)(2,1)}, bf16[20,64,1664]{2,1,0:T(8,128)(2,1)}) custom-call(bf16[2,10,64,6144]{3,2,1,0:T(8,128)(2,1)} %pad_maximum_fusion.refs_0_), custom_call_target="tpu_custom_call" | custom-call | tf_op jit(solution)/shard_map/row_exchange/pallas_call | solution.py:118
  191.3 7.5 %fusion.6 = f32[10,64,1152]{2,1,0:T(8,128)S(1)} fusion(bf16[10,64,2624]{2,1,0:T(8,128)(2,1)S(1)} %bitcast_dynamic-update-slice_fusion.10, bf16[2624,1152,1]{1,0,2:T(8,128)(2,1)} %bitcast.68), kind=kOutput, calls=%fused_computation.52 | convolution fusion | flops 3869245440 | bytes 12353536 | tf_op jit(solution)/shard_map/dot_general | solution.py:271
  198.8 0.1 slice_dynamic-update-slice_fusion.18
  198.9 0.1 slice_dynamic-update-slice_fusion.16
  199.0 0.1 slice_dynamic-update-slice_fusion.14
  199.1 0.1 slice_dynamic-update-slice_fusion.12
  199.3 0.1 slice_dynamic-update-slice_fusion.10
  199.4 0.1 copy.4
  199.4 1.8 mul.47
  201.2 2.0 mul.48
  203.3 1.1 fusion.2.refs_0_
  204.4 21.2 %layer_gather.3 = bf16[640,2048]{1,0:T(8,128)(2,1)} custom-call(bf16[640,512]{1,0:T(8,128)(2,1)} %fusion.2.refs_0_), custom_call_target="tpu_custom_call" | custom-call | tf_op jit(solution)/shard_map/layer_gather/pallas_call | solution.py:180
  225.6 1.8 fusion.3
  227.5 0.1 bitcast_dynamic-update-slice_fusion.8
  227.7 0.1 bitcast_dynamic-update-slice_fusion.6
  227.9 0.1 bitcast_dynamic-update-slice_fusion.4
  228.1 0.1 bitcast_dynamic-update-slice_fusion.2
  228.3 0.1 bitcast_dynamic-update-slice_fusion
  228.4 7.5 %fusion.7 = f32[10,64,1152]{2,1,0:T(8,128)S(1)} fusion(bf16[10,64,2624]{2,1,0:T(8,128)(2,1)S(1)} %bitcast_dynamic-update-slice_fusion, bf16[2624,1152,1]{1,0,2:T(8,128)(2,1)} %bitcast.69), kind=kOutput, calls=%fused_computation.53 | convolution fusion | flops 3869245440 | bytes 12353536 | tf_op jit(solution)/shard_map/dot_general | solution.py:271
  236.0 0.0 copy-start.1
  236.0 0.1 slice_dynamic-update-slice_fusion.8
  236.1 0.1 slice_dynamic-update-slice_fusion.6
  236.2 0.1 slice_dynamic-update-slice_fusion.4
  236.3 0.1 slice_dynamic-update-slice_fusion.2
  236.5 0.1 slice_dynamic-update-slice_fusion
  236.6 0.5 copy-done.1
  237.0 1.4 fusion.1
  (20 shorter events, 0.4 us)
Async XLA Ops:
  0.0 1.9 copy-start.2
  29.0 1.7 copy-start
  236.0 1.1 copy-start.1

commit v10 on v8

--- a/solution.py
+++ b/solution.py
@@ -29,7 +29,7 @@
     (slab_offsets, block_rows, pad_l, width, pair_width, far, own_start,
      steps, pair_steps) = plan
     band_ref, out_ref, pair_ref = refs[:3]
-    send_sem, recv_sem, pair_send, pair_recv, fwd_send, fwd_recv, local_sem = refs[3:]
+    send_sem, recv_sem, pair_send, pair_recv, fwd_send, fwd_recv, local_sem, stage = refs[3:]
     me = lax.axis_index("layer")
     core = lax.rem(me, 2)
     core_shift = 1 - 2 * core
@@ -81,8 +81,7 @@
         pair_groups.append((held, group(held, pair_width, pair_send.at[k], pair_recv.at[k], target)))
     for j in range(block_rows):
         start = me * slab_offsets - j + pad_l
-        pltpu.make_async_copy(window(j, start, width),
-                              out_ref.at[own_start + j], local_sem.at[0]).start()
+        pltpu.make_async_copy(window(j, start, width), stage.at[j], local_sem.at[0]).start()
     forwards = []
     for k, (held, grp) in enumerate(pair_groups):
         grp.wait_recv()
@@ -93,12 +92,16 @@
         forward.start()
         forwards.append(forward)
     pltpu.make_async_copy(band_ref.at[0, pl.ds(0, block_rows), :, pl.ds(0, width * bs)],
-                          out_ref.at[pl.ds(own_start, block_rows)], local_sem.at[0]).wait()
+                          stage, local_sem.at[0]).wait()
+    own_out = pltpu.make_async_copy(stage, out_ref.at[pl.ds(own_start, block_rows)],
+                                    local_sem.at[1])
+    own_out.start()
     for grp in waits:
         grp.wait()
     for k, (held, grp) in enumerate(pair_groups):
         grp.wait_send()
         forwards[k].wait()
+    own_out.wait()
 
 
 def row_exchange(sizes, plan, total_rows, pair_rows, band):
@@ -120,7 +123,8 @@
             pltpu.SemaphoreType.DMA((m,)),
             pltpu.SemaphoreType.DMA((m,)),
             pltpu.SemaphoreType.DMA((m,)),
-            pltpu.SemaphoreType.DMA((1,)),
+            pltpu.SemaphoreType.DMA((2,)),
+            pltpu.VMEM((block_rows, bs, width * bs), band.dtype),
         ],
         compiler_params=pltpu.CompilerParams(collective_id=0, has_side_effects=True),
         name="row_exchange",
@@ -128,7 +132,7 @@
 
 
 def _layer_gather_kernel(sizes, *refs):
-    src_ref, out_ref, send_sem, recv_sem, local_sem = refs
+    src_ref, out_ref, send_sem, recv_sem = refs
     count = sizes[0]
     me = lax.axis_index("layer")
     width = src_ref.shape[1]
@@ -150,8 +154,6 @@
     )
     to_far.start()
     to_core.start()
-    local = pltpu.make_async_copy(src_ref, mine, local_sem.at[0])
-    local.start()
     far_layer = lax.rem(me + far, count)
     to_far.wait_recv()
     forward = pltpu.make_async_remote_copy(
@@ -160,7 +162,6 @@
         device_id_type=pl.DeviceIdType.MESH,
     )
     forward.start()
-    local.wait()
     to_far.wait_send()
     to_core.wait()
     forward.wait()
@@ -169,7 +170,7 @@
 def layer_gather(sizes, slab, collective_id):
     count = sizes[0]
     any_spec = pl.BlockSpec(memory_space=pl.ANY)
-    return pl.pallas_call(
+    others = pl.pallas_call(
         lambda *refs: _layer_gather_kernel(sizes, *refs),
         out_shape=jax.ShapeDtypeStruct((slab.shape[0], slab.shape[1] * count), slab.dtype),
         in_specs=[any_spec],
@@ -177,11 +178,12 @@
         scratch_shapes=[
             pltpu.SemaphoreType.DMA((3,)),
             pltpu.SemaphoreType.DMA((3,)),
-            pltpu.SemaphoreType.DMA((1,)),
         ],
         compiler_params=pltpu.CompilerParams(collective_id=collective_id, has_side_effects=True),
         name="layer_gather",
     )(slab)
+    me = lax.axis_index("layer")
+    return lax.dynamic_update_slice_in_dim(others, slab, me * slab.shape[1], axis=1)
 
 
 def shifted(value, axis, steps):

time: 161 us -> 154 us (0.957)
  matrix products: 15.1 us -> 9.56 us
  Pallas kernels: 105 us -> 101 us
  local copies, waits for them, and re-layouts: 28.2 us -> 31.9 us
    dot_general x2, matrix products: 15.1 us -> 9.56 us  [product(): dense = jnp.dot(left, right, preferred_element_type=jnp.float32)]
    pallas_call x2, Pallas kernels: 45.5 us -> 40.1 us  [layer_gather(): pl.pallas_call(lambda *refs: _layer_gather_kernel(sizes, *refs), out_shap...]
    dynamic_update_slice x0 -> x2, local copies, waits for them, and re-layouts: none -> 1.89 us  [layer_gather(): lax.dynamic_update_slice_in_dim(others, slab, me * slab.shape[1], axis=1)]
    unnamed x46 -> x54, local copies, waits for them, and re-layouts: 12.8 us -> 14 us
where the time goes in v10:
time: 154 us
  Pallas kernels  101 us (66%)
  local copies, waits for them, and re-layouts  31.9 us (21%)
  other arithmetic  11.1 us (7%)
  matrix products  9.56 us (6%)
    pallas_call x1, Pallas kernels, row_exchange(): pl.pallas_call(lambda *refs: _row_exchange_kernel(sizes, plan, *refs), ou...  60.4 us
    pallas_call x2, Pallas kernels, layer_gather(): pl.pallas_call(lambda *refs: _layer_gather_kernel(sizes, *refs), out_shap...  40.1 us
    unnamed x54, local copies, waits for them, and re-layouts  14 us
    dot_general x2, matrix products, product(): dense = jnp.dot(left, right, preferred_element_type=jnp.float32)  9.56 us
    another operation x1, other arithmetic, body(): band = jnp.stack([band, moved], axis=0)  6.73 us
    mul x2, local copies, waits for them, and re-layouts, product(): return out.reshape(block_rows, bs, slab_offsets, bs) * pattern_f  4.02 us
    slice x1, local copies, waits for them, and re-layouts, body(): moved = jnp.pad(band[:, :, bs:], ((0, 0), (0, 0), (0, bs)))  3.81 us

profile of v10, /device:TPU:1, one launch (start us, length us, event | category | flops | bytes accessed | tf_op | source)
XLA Modules:
  0.0 153.5 jit_solution(17086013026228402881)
XLA Ops:
  0.0 0.8 fusion.5
  0.8 0.1 copy.3
  0.9 0.3 mul.52
  1.1 0.8 mul.53
  1.9 1.0 mul.54.refs_0_
  2.9 20.7 %layer_gather.2 = bf16[640,2048]{1,0:T(8,128)(2,1)} custom-call(bf16[640,512]{1,0:T(8,128)(2,1)} %mul.54.refs_0_), custom_call_target="tpu_custom_call" | custom-call | tf_op jit(solution)/shard_map/layer_gather/pallas_call | solution.py:173
  23.6 0.9 constant_dynamic-update-slice_fusion.1
  24.6 3.8 %pad_slice_fusion = bf16[10,64,6080]{2,1,0:T(8,128)(2,1)S(1)} fusion(bf16[10,64,2048]{2,1,0:T(8,128)(2,1)} %bitcast.66), kind=kLoop, calls=%fused_computation.1 | loop fusion | bytes 10403840 | tf_op jit(solution)/shard_map/slice | solution.py:229
  28.4 1.8 %pad_bitcast_fusion = (bf16[1,10,64,6144]{3,2,1,0:T(8,128)(2,1)S(1)}, bf16[1,10,64,6144]{3,2,1,0:T(8,128)(2,1)S(1)}) fusion(bf16[10,64,2048]{2,1,0:T(8,128)(2,1)S(1)} %bitcast.67, bf16[10,64,6080]{2,1,0:T(8,128)(2,1)S(1)} %pad_slice_fusion), kind=kLoop, calls=%fused_computation.2 | loop fusion | bytes 26132480 | tf_op jit(solution)/shard_map/stack | solution.py:230
  30.3 6.7 %pad_maximum_fusion.refs_0_ = bf16[2,10,64,6144]{3,2,1,0:T(8,128)(2,1)} fusion(bf16[1,10,64,6144]{3,2,1,0:T(8,128)(2,1)S(1)} %get-tuple-element.32, bf16[1,10,64,6144]{3,2,1,0:T(8,128)(2,1)S(1)} %get-tuple-element.31), kind=kLoop, calls=%fused_computation | loop fusion | flops 7864320 | bytes 31457280 | tf_op jit(solution)/shard_map/stack | solution.py:230
  37.0 60.4 %row_exchange.1 = (bf16[41,64,1152]{2,1,0:T(8,128)(2,1)}, bf16[20,64,1664]{2,1,0:T(8,128)(2,1)}) custom-call(bf16[2,10,64,6144]{3,2,1,0:T(8,128)(2,1)} %pad_maximum_fusion.refs_0_), custom_call_target="tpu_custom_call" | custom-call | tf_op jit(solution)/shard_map/row_exchange/pallas_call | solution.py:113
  97.4 2.2 %slice_dynamic-update-slice_fusion.1 = bf16[41,64,1152]{2,1,0:T(8,128)(2,1)} fusion(bf16[41,64,1152]{2,1,0:T(8,128)(2,1)} %get-tuple-element.7), kind=kLoop, calls=%fused_computation.12 | loop fusion | bytes 1769472
  99.5 2.6 %dynamic-slice_dynamic-update-slice_fusion.1 = bf16[41,64,1152]{2,1,0:T(8,128)(2,1)} fusion(bf16[41,64,1152]{2,1,0:T(8,128)(2,1)} %slice_dynamic-update-slice_fusion.1, bf16[20,64,1664]{2,1,0:T(8,128)(2,1)} %get-tuple-element.8, s32[]{:T(128)S(6)} %select_n.8), kind=kLoop, calls=%fused_computation.5 | loop fusion | bytes 2949124
  102.1 2.6 %slice_dynamic-update-slice_fusion = bf16[41,64,1152]{2,1,0:T(8,128)(2,1)} fusion(bf16[41,64,1152]{2,1,0:T(8,128)(2,1)} %dynamic-slice_dynamic-update-slice_fusion.1, bf16[41,64,1152]{2,1,0:T(8,128)(2,1)} %get-tuple-element.7), kind=kLoop, calls=%fused_computation.6 | loop fusion | bytes 2949120
  104.7 2.6 %dynamic-slice_dynamic-update-slice_fusion = bf16[41,64,1152]{2,1,0:T(8,128)(2,1)} fusion(bf16[41,64,1152]{2,1,0:T(8,128)(2,1)} %slice_dynamic-update-slice_fusion, bf16[20,64,1664]{2,1,0:T(8,128)(2,1)} %get-tuple-element.8, s32[]{:T(128)S(6)} %add.53, s32[]{:T(128)S(6)} %select_n.8), kind=kLoop, calls=%fused_computation.4 | loop fusion | bytes 2949128
  107.3 2.1 %slice_dynamic-update-slice_fusion.2 = bf16[41,64,1152]{2,1,0:T(8,128)(2,1)} fusion(bf16[41,64,1152]{2,1,0:T(8,128)(2,1)} %dynamic-slice_dynamic-update-slice_fusion, bf16[41,64,1152]{2,1,0:T(8,128)(2,1)} %get-tuple-element.7), kind=kLoop, calls=%fused_computation.13 | loop fusion | bytes 1474560 | tf_op jit(solution)/shard_map/concatenate | solution.py:259
  109.4 0.2 fusion.4
  109.6 0.1 bitcast_dynamic-update-slice_fusion.18
  109.8 0.1 bitcast_dynamic-update-slice_fusion.16
  110.0 0.1 bitcast_dynamic-update-slice_fusion.14
  110.2 0.1 bitcast_dynamic-update-slice_fusion.12
  110.4 0.1 bitcast_dynamic-update-slice_fusion.10
  110.5 1.8 %copy-done.4 = bf16[41,64,1152]{2,1,0:T(8,128)(2,1)S(1)} copy-done((bf16[41,64,1152]{2,1,0:T(8,128)(2,1)S(1)}, bf16[41,64,1152]{2,1,0:T(8,128)(2,1)}, u32[]{:S(2)}) %copy-start.4) | copy-done | bytes 6045720
  112.3 4.8 %fusion.6 = f32[10,64,1152]{2,1,0:T(8,128)S(1)} fusion(bf16[10,64,2624]{2,1,0:T(8,128)(2,1)S(1)} %bitcast_dynamic-update-slice_fusion.10, bf16[2624,1152,1]{1,0,2:T(8,128)(2,1)S(1)} %bitcast.68), kind=kOutput, calls=%fused_computation.59 | convolution fusion | flops 3869245440 | bytes 12353536 | tf_op jit(solution)/shard_map/dot_general | solution.py:270
  117.1 0.1 slice_dynamic-update-slice_fusion.21
  117.2 0.1 slice_dynamic-update-slice_fusion.19
  117.4 0.1 slice_dynamic-update-slice_fusion.17
  117.5 0.1 slice_dynamic-update-slice_fusion.15
  117.6 0.1 slice_dynamic-update-slice_fusion.13
  117.7 0.1 copy.4
  117.8 1.8 %mul.57 = f32[10,64,8,64]{3,2,1,0:T(8,128)} broadcast(f32[10,8]{1,0:T(8,128)S(1)} %copy.4), dimensions={0,2} | broadcast | bytes 1311040 | tf_op jit(solution)/shard_map/mul | solution.py:275
  119.6 2.2 %mul.58 = f32[640,512]{1,0:T(8,128)S(1)} reshape(f32[10,64,8,64]{3,2,1,0:T(8,128)} %mul.57) | data formatting | bytes 2621440 | tf_op jit(solution)/shard_map/mul | solution.py:275
  121.8 1.1 fusion.2.refs_0_
  123.0 19.4 %layer_gather.3 = bf16[640,2048]{1,0:T(8,128)(2,1)} custom-call(bf16[640,512]{1,0:T(8,128)(2,1)} %fusion.2.refs_0_), custom_call_target="tpu_custom_call" | custom-call | tf_op jit(solution)/shard_map/layer_gather/pallas_call | solution.py:173
  142.4 0.9 constant_dynamic-update-slice_fusion
  143.4 2.4 %fusion.3 = (bf16[64,2048]{1,0:T(8,128)(2,1)S(1)}, bf16[64,2048]{1,0:T(8,128)(2,1)S(1)}, bf16[64,2048]{1,0:T(8,128)(2,1)S(1)}, bf16[64,2048]{1,0:T(8,128)(2,1)S(...) fusion(bf16[640,2048]{1,0:T(8,128)(2,1)} %constant_dynamic-upda, ...), kind=kLoop, calls=%fused_computation.56 | loop fusion | bytes 5242880 | tf_op jit(solution)/shard_map/slice | solution.py:198
  145.8 0.1 bitcast_dynamic-update-slice_fusion.8
  146.0 0.1 bitcast_dynamic-update-slice_fusion.6
  146.2 0.1 bitcast_dynamic-update-slice_fusion.4
  146.3 0.1 bitcast_dynamic-update-slice_fusion.2
  146.5 0.1 bitcast_dynamic-update-slice_fusion
  146.7 4.8 %fusion.7 = f32[10,64,1152]{2,1,0:T(8,128)S(1)} fusion(bf16[10,64,2624]{2,1,0:T(8,128)(2,1)S(1)} %bitcast_dynamic-update-slice_fusion, bf16[2624,1152,1]{1,0,2:T(8,128)(2,1)S(1)} %bitcast.71), kind=kOutput, calls=%fused_computation.60 | convolution fusion | flops 3869245440 | bytes 12353536 | tf_op jit(solution)/shard_map/dot_general | solution.py:270
  151.5 0.1 slice_dynamic-update-slice_fusion.11
  151.6 0.1 slice_dynamic-update-slice_fusion.9
  151.8 0.1 slice_dynamic-update-slice_fusion.7
  151.9 0.1 slice_dynamic-update-slice_fusion.5
  152.0 0.1 slice_dynamic-update-slice_fusion.3
  152.1 1.5 fusion.1
  (34 shorter events, 0.4 us)
Async XLA Ops:
  0.0 1.9 %copy-start.3 = (bf16[640,512]{1,0:T(8,128)(2,1)S(1)}, bf16[640,512]{1,0:T(8,128)(2,1)}, u32[]{:S(2)}) copy-start(bf16[640,512]{1,0:T(8,128)(2,1)} %param.2) | copy-start | bytes 1966084
  2.9 20.7 %copy-start.2 = (bf16[640,512]{1,0:T(8,128)(2,1)S(1)}, bf16[640,512]{1,0:T(8,128)(2,1)}, u32[]{:S(2)}) copy-start(bf16[640,512]{1,0:T(8,128)(2,1)} %mul.54.refs_0_) | copy-start | bytes 1966084
  24.6 3.8 %copy-start = (bf16[640,2048]{1,0:T(8,128)(2,1)S(1)}, bf16[640,2048]{1,0:T(8,128)(2,1)}, u32[]{:S(2)}) copy-start(bf16[640,2048]{1,0:T(8,128)(2,1)} %constant_dynamic-update-slice_fusion.1) | copy-start | bytes 7864324
  109.6 2.7 %copy-start.4 = (bf16[41,64,1152]{2,1,0:T(8,128)(2,1)S(1)}, bf16[41,64,1152]{2,1,0:T(8,128)(2,1)}, u32[]{:S(2)}) copy-start(bf16[41,64,1152]{2,1,0:T(8,128)(2,1)} %slice_dynamic-update-slice_fusion.2) | copy-start | bytes 18137092
  122.9 19.5 %copy-start.1 = (bf16[640,512]{1,0:T(8,128)(2,1)S(1)}, bf16[640,512]{1,0:T(8,128)(2,1)}, u32[]{:S(2)}) copy-start(bf16[640,512]{1,0:T(8,128)(2,1)} %fusion.2.refs_0_) | copy-start | bytes 1966084
  142.4 4.3 %slice-start = ((s8[6045696]{0:T(1024)(128)(4,1)}), s8[4194304]{0:T(1024)(128)(4,1)S(1)}, s32[]{:S(2)}) async-start(s8[6045696]{0:T(1024)(128)(4,1)} %bitcast.69), calls=%async_computation | async-start | bytes 8388608
  143.4 3.3 %slice-start.1 = ((s8[6045696]{0:T(1024)(128)(4,1)}), s8[1851392]{0:T(1024)(128)(4,1)S(1)}, s32[]{:S(2)}) async-start(s8[6045696]{0:T(1024)(128)(4,1)} %bitcast.69), calls=%async_computation.1 | async-start | bytes 3702784

commit v11 on v10

--- a/solution.py
+++ b/solution.py
@@ -68,29 +68,54 @@
                      send_sem.at[k], recv_sem.at[k], target).start()
         waits.append(group(out_ref.at[pl.ds(row_start, last - first)], width,
                            send_sem.at[k], recv_sem.at[k], target))
-    pair_groups = []
+    x_me = me // far
     pair_base = (lax.rem(me + far, sizes[0]) - core) * slab_offsets
+    offsets = slab_offsets * sizes[0]
+
+    def rect(shift, half):
+        lo, hi = pair_width, 0
+        for j in range(block_rows):
+            b = 2 * slab_offsets * half + block_rows * shift - j
+            lo = min(lo, max(0, -b))
+            hi = max(hi, min(pair_width, offsets - b))
+        lo -= lo % 2
+        hi = min(pair_width, hi + hi % 2)
+        return lo, hi - lo
+
+    def held_cols(pair_start, c0, cw):
+        return pair_ref.at[pl.ds(pair_start + core * half_rows, half_rows), :, pl.ds(c0 * bs, cw * bs)]
+
     for k, (shift, pair_start) in enumerate(pair_steps):
         target = _peer(sizes, far, shift)
-        for jj in range(half_rows):
-            j = core * half_rows + jj
-            start = pair_base + block_rows * shift - j + pad_l
-            row_copy(j, start, pair_width, pair_ref.at[pair_start + j],
-                     pair_send.at[k], pair_recv.at[k], target).start()
-        held = pair_ref.at[pl.ds(pair_start + core * half_rows, half_rows)]
-        pair_groups.append((held, group(held, pair_width, pair_send.at[k], pair_recv.at[k], target)))
+        for half in range(2):
+            c0, cw = rect(shift, half)
+
+            @pl.when(x_me == 1 - half)
+            def _():
+                for jj in range(half_rows):
+                    j = core * half_rows + jj
+                    start = pair_base + block_rows * shift - j + pad_l + c0
+                    row_copy(j, start, cw, pair_ref.at[pair_start + j, :, pl.ds(c0 * bs, cw * bs)],
+                             pair_send.at[k], pair_recv.at[k], target).start()
     for j in range(block_rows):
         start = me * slab_offsets - j + pad_l
         pltpu.make_async_copy(window(j, start, width), stage.at[j], local_sem.at[0]).start()
-    forwards = []
-    for k, (held, grp) in enumerate(pair_groups):
-        grp.wait_recv()
-        forward = pltpu.make_async_remote_copy(
+    def forward(k, held):
+        return pltpu.make_async_remote_copy(
             src_ref=held, dst_ref=held, send_sem=fwd_send.at[k], recv_sem=fwd_recv.at[k],
             device_id=_peer(sizes, core_shift, 0), device_id_type=mesh,
         )
-        forward.start()
-        forwards.append(forward)
+
+    for k, (shift, pair_start) in enumerate(pair_steps):
+        target = _peer(sizes, far, shift)
+        for half in range(2):
+            c0, cw = rect(shift, half)
+
+            @pl.when(x_me == half)
+            def _():
+                held = held_cols(pair_start, c0, cw)
+                group(held, cw, pair_send.at[k], pair_recv.at[k], target).wait_recv()
+                forward(k, held).start()
     pltpu.make_async_copy(band_ref.at[0, pl.ds(0, block_rows), :, pl.ds(0, width * bs)],
                           stage, local_sem.at[0]).wait()
     own_out = pltpu.make_async_copy(stage, out_ref.at[pl.ds(own_start, block_rows)],
@@ -98,9 +123,19 @@
     own_out.start()
     for grp in waits:
         grp.wait()
-    for k, (held, grp) in enumerate(pair_groups):
-        grp.wait_send()
-        forwards[k].wait()
+    for k, (shift, pair_start) in enumerate(pair_steps):
+        target = _peer(sizes, far, shift)
+        for half in range(2):
+            c0, cw = rect(shift, half)
+
+            @pl.when(x_me == 1 - half)
+            def _():
+                group(held_cols(pair_start, c0, cw), cw, pair_send.at[k], pair_recv.at[k],
+                      target).wait_send()
+
+            @pl.when(x_me == half)
+            def _():
+                forward(k, held_cols(pair_start, c0, cw)).wait()
     own_out.wait()
 
 
@@ -260,6 +295,11 @@
         right[:lower_start], pair_part[:block_rows], right[below:below + block_rows],
         pair_part[block_rows:], right[upper_start + block_rows:],
     ], axis=0)
+    t_ids = lax.broadcasted_iota(jnp.int32, (total_rows, 1, width, 1), 0)
+    u_ids = lax.broadcasted_iota(jnp.int32, (total_rows, 1, width, 1), 2)
+    b_ids = layer_id * slab_offsets + half + u_ids - t_ids
+    inside = (b_ids >= 0) & (b_ids < offsets)
+    right = jnp.where(inside, right.reshape(total_rows, bs, width, bs), jnp.zeros((), right.dtype))
     right = right.reshape(total_rows * bs, width * bs)
 
     pattern_f = pattern.astype(jnp.float32)[:, None, :, None]

time: 154 us -> 202 us (1.31)
  local copies, waits for them, and re-layouts: 31.9 us -> 76 us
  matrix products: 9.56 us -> 14.8 us
  Pallas kernels: 101 us -> 98 us
    broadcast_in_dim x0 -> x2, local copies, waits for them, and re-layouts: none -> 21.6 us  [body(): jnp.where(inside, right.reshape(total_rows, bs, width, bs), jnp.zeros((),...]
    unnamed x54 -> x56, local copies, waits for them, and re-layouts: 14 us -> 25.9 us
    reshape x0 -> x1, local copies, waits for them, and re-layouts: none -> 9.26 us  [body(): right.reshape(total_rows, bs, width, bs)]
    dot_general x2, matrix products: 9.56 us -> 14.8 us  [product(): dense = jnp.dot(left, right, preferred_element_type=jnp.float32)]
    pallas_call x1, Pallas kernels: 60.4 us -> 57.8 us  [row_exchange(): pl.pallas_call(lambda *refs: _row_exchange_kernel(sizes, plan, *refs), ou...]
where the time goes in v11:
time: 202 us
  Pallas kernels  98 us (49%)
  local copies, waits for them, and re-layouts  76 us (38%)
  matrix products  14.8 us (7%)
  other arithmetic  12.4 us (6%)
    pallas_call x1, Pallas kernels, row_exchange(): pl.pallas_call(lambda *refs: _row_exchange_kernel(sizes, plan, *refs), ou...  57.8 us
    pallas_call x2, Pallas kernels, layer_gather(): pl.pallas_call(lambda *refs: _layer_gather_kernel(sizes, *refs), out_shap...  40.1 us
    unnamed x56, local copies, waits for them, and re-layouts  25.9 us
    broadcast_in_dim x2, local copies, waits for them, and re-layouts, body(): jnp.where(inside, right.reshape(total_rows, bs, width, bs), jnp.zeros((),...  21.6 us
    dot_general x2, matrix products, product(): dense = jnp.dot(left, right, preferred_element_type=jnp.float32)  14.8 us
    reshape x1, local copies, waits for them, and re-layouts, body(): right.reshape(total_rows, bs, width, bs)  9.26 us
    another operation x1, other arithmetic, body(): band = jnp.stack([band, moved], axis=0)  6.74 us

profile of v11, /device:TPU:1, one launch (start us, length us, event | category | flops | bytes accessed | tf_op | source)
XLA Modules:
  0.0 201.6 jit_solution(13865096458602116525)
XLA Ops:
  0.0 0.8 fusion.18
  0.9 0.3 mul.55
  1.1 0.8 mul.56
  1.9 1.0 mul.57.refs_0_
  2.9 20.7 %layer_gather.2 = bf16[640,2048]{1,0:T(8,128)(2,1)} custom-call(bf16[640,512]{1,0:T(8,128)(2,1)} %mul.57.refs_0_), custom_call_target="tpu_custom_call" | custom-call | tf_op jit(solution)/shard_map/layer_gather/pallas_call | solution.py:208
  23.6 0.9 constant_dynamic-update-slice_fusion.1
  24.6 3.8 %pad_slice_fusion = bf16[10,64,6080]{2,1,0:T(8,128)(2,1)S(1)} fusion(bf16[10,64,2048]{2,1,0:T(8,128)(2,1)} %bitcast.70), kind=kLoop, calls=%fused_computation.1 | loop fusion | bytes 10403840 | tf_op jit(solution)/shard_map/slice | solution.py:264
  28.4 1.8 pad_bitcast_fusion
  30.3 6.7 %pad_maximum_fusion.refs_0_ = bf16[2,10,64,6144]{3,2,1,0:T(8,128)(2,1)} fusion(bf16[1,10,64,6144]{3,2,1,0:T(8,128)(2,1)S(1)} %get-tuple-element.32, bf16[1,10,64,6144]{3,2,1,0:T(8,128)(2,1)S(1)} %get-tuple-element.31), kind=kLoop, calls=%fused_computation | loop fusion | flops 7864320 | bytes 31457280 | tf_op jit(solution)/shard_map/stack | solution.py:265
  37.0 57.8 %row_exchange.1 = (bf16[41,64,1152]{2,1,0:T(8,128)(2,1)}, bf16[20,64,1664]{2,1,0:T(8,128)(2,1)}) custom-call(bf16[2,10,64,6144]{3,2,1,0:T(8,128)(2,1)} %pad_maximum_fusion.refs_0_), custom_call_target="tpu_custom_call" | custom-call | tf_op jit(solution)/shard_map/row_exchange/pallas_call | solution.py:148
  94.8 2.1 %slice_dynamic-update-slice_fusion.1 = bf16[41,64,1152]{2,1,0:T(8,128)(2,1)} fusion(bf16[41,64,1152]{2,1,0:T(8,128)(2,1)} %get-tuple-element.7), kind=kLoop, calls=%fused_computation.20 | loop fusion | bytes 1769472
  97.0 2.6 %dynamic-slice_dynamic-update-slice_fusion.1 = bf16[41,64,1152]{2,1,0:T(8,128)(2,1)} fusion(bf16[41,64,1152]{2,1,0:T(8,128)(2,1)} %slice_dynamic-update-slice_fusion.1, bf16[20,64,1664]{2,1,0:T(8,128)(2,1)} %get-tuple-element.8, s32[]{:T(128)S(6)} %select_n.16), kind=kLoop, calls=%fused_computation.13 | loop fusion | bytes 2949124
  99.6 2.6 %slice_dynamic-update-slice_fusion = bf16[41,64,1152]{2,1,0:T(8,128)(2,1)} fusion(bf16[41,64,1152]{2,1,0:T(8,128)(2,1)} %dynamic-slice_dynamic-update-slice_fusion.1, bf16[41,64,1152]{2,1,0:T(8,128)(2,1)} %get-tuple-element.7), kind=kLoop, calls=%fused_computation.14 | loop fusion | bytes 2949120
  102.2 2.6 %dynamic-slice_dynamic-update-slice_fusion = bf16[41,64,1152]{2,1,0:T(8,128)(2,1)} fusion(bf16[41,64,1152]{2,1,0:T(8,128)(2,1)} %slice_dynamic-update-slice_fusion, bf16[20,64,1664]{2,1,0:T(8,128)(2,1)} %get-tuple-element.8, s32[]{:T(128)S(6)} %add.66, s32[]{:T(128)S(6)} %select_n.16), kind=kLoop, calls=%fused_computation.12 | loop fusion | bytes 2949128
  104.8 2.1 %slice_dynamic-update-slice_fusion.2 = bf16[41,64,1152]{2,1,0:T(8,128)(2,1)} fusion(bf16[41,64,1152]{2,1,0:T(8,128)(2,1)} %dynamic-slice_dynamic-update-slice_fusion, bf16[41,64,1152]{2,1,0:T(8,128)(2,1)} %get-tuple-element.7), kind=kLoop, calls=%fused_computation.21 | loop fusion | bytes 1474560 | tf_op jit(solution)/shard_map/concatenate | solution.py:294
  106.9 9.3 %copy.6 = bf16[2624,1152]{0,1:T(8,128)(2,1)} copy(bf16[2624,1152]{1,0:T(8,128)(2,1)} %bitcast.13) | data formatting | bytes 12091392 | tf_op jit(solution)/shard_map/reshape | solution.py:302
  116.4 0.8 bitcast_dynamic-update-slice_fusion.19
  117.1 0.9 bitcast_dynamic-update-slice_fusion.18
  118.0 0.7 bitcast_dynamic-update-slice_fusion.17
  118.8 0.9 bitcast_dynamic-update-slice_fusion.16
  119.6 0.8 bitcast_dynamic-update-slice_fusion.15
  120.4 0.9 bitcast_dynamic-update-slice_fusion.14
  121.3 0.8 bitcast_dynamic-update-slice_fusion.13
  122.1 0.9 bitcast_dynamic-update-slice_fusion.12
  122.9 0.7 bitcast_dynamic-update-slice_fusion.11
  123.7 0.9 bitcast_dynamic-update-slice_fusion.10
  124.7 4.8 %broadcast_in_dim.16 = pred[41,64,18,64]{1,0,3,2:T(8,128)(4,1)} broadcast(pred[41,18]{0,1:T(8,128)(4,1)S(1)} %fusion.13), dimensions={0,2} | broadcast | bytes 3023586 | tf_op jit(solution)/shard_map/jit(_where)/broadcast_in_dim | solution.py:302
  129.5 16.8 %broadcast_in_dim.17 = pred[2624,1152]{0,1:T(32,128)(4,1)S(1)} reshape(pred[41,64,18,64]{1,0,3,2:T(8,128)(4,1)} %broadcast_in_dim.16) | data formatting | bytes 6045696 | tf_op jit(solution)/shard_map/jit(_where)/broadcast_in_dim | solution.py:302
  146.3 9.8 %fusion.2 = f32[10,64,1152]{2,1,0:T(8,128)S(1)} fusion(bf16[10,64,2624]{2,1,0:T(8,128)(2,1)} %bitcast_dynamic-update-slice_fusion.10, pred[2624,1152]{0,1:T(32,128)(4,1)S(1)} %broadcast_in_dim.17, bf16[2624,1152]{0,1:T(8,128)(2,1)} %copy.6), kind=kOutput, calls=%fused_computation.6 | convolution fusion | flops 3872268288 | bytes 15376384 | tf_op jit(solution)/shard_map/dot_general | solution.py:310
  156.1 0.7 slice_dynamic-update-slice_fusion.22
  156.8 0.8 slice_dynamic-update-slice_fusion.21
  157.5 0.7 slice_dynamic-update-slice_fusion.20
  158.2 0.8 slice_dynamic-update-slice_fusion.19
  159.0 0.7 slice_dynamic-update-slice_fusion.18
  159.6 0.8 slice_dynamic-update-slice_fusion.17
  160.4 0.7 slice_dynamic-update-slice_fusion.16
  161.0 0.8 slice_dynamic-update-slice_fusion.15
  161.8 0.7 slice_dynamic-update-slice_fusion.14
  162.5 0.8 slice_dynamic-update-slice_fusion.13
  163.3 1.8 mul.61
  165.1 2.3 %mul.62 = f32[640,512]{1,0:T(8,128)S(1)} reshape(f32[10,64,8,64]{3,2,1,0:T(8,128)} %mul.61) | data formatting | bytes 2621440 | tf_op jit(solution)/shard_map/mul | solution.py:315
  167.3 2.4 %fusion.10.refs_0_ = bf16[640,512]{1,0:T(8,128)(2,1)} fusion(f32[640,512]{1,0:T(8,128)S(1)} %mul.62, f32[10,64,512]{2,1,0:T(8,128)} %slice_dynamic-update-slice_fusion.13), kind=kLoop, calls=%fused_computation.19 | loop fusion | flops 655360 | bytes 3276800 | tf_op jit(solution)/shard_map/convert_element_type | solution.py:317
  169.7 19.4 %layer_gather.3 = bf16[640,2048]{1,0:T(8,128)(2,1)} custom-call(bf16[640,512]{1,0:T(8,128)(2,1)} %fusion.10.refs_0_), custom_call_target="tpu_custom_call" | custom-call | tf_op jit(solution)/shard_map/layer_gather/pallas_call | solution.py:208
  189.2 0.9 constant_dynamic-update-slice_fusion
  190.1 2.4 %fusion.16 = (bf16[64,2048]{1,0:T(8,128)(2,1)S(1)}, bf16[64,2048]{1,0:T(8,128)(2,1)S(1)}, bf16[64,2048]{1,0:T(8,128)(2,1)S(1)}, bf16[64,2048]{1,0:T(8,128)(2,1)S...) fusion(bf16[640,2048]{1,0:T(8,128)(2,1)} %constant_dynamic-upda, ...), kind=kLoop, calls=%fused_computation.71 | loop fusion | bytes 5242880 | tf_op jit(solution)/shard_map/slice | solution.py:233
  193.5 1.1 copy-done.4
  194.5 5.0 %fusion = f32[10,64,1152]{2,1,0:T(8,128)S(1)} fusion(bf16[10,64,2624]{2,1,0:T(8,128)(2,1)S(1)} %bitcast_dynamic-update-slice_fusion, pred[2624,1152]{0,1:T(32,128)(4,1)S(1)} %copy-done.4, bf16[2624,1152]{0,1:T(8,128)(2,1)S(1)} %bitcast.73), kind=kOutput, calls=%fused_computation.4 | convolution fusion | flops 3872268288 | bytes 15376384 | tf_op jit(solution)/shard_map/dot_general | solution.py:310
  200.2 1.5 fusion.9
  (41 shorter events, 1.8 us)
Async XLA Ops:
  0.0 1.9 copy-start.5
  2.9 20.7 %copy-start.2 = (bf16[640,512]{1,0:T(8,128)(2,1)S(1)}, bf16[640,512]{1,0:T(8,128)(2,1)}, u32[]{:S(2)}) copy-start(bf16[640,512]{1,0:T(8,128)(2,1)} %mul.57.refs_0_) | copy-start | bytes 1966084
  24.6 3.8 %copy-start = (bf16[640,2048]{1,0:T(8,128)(2,1)S(1)}, bf16[640,2048]{1,0:T(8,128)(2,1)}, u32[]{:S(2)}) copy-start(bf16[640,2048]{1,0:T(8,128)(2,1)} %constant_dynamic-update-slice_fusion.1) | copy-start | bytes 7864324
  146.3 9.8 %copy-start.3 = (pred[2624,1152]{0,1:T(32,128)(4,1)}, pred[2624,1152]{0,1:T(32,128)(4,1)S(1)}, u32[]{:S(2)}) copy-start(pred[2624,1152]{0,1:T(32,128)(4,1)S(1)} %broadcast_in_dim.17) | copy-start | bytes 9068548
  169.7 19.5 %copy-start.1 = (bf16[640,512]{1,0:T(8,128)(2,1)S(1)}, bf16[640,512]{1,0:T(8,128)(2,1)}, u32[]{:S(2)}) copy-start(bf16[640,512]{1,0:T(8,128)(2,1)} %fusion.10.refs_0_) | copy-start | bytes 1966084
  189.2 4.3 %slice-start = ((s8[6193152]{0:T(1024)(128)(4,1)}), s8[4194304]{0:T(1024)(128)(4,1)S(1)}, s32[]{:S(2)}) async-start(s8[6193152]{0:T(1024)(128)(4,1)} %bitcast.72), calls=%async_computation | async-start | bytes 8388608
  190.1 3.3 %slice-start.1 = ((s8[6193152]{0:T(1024)(128)(4,1)}), s8[1998848]{0:T(1024)(128)(4,1)S(1)}, s32[]{:S(2)}) async-start(s8[6193152]{0:T(1024)(128)(4,1)} %bitcast.72), calls=%async_computation.1 | async-start | bytes 3997696
  192.5 2.0 %copy-start.4 = (pred[2624,1152]{0,1:T(32,128)(4,1)S(1)}, pred[2624,1152]{0,1:T(32,128)(4,1)}, u32[]{:S(2)}) copy-start(pred[2624,1152]{0,1:T(32,128)(4,1)} %copy-done.3) | copy-start | bytes 9068548

commit v12 on v10

--- a/solution.py
+++ b/solution.py
@@ -68,29 +68,29 @@
                      send_sem.at[k], recv_sem.at[k], target).start()
         waits.append(group(out_ref.at[pl.ds(row_start, last - first)], width,
                            send_sem.at[k], recv_sem.at[k], target))
-    pair_groups = []
     pair_base = (lax.rem(me + far, sizes[0]) - core) * slab_offsets
+    pair_rows = []
     for k, (shift, pair_start) in enumerate(pair_steps):
         target = _peer(sizes, far, shift)
         for jj in range(half_rows):
             j = core * half_rows + jj
             start = pair_base + block_rows * shift - j + pad_l
-            row_copy(j, start, pair_width, pair_ref.at[pair_start + j],
-                     pair_send.at[k], pair_recv.at[k], target).start()
-        held = pair_ref.at[pl.ds(pair_start + core * half_rows, half_rows)]
-        pair_groups.append((held, group(held, pair_width, pair_send.at[k], pair_recv.at[k], target)))
+            copy = row_copy(j, start, pair_width, pair_ref.at[pair_start + j],
+                            pair_send.at[k * half_rows + jj], pair_recv.at[k * half_rows + jj],
+                            target)
+            copy.start()
+            pair_rows.append(copy)
     for j in range(block_rows):
         start = me * slab_offsets - j + pad_l
         pltpu.make_async_copy(window(j, start, width), stage.at[j], local_sem.at[0]).start()
-    forwards = []
-    for k, (held, grp) in enumerate(pair_groups):
-        grp.wait_recv()
-        forward = pltpu.make_async_remote_copy(
-            src_ref=held, dst_ref=held, send_sem=fwd_send.at[k], recv_sem=fwd_recv.at[k],
-            device_id=_peer(sizes, core_shift, 0), device_id_type=mesh,
-        )
-        forward.start()
-        forwards.append(forward)
+    for jj in range(half_rows):
+        for k, (shift, pair_start) in enumerate(pair_steps):
+            pair_rows[k * half_rows + jj].wait_recv()
+            held = pair_ref.at[pair_start + core * half_rows + jj]
+            pltpu.make_async_remote_copy(
+                src_ref=held, dst_ref=held, send_sem=fwd_send.at[k], recv_sem=fwd_recv.at[k],
+                device_id=_peer(sizes, core_shift, 0), device_id_type=mesh,
+            ).start()
     pltpu.make_async_copy(band_ref.at[0, pl.ds(0, block_rows), :, pl.ds(0, width * bs)],
                           stage, local_sem.at[0]).wait()
     own_out = pltpu.make_async_copy(stage, out_ref.at[pl.ds(own_start, block_rows)],
@@ -98,9 +98,12 @@
     own_out.start()
     for grp in waits:
         grp.wait()
-    for k, (held, grp) in enumerate(pair_groups):
-        grp.wait_send()
-        forwards[k].wait()
+    for copy in pair_rows:
+        copy.wait_send()
+    for k, (shift, pair_start) in enumerate(pair_steps):
+        held = pair_ref.at[pl.ds(pair_start + core * half_rows, half_rows)]
+        group(held, pair_width, fwd_send.at[k], fwd_recv.at[k],
+              _peer(sizes, core_shift, 0)).wait()
     own_out.wait()
 
 
@@ -119,8 +122,8 @@
         scratch_shapes=[
             pltpu.SemaphoreType.DMA((n,)),
             pltpu.SemaphoreType.DMA((n,)),
-            pltpu.SemaphoreType.DMA((m,)),
-            pltpu.SemaphoreType.DMA((m,)),
+            pltpu.SemaphoreType.DMA((m * (block_rows // 2),)),
+            pltpu.SemaphoreType.DMA((m * (block_rows // 2),)),
             pltpu.SemaphoreType.DMA((m,)),
             pltpu.SemaphoreType.DMA((m,)),
             pltpu.SemaphoreType.DMA((2,)),

time: 154 us -> 153 us (level)
  Pallas kernels: 101 us -> 99.4 us
where the time goes in v12:
time: 153 us; the launch traced here: 152 us
  Pallas kernels  99.4 us (65%)
  local copies, waits for them, and re-layouts  31.9 us (21%)
  other arithmetic  11.1 us (7%)
  matrix products  9.56 us (6%)
    pallas_call x1, Pallas kernels, row_exchange(): pl.pallas_call(lambda *refs: _row_exchange_kernel(sizes, plan, *refs), ou...  59.3 us
    pallas_call x2, Pallas kernels, layer_gather(): pl.pallas_call(lambda *refs: _layer_gather_kernel(sizes, *refs), out_shap...  40.1 us
    unnamed x54, local copies, waits for them, and re-layouts  14 us
    dot_general x2, matrix products, product(): dense = jnp.dot(left, right, preferred_element_type=jnp.float32)  9.56 us
    another operation x1, other arithmetic, body(): band = jnp.stack([band, moved], axis=0)  6.73 us
    mul x2, local copies, waits for them, and re-layouts, product(): return out.reshape(block_rows, bs, slab_offsets, bs) * pattern_f  4.02 us
    slice x1, local copies, waits for them, and re-layouts, body(): moved = jnp.pad(band[:, :, bs:], ((0, 0), (0, 0), (0, bs)))  3.81 us

profile of v12, /device:TPU:1, one launch (start us, length us, event | category | flops | bytes accessed | tf_op | source)
XLA Modules:
  0.0 152.5 jit_solution(1120342559956790358)
XLA Ops:
  0.0 0.8 fusion.5
  0.8 0.1 copy.3
  0.9 0.3 mul.52
  1.1 0.8 mul.53
  1.9 1.0 mul.54.refs_0_
  2.9 20.7 %layer_gather.2 = bf16[640,2048]{1,0:T(8,128)(2,1)} custom-call(bf16[640,512]{1,0:T(8,128)(2,1)} %mul.54.refs_0_), custom_call_target="tpu_custom_call" | custom-call | tf_op jit(solution)/shard_map/layer_gather/pallas_call | solution.py:176
  23.6 0.9 constant_dynamic-update-slice_fusion.1
  24.6 3.8 %pad_slice_fusion = bf16[10,64,6080]{2,1,0:T(8,128)(2,1)S(1)} fusion(bf16[10,64,2048]{2,1,0:T(8,128)(2,1)} %bitcast.66), kind=kLoop, calls=%fused_computation.1 | loop fusion | bytes 10403840 | tf_op jit(solution)/shard_map/slice | solution.py:232
  28.4 1.8 %pad_bitcast_fusion = (bf16[1,10,64,6144]{3,2,1,0:T(8,128)(2,1)S(1)}, bf16[1,10,64,6144]{3,2,1,0:T(8,128)(2,1)S(1)}) fusion(bf16[10,64,2048]{2,1,0:T(8,128)(2,1)S(1)} %bitcast.67, bf16[10,64,6080]{2,1,0:T(8,128)(2,1)S(1)} %pad_slice_fusion), kind=kLoop, calls=%fused_computation.2 | loop fusion | bytes 26132480 | tf_op jit(solution)/shard_map/stack | solution.py:233
  30.3 6.7 %pad_maximum_fusion.refs_0_ = bf16[2,10,64,6144]{3,2,1,0:T(8,128)(2,1)} fusion(bf16[1,10,64,6144]{3,2,1,0:T(8,128)(2,1)S(1)} %get-tuple-element.32, bf16[1,10,64,6144]{3,2,1,0:T(8,128)(2,1)S(1)} %get-tuple-element.31), kind=kLoop, calls=%fused_computation | loop fusion | flops 7864320 | bytes 31457280 | tf_op jit(solution)/shard_map/stack | solution.py:233
  37.0 59.3 %row_exchange.1 = (bf16[41,64,1152]{2,1,0:T(8,128)(2,1)}, bf16[20,64,1664]{2,1,0:T(8,128)(2,1)}) custom-call(bf16[2,10,64,6144]{3,2,1,0:T(8,128)(2,1)} %pad_maximum_fusion.refs_0_), custom_call_target="tpu_custom_call" | custom-call | tf_op jit(solution)/shard_map/row_exchange/pallas_call | solution.py:116
  96.3 2.2 %slice_dynamic-update-slice_fusion.1 = bf16[41,64,1152]{2,1,0:T(8,128)(2,1)} fusion(bf16[41,64,1152]{2,1,0:T(8,128)(2,1)} %get-tuple-element.7), kind=kLoop, calls=%fused_computation.12 | loop fusion | bytes 1769472
  98.4 2.6 %dynamic-slice_dynamic-update-slice_fusion.1 = bf16[41,64,1152]{2,1,0:T(8,128)(2,1)} fusion(bf16[41,64,1152]{2,1,0:T(8,128)(2,1)} %slice_dynamic-update-slice_fusion.1, bf16[20,64,1664]{2,1,0:T(8,128)(2,1)} %get-tuple-element.8, s32[]{:T(128)S(6)} %select_n.8), kind=kLoop, calls=%fused_computation.5 | loop fusion | bytes 2949124
  101.1 2.6 %slice_dynamic-update-slice_fusion = bf16[41,64,1152]{2,1,0:T(8,128)(2,1)} fusion(bf16[41,64,1152]{2,1,0:T(8,128)(2,1)} %dynamic-slice_dynamic-update-slice_fusion.1, bf16[41,64,1152]{2,1,0:T(8,128)(2,1)} %get-tuple-element.7), kind=kLoop, calls=%fused_computation.6 | loop fusion | bytes 2949120
  103.7 2.6 %dynamic-slice_dynamic-update-slice_fusion = bf16[41,64,1152]{2,1,0:T(8,128)(2,1)} fusion(bf16[41,64,1152]{2,1,0:T(8,128)(2,1)} %slice_dynamic-update-slice_fusion, bf16[20,64,1664]{2,1,0:T(8,128)(2,1)} %get-tuple-element.8, s32[]{:T(128)S(6)} %add.53, s32[]{:T(128)S(6)} %select_n.8), kind=kLoop, calls=%fused_computation.4 | loop fusion | bytes 2949128
  106.3 2.1 %slice_dynamic-update-slice_fusion.2 = bf16[41,64,1152]{2,1,0:T(8,128)(2,1)} fusion(bf16[41,64,1152]{2,1,0:T(8,128)(2,1)} %dynamic-slice_dynamic-update-slice_fusion, bf16[41,64,1152]{2,1,0:T(8,128)(2,1)} %get-tuple-element.7), kind=kLoop, calls=%fused_computation.13 | loop fusion | bytes 1474560 | tf_op jit(solution)/shard_map/concatenate | solution.py:262
  108.3 0.2 fusion.4
  108.6 0.1 bitcast_dynamic-update-slice_fusion.18
  108.8 0.1 bitcast_dynamic-update-slice_fusion.16
  108.9 0.1 bitcast_dynamic-update-slice_fusion.14
  109.1 0.1 bitcast_dynamic-update-slice_fusion.12
  109.3 0.1 bitcast_dynamic-update-slice_fusion.10
  109.5 1.8 %copy-done.4 = bf16[41,64,1152]{2,1,0:T(8,128)(2,1)S(1)} copy-done((bf16[41,64,1152]{2,1,0:T(8,128)(2,1)S(1)}, bf16[41,64,1152]{2,1,0:T(8,128)(2,1)}, u32[]{:S(2)}) %copy-start.4) | copy-done | bytes 6045720
  111.2 4.8 %fusion.6 = f32[10,64,1152]{2,1,0:T(8,128)S(1)} fusion(bf16[10,64,2624]{2,1,0:T(8,128)(2,1)S(1)} %bitcast_dynamic-update-slice_fusion.10, bf16[2624,1152,1]{1,0,2:T(8,128)(2,1)S(1)} %bitcast.68), kind=kOutput, calls=%fused_computation.59 | convolution fusion | flops 3869245440 | bytes 12353536 | tf_op jit(solution)/shard_map/dot_general | solution.py:273
  116.0 0.1 slice_dynamic-update-slice_fusion.21
  116.2 0.1 slice_dynamic-update-slice_fusion.19
  116.3 0.1 slice_dynamic-update-slice_fusion.17
  116.4 0.1 slice_dynamic-update-slice_fusion.15
  116.5 0.1 slice_dynamic-update-slice_fusion.13
  116.6 0.1 copy.4
  116.7 1.8 %mul.57 = f32[10,64,8,64]{3,2,1,0:T(8,128)} broadcast(f32[10,8]{1,0:T(8,128)S(1)} %copy.4), dimensions={0,2} | broadcast | bytes 1311040 | tf_op jit(solution)/shard_map/mul | solution.py:278
  118.5 2.2 %mul.58 = f32[640,512]{1,0:T(8,128)S(1)} reshape(f32[10,64,8,64]{3,2,1,0:T(8,128)} %mul.57) | data formatting | bytes 2621440 | tf_op jit(solution)/shard_map/mul | solution.py:278
  120.7 1.1 fusion.2.refs_0_
  121.9 19.4 %layer_gather.3 = bf16[640,2048]{1,0:T(8,128)(2,1)} custom-call(bf16[640,512]{1,0:T(8,128)(2,1)} %fusion.2.refs_0_), custom_call_target="tpu_custom_call" | custom-call | tf_op jit(solution)/shard_map/layer_gather/pallas_call | solution.py:176
  141.3 0.9 constant_dynamic-update-slice_fusion
  142.3 2.4 %fusion.3 = (bf16[64,2048]{1,0:T(8,128)(2,1)S(1)}, bf16[64,2048]{1,0:T(8,128)(2,1)S(1)}, bf16[64,2048]{1,0:T(8,128)(2,1)S(1)}, bf16[64,2048]{1,0:T(8,128)(2,1)S(...) fusion(bf16[640,2048]{1,0:T(8,128)(2,1)} %constant_dynamic-upda, ...), kind=kLoop, calls=%fused_computation.56 | loop fusion | bytes 5242880 | tf_op jit(solution)/shard_map/slice | solution.py:201
  144.7 0.1 bitcast_dynamic-update-slice_fusion.8
  144.9 0.1 bitcast_dynamic-update-slice_fusion.6
  145.1 0.1 bitcast_dynamic-update-slice_fusion.4
  145.3 0.1 bitcast_dynamic-update-slice_fusion.2
  145.5 0.1 bitcast_dynamic-update-slice_fusion
  145.6 4.8 %fusion.7 = f32[10,64,1152]{2,1,0:T(8,128)S(1)} fusion(bf16[10,64,2624]{2,1,0:T(8,128)(2,1)S(1)} %bitcast_dynamic-update-slice_fusion, bf16[2624,1152,1]{1,0,2:T(8,128)(2,1)S(1)} %bitcast.71), kind=kOutput, calls=%fused_computation.60 | convolution fusion | flops 3869245440 | bytes 12353536 | tf_op jit(solution)/shard_map/dot_general | solution.py:273
  150.4 0.1 slice_dynamic-update-slice_fusion.11
  150.6 0.1 slice_dynamic-update-slice_fusion.9
  150.7 0.1 slice_dynamic-update-slice_fusion.7
  150.8 0.1 slice_dynamic-update-slice_fusion.5
  150.9 0.1 slice_dynamic-update-slice_fusion.3
  151.0 1.5 fusion.1
  (34 shorter events, 0.4 us)
Async XLA Ops:
  0.0 1.9 %copy-start.3 = (bf16[640,512]{1,0:T(8,128)(2,1)S(1)}, bf16[640,512]{1,0:T(8,128)(2,1)}, u32[]{:S(2)}) copy-start(bf16[640,512]{1,0:T(8,128)(2,1)} %param.2) | copy-start | bytes 1966084
  2.9 20.7 %copy-start.2 = (bf16[640,512]{1,0:T(8,128)(2,1)S(1)}, bf16[640,512]{1,0:T(8,128)(2,1)}, u32[]{:S(2)}) copy-start(bf16[640,512]{1,0:T(8,128)(2,1)} %mul.54.refs_0_) | copy-start | bytes 1966084
  24.6 3.8 %copy-start = (bf16[640,2048]{1,0:T(8,128)(2,1)S(1)}, bf16[640,2048]{1,0:T(8,128)(2,1)}, u32[]{:S(2)}) copy-start(bf16[640,2048]{1,0:T(8,128)(2,1)} %constant_dynamic-update-slice_fusion.1) | copy-start | bytes 7864324
  108.5 2.7 %copy-start.4 = (bf16[41,64,1152]{2,1,0:T(8,128)(2,1)S(1)}, bf16[41,64,1152]{2,1,0:T(8,128)(2,1)}, u32[]{:S(2)}) copy-start(bf16[41,64,1152]{2,1,0:T(8,128)(2,1)} %slice_dynamic-update-slice_fusion.2) | copy-start | bytes 18137092
  121.9 19.5 %copy-start.1 = (bf16[640,512]{1,0:T(8,128)(2,1)S(1)}, bf16[640,512]{1,0:T(8,128)(2,1)}, u32[]{:S(2)}) copy-start(bf16[640,512]{1,0:T(8,128)(2,1)} %fusion.2.refs_0_) | copy-start | bytes 1966084
  141.3 4.3 %slice-start = ((s8[6045696]{0:T(1024)(128)(4,1)}), s8[4194304]{0:T(1024)(128)(4,1)S(1)}, s32[]{:S(2)}) async-start(s8[6045696]{0:T(1024)(128)(4,1)} %bitcast.69), calls=%async_computation | async-start | bytes 8388608
  142.3 3.3 %slice-start.1 = ((s8[6045696]{0:T(1024)(128)(4,1)}), s8[1851392]{0:T(1024)(128)(4,1)S(1)}, s32[]{:S(2)}) async-start(s8[6045696]{0:T(1024)(128)(4,1)} %bitcast.69), calls=%async_computation.1 | async-start | bytes 3702784

commit v13 on v12

--- a/solution.py
+++ b/solution.py
@@ -223,8 +223,12 @@
     far = layers // 2
     width = width + width % 2
     pair_width = width + slab_offsets
-    span = pad_l + 2 * block_rows + pair_width + 2
-    total_blocks = slab_offsets * (layers - 1) + span
+    reach = (half + block_rows - 1) // block_rows
+    total_blocks = max(
+        slab_offsets * (layers - 1) + block_rows * reach + pad_l + width,
+        slab_offsets * (layers - 2) + block_rows + pad_l + pair_width,
+        pad_l + offsets,
+    )
     total_blocks += total_blocks % 2
     pad_r = total_blocks - offsets - pad_l
     band = jnp.pad(own_band.reshape(block_rows, bs, offsets * bs),
@@ -259,10 +263,8 @@
             tuple(steps), pair_steps)
     right, pair_buf = row_exchange(sizes, plan, total_rows, 2 * block_rows, band)
     pair_part = lax.dynamic_slice_in_dim(pair_buf, core * slab_offsets * bs, width * bs, axis=2)
-    right = jnp.concatenate([
-        right[:lower_start], pair_part[:block_rows], right[below:below + block_rows],
-        pair_part[block_rows:], right[upper_start + block_rows:],
-    ], axis=0)
+    right = lax.dynamic_update_slice_in_dim(right, pair_part[:block_rows], lower_start, axis=0)
+    right = lax.dynamic_update_slice_in_dim(right, pair_part[block_rows:], upper_start, axis=0)
     right = right.reshape(total_rows * bs, width * bs)
 
     pattern_f = pattern.astype(jnp.float32)[:, None, :, None]

time: 153 us -> 144 us (0.941)
  local copies, waits for them, and re-layouts: 31.9 us -> 24.2 us
    unnamed x54 -> x50, local copies, waits for them, and re-layouts: 14 us -> 4.06 us
    dynamic_update_slice x0 -> x2, local copies, waits for them, and re-layouts: none -> 5.24 us  [the longest x1 2.63 us: body(): lax.dynamic_update_slice_in_dim(right, pair_part[:block_rows], lower_star...]
    concatenate x1 -> x0, local copies, waits for them, and re-layouts: 2.08 us -> none  [body(): jnp.concatenate([right[:lower_start], pair_part[:block_rows], right[below...]
where the time goes in v13:
time: 144 us; the launch traced here: 143 us
  Pallas kernels  99.4 us (69%)
  local copies, waits for them, and re-layouts  24.2 us (17%)
  other arithmetic  9.72 us (7%)
  matrix products  9.56 us (7%)
    pallas_call x1, Pallas kernels, row_exchange(): pl.pallas_call(lambda *refs: _row_exchange_kernel(sizes, plan, *refs), ou...  59.3 us
    pallas_call x2, Pallas kernels, layer_gather(): pl.pallas_call(lambda *refs: _layer_gather_kernel(sizes, *refs), out_shap...  40.1 us
    dot_general x2, matrix products, product(): dense = jnp.dot(left, right, preferred_element_type=jnp.float32)  9.56 us
    another operation x1, other arithmetic, body(): band = jnp.stack([band, moved], axis=0)  5.35 us
    unnamed x50, local copies, waits for them, and re-layouts  4.06 us
    mul x2, local copies, waits for them, and re-layouts, product(): return out.reshape(block_rows, bs, slab_offsets, bs) * pattern_f  3.98 us
    slice x1, local copies, waits for them, and re-layouts, body(): moved = jnp.pad(band[:, :, bs:], ((0, 0), (0, 0), (0, bs)))  3.54 us

profile of v13, /device:TPU:1, one launch (start us, length us, event | category | flops | bytes accessed | tf_op | source)
XLA Modules:
  0.0 143.4 jit_solution(12423483345390190656)
XLA Ops:
  0.0 0.8 fusion.5
  0.8 0.1 copy.3
  0.9 0.3 mul.52
  1.1 0.8 mul.53
  1.9 1.0 mul.54.refs_0_
  2.9 20.7 %layer_gather.2 = bf16[640,2048]{1,0:T(8,128)(2,1)} custom-call(bf16[640,512]{1,0:T(8,128)(2,1)} %mul.54.refs_0_), custom_call_target="tpu_custom_call" | custom-call | tf_op jit(solution)/shard_map/layer_gather/pallas_call | solution.py:176
  23.6 0.9 constant_dynamic-update-slice_fusion.1
  24.6 3.5 %pad_slice_fusion = bf16[10,64,5440]{2,1,0:T(8,128)(2,1)S(1)} fusion(bf16[10,64,2048]{2,1,0:T(8,128)(2,1)} %bitcast.66), kind=kLoop, calls=%fused_computation.1 | loop fusion | bytes 9584640 | tf_op jit(solution)/shard_map/slice | solution.py:236
  28.1 1.3 pad_bitcast_fusion
  29.4 5.3 %pad_maximum_fusion.refs_0_ = bf16[2,10,64,5504]{3,2,1,0:T(8,128)(2,1)} fusion(bf16[1,10,64,5504]{3,2,1,0:T(8,128)(2,1)S(1)} %get-tuple-element.32, bf16[1,10,64,5504]{3,2,1,0:T(8,128)(2,1)S(1)} %get-tuple-element.31), kind=kLoop, calls=%fused_computation | loop fusion | flops 7045120 | bytes 28180480 | tf_op jit(solution)/shard_map/stack | solution.py:237
  34.8 59.3 %row_exchange.1 = (bf16[41,64,1152]{2,1,0:T(8,128)(2,1)}, bf16[20,64,1664]{2,1,0:T(8,128)(2,1)}) custom-call(bf16[2,10,64,5504]{3,2,1,0:T(8,128)(2,1)} %pad_maximum_fusion.refs_0_), custom_call_target="tpu_custom_call" | custom-call | tf_op jit(solution)/shard_map/row_exchange/pallas_call | solution.py:116
  94.1 2.6 %dynamic-slice_dynamic-update-slice_fusion.1 = bf16[41,64,1152]{2,1,0:T(8,128)(2,1)} fusion(bf16[41,64,1152]{2,1,0:T(8,128)(2,1)} %get-tuple-element.7, bf16[20,64,1664]{2,1,0:T(8,128)(2,1)} %get-tuple-element.8, s32[]{:T(128)S(6)} %select_n.8), kind=kLoop, calls=%fused_computation.5 | loop fusion | bytes 2949124 | tf_op jit(solution)/shard_map/dynamic_update_slice | solution.py:266
  96.7 2.6 %dynamic-slice_dynamic-update-slice_fusion = bf16[41,64,1152]{2,1,0:T(8,128)(2,1)} fusion(bf16[41,64,1152]{2,1,0:T(8,128)(2,1)} %dynamic-slice_dynamic-update-slice_fusion.1, bf16[20,64,1664]{2,1,0:T(8,128)(2,1)} %get-tuple-element.8, s32[]{:T(128)S(6)} %add.53, s32[]{:T(128)S(6)} %select_n.8), kind=kLoop, calls=%fused_computation.4 | loop fusion | bytes 2949128 | tf_op jit(solution)/shard_map/dynamic_update_slice | solution.py:267
  99.3 0.2 fusion.4
  99.5 0.1 bitcast_dynamic-update-slice_fusion.18
  99.7 0.1 bitcast_dynamic-update-slice_fusion.16
  99.9 0.1 bitcast_dynamic-update-slice_fusion.14
  100.1 0.1 bitcast_dynamic-update-slice_fusion.12
  100.3 0.1 bitcast_dynamic-update-slice_fusion.10
  100.4 1.8 %copy-done.4 = bf16[41,64,1152]{2,1,0:T(8,128)(2,1)S(1)} copy-done((bf16[41,64,1152]{2,1,0:T(8,128)(2,1)S(1)}, bf16[41,64,1152]{2,1,0:T(8,128)(2,1)}, u32[]{:S(2)}) %copy-start.4) | copy-done | bytes 6045720
  102.2 4.8 %fusion.6 = f32[10,64,1152]{2,1,0:T(8,128)S(1)} fusion(bf16[10,64,2624]{2,1,0:T(8,128)(2,1)S(1)} %bitcast_dynamic-update-slice_fusion.10, bf16[2624,1152,1]{1,0,2:T(8,128)(2,1)S(1)} %bitcast.68), kind=kOutput, calls=%fused_computation.56 | convolution fusion | flops 3869245440 | bytes 12353536 | tf_op jit(solution)/shard_map/dot_general | solution.py:275
  107.0 0.1 slice_dynamic-update-slice_fusion.18
  107.1 0.1 slice_dynamic-update-slice_fusion.16
  107.2 0.1 slice_dynamic-update-slice_fusion.14
  107.4 0.1 slice_dynamic-update-slice_fusion.12
  107.5 0.1 slice_dynamic-update-slice_fusion.10
  107.6 0.1 copy.4
  107.7 1.8 %mul.57 = f32[10,64,8,64]{3,2,1,0:T(8,128)} broadcast(f32[10,8]{1,0:T(8,128)S(1)} %copy.4), dimensions={0,2} | broadcast | bytes 1311040 | tf_op jit(solution)/shard_map/mul | solution.py:280
  109.4 2.2 %mul.58 = f32[640,512]{1,0:T(8,128)S(1)} reshape(f32[10,64,8,64]{3,2,1,0:T(8,128)} %mul.57) | data formatting | bytes 2621440 | tf_op jit(solution)/shard_map/mul | solution.py:280
  111.6 1.1 fusion.2.refs_0_
  112.8 19.4 %layer_gather.3 = bf16[640,2048]{1,0:T(8,128)(2,1)} custom-call(bf16[640,512]{1,0:T(8,128)(2,1)} %fusion.2.refs_0_), custom_call_target="tpu_custom_call" | custom-call | tf_op jit(solution)/shard_map/layer_gather/pallas_call | solution.py:176
  132.3 0.0 slice-start
  132.3 0.9 constant_dynamic-update-slice_fusion
  133.2 2.4 %fusion.3 = (bf16[64,2048]{1,0:T(8,128)(2,1)S(1)}, bf16[64,2048]{1,0:T(8,128)(2,1)S(1)}, bf16[64,2048]{1,0:T(8,128)(2,1)S(1)}, bf16[64,2048]{1,0:T(8,128)(2,1)S(...) fusion(bf16[640,2048]{1,0:T(8,128)(2,1)} %constant_dynamic-upda, ...), kind=kLoop, calls=%fused_computation.53 | loop fusion | bytes 5242880 | tf_op jit(solution)/shard_map/slice | solution.py:201
  135.6 0.1 bitcast_dynamic-update-slice_fusion.8
  135.8 0.1 bitcast_dynamic-update-slice_fusion.6
  136.0 0.1 bitcast_dynamic-update-slice_fusion.4
  136.2 0.1 bitcast_dynamic-update-slice_fusion.2
  136.4 0.1 bitcast_dynamic-update-slice_fusion
  136.5 0.0 slice-done
  136.5 0.0 slice-done.1
  136.6 4.8 %fusion.7 = f32[10,64,1152]{2,1,0:T(8,128)S(1)} fusion(bf16[10,64,2624]{2,1,0:T(8,128)(2,1)S(1)} %bitcast_dynamic-update-slice_fusion, bf16[2624,1152,1]{1,0,2:T(8,128)(2,1)S(1)} %bitcast.71), kind=kOutput, calls=%fused_computation.57 | convolution fusion | flops 3869245440 | bytes 12353536 | tf_op jit(solution)/shard_map/dot_general | solution.py:275
  141.4 0.1 slice_dynamic-update-slice_fusion.8
  141.5 0.1 slice_dynamic-update-slice_fusion.6
  141.6 0.1 slice_dynamic-update-slice_fusion.4
  141.7 0.1 slice_dynamic-update-slice_fusion.2
  141.8 0.1 slice_dynamic-update-slice_fusion
  141.9 1.5 %fusion.1 = f32[640,512]{1,0:T(8,128)} fusion(f32[640,512]{1,0:T(8,128)S(1)} %mul.58, f32[10,64,512]{2,1,0:T(8,128)S(1)} %slice_dynamic-update-slice_fusion, bf16[640,512]{1,0:T(8,128)(2,1)S(1)} %copy-done.1), kind=kLoop, calls=%fused_computation.8 | loop fusion | flops 1638400 | bytes 4587520 | tf_op jit(solution)/shard_map/sub | solution.py:285
  (31 shorter events, 0.4 us)
Async XLA Ops:
  0.0 1.9 %copy-start.3 = (bf16[640,512]{1,0:T(8,128)(2,1)S(1)}, bf16[640,512]{1,0:T(8,128)(2,1)}, u32[]{:S(2)}) copy-start(bf16[640,512]{1,0:T(8,128)(2,1)} %param.2) | copy-start | bytes 1966084
  2.9 20.7 %copy-start.2 = (bf16[640,512]{1,0:T(8,128)(2,1)S(1)}, bf16[640,512]{1,0:T(8,128)(2,1)}, u32[]{:S(2)}) copy-start(bf16[640,512]{1,0:T(8,128)(2,1)} %mul.54.refs_0_) | copy-start | bytes 1966084
  24.6 3.6 %copy-start = (bf16[640,2048]{1,0:T(8,128)(2,1)S(1)}, bf16[640,2048]{1,0:T(8,128)(2,1)}, u32[]{:S(2)}) copy-start(bf16[640,2048]{1,0:T(8,128)(2,1)} %constant_dynamic-update-slice_fusion.1) | copy-start | bytes 7864324
  99.5 2.7 %copy-start.4 = (bf16[41,64,1152]{2,1,0:T(8,128)(2,1)S(1)}, bf16[41,64,1152]{2,1,0:T(8,128)(2,1)}, u32[]{:S(2)}) copy-start(bf16[41,64,1152]{2,1,0:T(8,128)(2,1)} %dynamic-slice_dynamic-update-slice_fusion) | copy-start | bytes 18137092
  112.8 19.5 %copy-start.1 = (bf16[640,512]{1,0:T(8,128)(2,1)S(1)}, bf16[640,512]{1,0:T(8,128)(2,1)}, u32[]{:S(2)}) copy-start(bf16[640,512]{1,0:T(8,128)(2,1)} %fusion.2.refs_0_) | copy-start | bytes 1966084
  132.3 4.3 %slice-start = ((s8[6045696]{0:T(1024)(128)(4,1)}), s8[4194304]{0:T(1024)(128)(4,1)S(1)}, s32[]{:S(2)}) async-start(s8[6045696]{0:T(1024)(128)(4,1)} %bitcast.69), calls=%async_computation | async-start | bytes 8388608
  133.2 3.3 %slice-start.1 = ((s8[6045696]{0:T(1024)(128)(4,1)}), s8[1851392]{0:T(1024)(128)(4,1)S(1)}, s32[]{:S(2)}) async-start(s8[6045696]{0:T(1024)(128)(4,1)} %bitcast.69), calls=%async_computation.1 | async-start | bytes 3702784

commit v14 on v13

--- a/solution.py
+++ b/solution.py
@@ -147,27 +147,42 @@
         return out_ref.at[:, pl.ds(pl.multiple_of(layer * width, width), width)]
 
     mine = cols(me)
-    to_far = pltpu.make_async_remote_copy(
-        src_ref=src_ref, dst_ref=mine, send_sem=send_sem.at[0], recv_sem=recv_sem.at[0],
-        device_id=_peer(sizes, far, 0), device_id_type=pl.DeviceIdType.MESH,
+    rows = src_ref.shape[0]
+    chunks = 4 if rows % 32 == 0 else 1
+    part = rows // chunks
+    mesh = pl.DeviceIdType.MESH
+    to_far = []
+    for c in range(chunks):
+        piece = pl.ds(c * part, part)
+        copy = pltpu.make_async_remote_copy(
+            src_ref=src_ref.at[piece], dst_ref=mine.at[piece], send_sem=send_sem.at[c],
+            recv_sem=recv_sem.at[c], device_id=_peer(sizes, far, 0), device_id_type=mesh,
+        )
+        copy.start()
+        to_far.append(copy)
+    to_core = pltpu.make_async_remote_copy(
+        src_ref=src_ref, dst_ref=mine, send_sem=send_sem.at[chunks],
+        recv_sem=recv_sem.at[chunks], device_id=_peer(sizes, core_shift, 0),
+        device_id_type=mesh,
     )
-    to_core = pltpu.make_async_remote_copy(
-        src_ref=src_ref, dst_ref=mine, send_sem=send_sem.at[1], recv_sem=recv_sem.at[1],
-        device_id=_peer(sizes, core_shift, 0), device_id_type=pl.DeviceIdType.MESH,
-    )
-    to_far.start()
     to_core.start()
-    far_layer = lax.rem(me + far, count)
-    to_far.wait_recv()
-    forward = pltpu.make_async_remote_copy(
-        src_ref=cols(far_layer), dst_ref=cols(far_layer), send_sem=send_sem.at[2],
-        recv_sem=recv_sem.at[2], device_id=_peer(sizes, core_shift, 0),
-        device_id_type=pl.DeviceIdType.MESH,
-    )
-    forward.start()
-    to_far.wait_send()
+    far_cols = cols(lax.rem(me + far, count))
+    for c in range(chunks):
+        piece = pl.ds(c * part, part)
+        to_far[c].wait_recv()
+        pltpu.make_async_remote_copy(
+            src_ref=far_cols.at[piece], dst_ref=far_cols.at[piece],
+            send_sem=send_sem.at[chunks + 1], recv_sem=recv_sem.at[chunks + 1],
+            device_id=_peer(sizes, core_shift, 0), device_id_type=mesh,
+        ).start()
+    for c in range(chunks):
+        to_far[c].wait_send()
     to_core.wait()
-    forward.wait()
+    pltpu.make_async_remote_copy(
+        src_ref=far_cols, dst_ref=far_cols, send_sem=send_sem.at[chunks + 1],
+        recv_sem=recv_sem.at[chunks + 1], device_id=_peer(sizes, core_shift, 0),
+        device_id_type=mesh,
+    ).wait()
 
 
 def layer_gather(sizes, slab, collective_id):
@@ -179,8 +194,8 @@
         in_specs=[any_spec],
         out_specs=any_spec,
         scratch_shapes=[
-            pltpu.SemaphoreType.DMA((3,)),
-            pltpu.SemaphoreType.DMA((3,)),
+            pltpu.SemaphoreType.DMA((6,)),
+            pltpu.SemaphoreType.DMA((6,)),
         ],
         compiler_params=pltpu.CompilerParams(collective_id=collective_id, has_side_effects=True),
         name="layer_gather",

time: 144 us -> 142 us (0.986)
  no operation moved by 1% of the time
where the time goes in v14:
time: 142 us
  Pallas kernels  98.1 us (69%)
  local copies, waits for them, and re-layouts  24.2 us (17%)
  other arithmetic  9.72 us (7%)
  matrix products  9.56 us (7%)
    pallas_call x1, Pallas kernels, row_exchange(): pl.pallas_call(lambda *refs: _row_exchange_kernel(sizes, plan, *refs), ou...  59.3 us
    pallas_call x2, Pallas kernels, layer_gather(): pl.pallas_call(lambda *refs: _layer_gather_kernel(sizes, *refs), out_shap...  38.8 us
    dot_general x2, matrix products, product(): dense = jnp.dot(left, right, preferred_element_type=jnp.float32)  9.56 us
    another operation x1, other arithmetic, body(): band = jnp.stack([band, moved], axis=0)  5.35 us
    unnamed x50, local copies, waits for them, and re-layouts  4.06 us
    mul x2, local copies, waits for them, and re-layouts, product(): return out.reshape(block_rows, bs, slab_offsets, bs) * pattern_f  3.98 us
    slice x1, local copies, waits for them, and re-layouts, body(): moved = jnp.pad(band[:, :, bs:], ((0, 0), (0, 0), (0, bs)))  3.54 us

profile of v14, /device:TPU:1, one launch (start us, length us, event | category | flops | bytes accessed | tf_op | source)
XLA Modules:
  0.0 142.1 jit_solution(15747922708700643013)
XLA Ops:
  0.0 0.8 fusion.5
  0.8 0.1 copy.3
  0.9 0.3 mul.52
  1.1 0.8 mul.53
  1.9 1.0 mul.54.refs_0_
  2.9 20.0 %layer_gather.2 = bf16[640,2048]{1,0:T(8,128)(2,1)} custom-call(bf16[640,512]{1,0:T(8,128)(2,1)} %mul.54.refs_0_), custom_call_target="tpu_custom_call" | custom-call | tf_op jit(solution)/shard_map/layer_gather/pallas_call | solution.py:191
  23.0 0.0 copy-done.2
  23.0 0.9 constant_dynamic-update-slice_fusion.1
  23.9 3.5 %pad_slice_fusion = bf16[10,64,5440]{2,1,0:T(8,128)(2,1)S(1)} fusion(bf16[10,64,2048]{2,1,0:T(8,128)(2,1)} %bitcast.66), kind=kLoop, calls=%fused_computation.1 | loop fusion | bytes 9584640 | tf_op jit(solution)/shard_map/slice | solution.py:251
  27.5 0.0 copy-done
  27.5 1.3 pad_bitcast_fusion
  28.8 5.3 %pad_maximum_fusion.refs_0_ = bf16[2,10,64,5504]{3,2,1,0:T(8,128)(2,1)} fusion(bf16[1,10,64,5504]{3,2,1,0:T(8,128)(2,1)S(1)} %get-tuple-element.32, bf16[1,10,64,5504]{3,2,1,0:T(8,128)(2,1)S(1)} %get-tuple-element.31), kind=kLoop, calls=%fused_computation | loop fusion | flops 7045120 | bytes 28180480 | tf_op jit(solution)/shard_map/stack | solution.py:252
  34.1 59.3 %row_exchange.1 = (bf16[41,64,1152]{2,1,0:T(8,128)(2,1)}, bf16[20,64,1664]{2,1,0:T(8,128)(2,1)}) custom-call(bf16[2,10,64,5504]{3,2,1,0:T(8,128)(2,1)} %pad_maximum_fusion.refs_0_), custom_call_target="tpu_custom_call" | custom-call | tf_op jit(solution)/shard_map/row_exchange/pallas_call | solution.py:116
  93.4 2.6 %dynamic-slice_dynamic-update-slice_fusion.1 = bf16[41,64,1152]{2,1,0:T(8,128)(2,1)} fusion(bf16[41,64,1152]{2,1,0:T(8,128)(2,1)} %get-tuple-element.7, bf16[20,64,1664]{2,1,0:T(8,128)(2,1)} %get-tuple-element.8, s32[]{:T(128)S(6)} %select_n.8), kind=kLoop, calls=%fused_computation.5 | loop fusion | bytes 2949124 | tf_op jit(solution)/shard_map/dynamic_update_slice | solution.py:281
  96.0 2.6 %dynamic-slice_dynamic-update-slice_fusion = bf16[41,64,1152]{2,1,0:T(8,128)(2,1)} fusion(bf16[41,64,1152]{2,1,0:T(8,128)(2,1)} %dynamic-slice_dynamic-update-slice_fusion.1, bf16[20,64,1664]{2,1,0:T(8,128)(2,1)} %get-tuple-element.8, s32[]{:T(128)S(6)} %add.53, s32[]{:T(128)S(6)} %select_n.8), kind=kLoop, calls=%fused_computation.4 | loop fusion | bytes 2949128 | tf_op jit(solution)/shard_map/dynamic_update_slice | solution.py:282
  98.7 0.2 fusion.4
  98.9 0.1 bitcast_dynamic-update-slice_fusion.18
  99.1 0.1 bitcast_dynamic-update-slice_fusion.16
  99.2 0.1 bitcast_dynamic-update-slice_fusion.14
  99.4 0.1 bitcast_dynamic-update-slice_fusion.12
  99.6 0.1 bitcast_dynamic-update-slice_fusion.10
  99.8 1.8 %copy-done.4 = bf16[41,64,1152]{2,1,0:T(8,128)(2,1)S(1)} copy-done((bf16[41,64,1152]{2,1,0:T(8,128)(2,1)S(1)}, bf16[41,64,1152]{2,1,0:T(8,128)(2,1)}, u32[]{:S(2)}) %copy-start.4) | copy-done | bytes 6045720
  101.6 4.8 %fusion.6 = f32[10,64,1152]{2,1,0:T(8,128)S(1)} fusion(bf16[10,64,2624]{2,1,0:T(8,128)(2,1)S(1)} %bitcast_dynamic-update-slice_fusion.10, bf16[2624,1152,1]{1,0,2:T(8,128)(2,1)S(1)} %bitcast.68), kind=kOutput, calls=%fused_computation.56 | convolution fusion | flops 3869245440 | bytes 12353536 | tf_op jit(solution)/shard_map/dot_general | solution.py:290
  106.4 0.1 slice_dynamic-update-slice_fusion.18
  106.5 0.1 slice_dynamic-update-slice_fusion.16
  106.6 0.1 slice_dynamic-update-slice_fusion.14
  106.7 0.1 slice_dynamic-update-slice_fusion.12
  106.8 0.1 slice_dynamic-update-slice_fusion.10
  106.9 0.1 copy.4
  107.0 1.8 %mul.57 = f32[10,64,8,64]{3,2,1,0:T(8,128)} broadcast(f32[10,8]{1,0:T(8,128)S(1)} %copy.4), dimensions={0,2} | broadcast | bytes 1311040 | tf_op jit(solution)/shard_map/mul | solution.py:295
  108.8 2.2 %mul.58 = f32[640,512]{1,0:T(8,128)S(1)} reshape(f32[10,64,8,64]{3,2,1,0:T(8,128)} %mul.57) | data formatting | bytes 2621440 | tf_op jit(solution)/shard_map/mul | solution.py:295
  111.0 1.1 fusion.2.refs_0_
  112.1 18.8 %layer_gather.3 = bf16[640,2048]{1,0:T(8,128)(2,1)} custom-call(bf16[640,512]{1,0:T(8,128)(2,1)} %fusion.2.refs_0_), custom_call_target="tpu_custom_call" | custom-call | tf_op jit(solution)/shard_map/layer_gather/pallas_call | solution.py:191
  131.0 0.0 slice-start
  131.0 0.9 constant_dynamic-update-slice_fusion
  131.9 2.4 %fusion.3 = (bf16[64,2048]{1,0:T(8,128)(2,1)S(1)}, bf16[64,2048]{1,0:T(8,128)(2,1)S(1)}, bf16[64,2048]{1,0:T(8,128)(2,1)S(1)}, bf16[64,2048]{1,0:T(8,128)(2,1)S(...) fusion(bf16[640,2048]{1,0:T(8,128)(2,1)} %constant_dynamic-upda, ...), kind=kLoop, calls=%fused_computation.53 | loop fusion | bytes 5242880 | tf_op jit(solution)/shard_map/slice | solution.py:216
  134.3 0.1 bitcast_dynamic-update-slice_fusion.8
  134.5 0.1 bitcast_dynamic-update-slice_fusion.6
  134.7 0.1 bitcast_dynamic-update-slice_fusion.4
  134.9 0.1 bitcast_dynamic-update-slice_fusion.2
  135.1 0.1 bitcast_dynamic-update-slice_fusion
  135.3 4.8 %fusion.7 = f32[10,64,1152]{2,1,0:T(8,128)S(1)} fusion(bf16[10,64,2624]{2,1,0:T(8,128)(2,1)S(1)} %bitcast_dynamic-update-slice_fusion, bf16[2624,1152,1]{1,0,2:T(8,128)(2,1)S(1)} %bitcast.71), kind=kOutput, calls=%fused_computation.57 | convolution fusion | flops 3869245440 | bytes 12353536 | tf_op jit(solution)/shard_map/dot_general | solution.py:290
  140.1 0.1 slice_dynamic-update-slice_fusion.8
  140.2 0.1 slice_dynamic-update-slice_fusion.6
  140.3 0.1 slice_dynamic-update-slice_fusion.4
  140.4 0.1 slice_dynamic-update-slice_fusion.2
  140.5 0.1 slice_dynamic-update-slice_fusion
  140.6 1.5 %fusion.1 = f32[640,512]{1,0:T(8,128)} fusion(f32[640,512]{1,0:T(8,128)S(1)} %mul.58, f32[10,64,512]{2,1,0:T(8,128)S(1)} %slice_dynamic-update-slice_fusion, bf16[640,512]{1,0:T(8,128)(2,1)S(1)} %copy-done.1), kind=kLoop, calls=%fused_computation.8 | loop fusion | flops 1638400 | bytes 4587520 | tf_op jit(solution)/shard_map/sub | solution.py:300
  (31 shorter events, 0.4 us)
Async XLA Ops:
  0.0 1.9 %copy-start.3 = (bf16[640,512]{1,0:T(8,128)(2,1)S(1)}, bf16[640,512]{1,0:T(8,128)(2,1)}, u32[]{:S(2)}) copy-start(bf16[640,512]{1,0:T(8,128)(2,1)} %param.2) | copy-start | bytes 1966084
  2.9 20.1 %copy-start.2 = (bf16[640,512]{1,0:T(8,128)(2,1)S(1)}, bf16[640,512]{1,0:T(8,128)(2,1)}, u32[]{:S(2)}) copy-start(bf16[640,512]{1,0:T(8,128)(2,1)} %mul.54.refs_0_) | copy-start | bytes 1966084
  23.9 3.6 %copy-start = (bf16[640,2048]{1,0:T(8,128)(2,1)S(1)}, bf16[640,2048]{1,0:T(8,128)(2,1)}, u32[]{:S(2)}) copy-start(bf16[640,2048]{1,0:T(8,128)(2,1)} %constant_dynamic-update-slice_fusion.1) | copy-start | bytes 7864324
  98.8 2.7 %copy-start.4 = (bf16[41,64,1152]{2,1,0:T(8,128)(2,1)S(1)}, bf16[41,64,1152]{2,1,0:T(8,128)(2,1)}, u32[]{:S(2)}) copy-start(bf16[41,64,1152]{2,1,0:T(8,128)(2,1)} %dynamic-slice_dynamic-update-slice_fusion) | copy-start | bytes 18137092
  112.1 18.8 %copy-start.1 = (bf16[640,512]{1,0:T(8,128)(2,1)S(1)}, bf16[640,512]{1,0:T(8,128)(2,1)}, u32[]{:S(2)}) copy-start(bf16[640,512]{1,0:T(8,128)(2,1)} %fusion.2.refs_0_) | copy-start | bytes 1966084
  131.0 4.3 %slice-start = ((s8[6045696]{0:T(1024)(128)(4,1)}), s8[4194304]{0:T(1024)(128)(4,1)S(1)}, s32[]{:S(2)}) async-start(s8[6045696]{0:T(1024)(128)(4,1)} %bitcast.69), calls=%async_computation | async-start | bytes 8388608
  131.9 3.3 %slice-start.1 = ((s8[6045696]{0:T(1024)(128)(4,1)}), s8[1851392]{0:T(1024)(128)(4,1)S(1)}, s32[]{:S(2)}) async-start(s8[6045696]{0:T(1024)(128)(4,1)} %bitcast.69), calls=%async_computation.1 | async-start | bytes 3702784

commit v15 on v14

--- a/solution.py
+++ b/solution.py
@@ -28,8 +28,8 @@
 def _row_exchange_kernel(sizes, plan, *refs):
     (slab_offsets, block_rows, pad_l, width, pair_width, far, own_start,
      steps, pair_steps) = plan
-    band_ref, out_ref, pair_ref = refs[:3]
-    send_sem, recv_sem, pair_send, pair_recv, fwd_send, fwd_recv, local_sem, stage = refs[3:]
+    band_ref, moved_ref, out_ref, pair_ref = refs[:4]
+    send_sem, recv_sem, pair_send, pair_recv, fwd_send, fwd_recv, local_sem, stage = refs[4:]
     me = lax.axis_index("layer")
     core = lax.rem(me, 2)
     core_shift = 1 - 2 * core
@@ -39,22 +39,21 @@
     _greet(sizes, shifts + [(core_shift, 0)])
     mesh = pl.DeviceIdType.MESH
 
-    bs = band_ref.shape[2]
-
-    def window(j, start, count):
-        odd = lax.rem(start, 2)
+    bs = band_ref.shape[1]
+
+    def window(j, start, count, odd):
         first = pl.multiple_of((start - odd) * bs, 2 * bs)
-        return band_ref.at[odd, j, :, pl.ds(first, count * bs)]
-
-    def row_copy(j, start, count, dst, send, recv, target):
+        return (moved_ref if odd else band_ref).at[j, :, pl.ds(first, count * bs)]
+
+    def row_copy(j, start, count, dst, send, recv, target, odd):
         return pltpu.make_async_remote_copy(
-            src_ref=window(j, start, count), dst_ref=dst,
+            src_ref=window(j, start, count, odd), dst_ref=dst,
             send_sem=send, recv_sem=recv, device_id=target, device_id_type=mesh,
         )
 
     def group(dst_rows, count, send, recv, target):
         return pltpu.make_async_remote_copy(
-            src_ref=band_ref.at[0, pl.ds(0, dst_rows.shape[0]), :, pl.ds(0, count * bs)],
+            src_ref=band_ref.at[pl.ds(0, dst_rows.shape[0]), :, pl.ds(0, count * bs)],
             dst_ref=dst_rows, send_sem=send, recv_sem=recv, device_id=target,
             device_id_type=mesh,
         )
@@ -64,8 +63,9 @@
         target = _peer(sizes, 0, shift)
         for j in range(first, last):
             start = me * slab_offsets + block_rows * shift - j + pad_l
+            odd = (block_rows * shift - j + pad_l) % 2
             row_copy(j, start, width, out_ref.at[row_start + j - first],
-                     send_sem.at[k], recv_sem.at[k], target).start()
+                     send_sem.at[k], recv_sem.at[k], target, odd).start()
         waits.append(group(out_ref.at[pl.ds(row_start, last - first)], width,
                            send_sem.at[k], recv_sem.at[k], target))
     pair_base = (lax.rem(me + far, sizes[0]) - core) * slab_offsets
@@ -75,14 +75,21 @@
         for jj in range(half_rows):
             j = core * half_rows + jj
             start = pair_base + block_rows * shift - j + pad_l
-            copy = row_copy(j, start, pair_width, pair_ref.at[pair_start + j],
-                            pair_send.at[k * half_rows + jj], pair_recv.at[k * half_rows + jj],
-                            target)
-            copy.start()
-            pair_rows.append(copy)
+            sems = (pair_send.at[k * half_rows + jj], pair_recv.at[k * half_rows + jj])
+            for odd in (0, 1):
+                @pl.when(lax.rem(block_rows * shift - j + pad_l, 2) == odd)
+                def _():
+                    row_copy(j, start, pair_width, pair_ref.at[pair_start + j],
+                             *sems, target, odd).start()
+            pair_rows.append(pltpu.make_async_remote_copy(
+                src_ref=band_ref.at[j, :, pl.ds(0, pair_width * bs)],
+                dst_ref=pair_ref.at[pair_start + j], send_sem=sems[0], recv_sem=sems[1],
+                device_id=target, device_id_type=mesh,
+            ))
     for j in range(block_rows):
         start = me * slab_offsets - j + pad_l
-        pltpu.make_async_copy(window(j, start, width), stage.at[j], local_sem.at[0]).start()
+        odd = (pad_l - j) % 2
+        pltpu.make_async_copy(window(j, start, width, odd), stage.at[j], local_sem.at[0]).start()
     for jj in range(half_rows):
         for k, (shift, pair_start) in enumerate(pair_steps):
             pair_rows[k * half_rows + jj].wait_recv()
@@ -91,7 +98,7 @@
                 src_ref=held, dst_ref=held, send_sem=fwd_send.at[k], recv_sem=fwd_recv.at[k],
                 device_id=_peer(sizes, core_shift, 0), device_id_type=mesh,
             ).start()
-    pltpu.make_async_copy(band_ref.at[0, pl.ds(0, block_rows), :, pl.ds(0, width * bs)],
+    pltpu.make_async_copy(band_ref.at[pl.ds(0, block_rows), :, pl.ds(0, width * bs)],
                           stage, local_sem.at[0]).wait()
     own_out = pltpu.make_async_copy(stage, out_ref.at[pl.ds(own_start, block_rows)],
                                     local_sem.at[1])
@@ -107,17 +114,17 @@
     own_out.wait()
 
 
-def row_exchange(sizes, plan, total_rows, pair_rows, band):
+def row_exchange(sizes, plan, total_rows, pair_rows, band, moved):
     (slab_offsets, block_rows, pad_l, width, pair_width, far, own_start,
      steps, pair_steps) = plan
-    bs = band.shape[2]
+    bs = band.shape[1]
     any_spec = pl.BlockSpec(memory_space=pl.ANY)
     n, m = len(steps), len(pair_steps)
     return pl.pallas_call(
         lambda *refs: _row_exchange_kernel(sizes, plan, *refs),
         out_shape=(jax.ShapeDtypeStruct((total_rows, bs, width * bs), band.dtype),
                    jax.ShapeDtypeStruct((pair_rows, bs, pair_width * bs), band.dtype)),
-        in_specs=[any_spec],
+        in_specs=[any_spec, any_spec],
         out_specs=(any_spec, any_spec),
         scratch_shapes=[
             pltpu.SemaphoreType.DMA((n,)),
@@ -131,7 +138,7 @@
         ],
         compiler_params=pltpu.CompilerParams(collective_id=0, has_side_effects=True),
         name="row_exchange",
-    )(band)
+    )(band, moved)
 
 
 def _layer_gather_kernel(sizes, *refs):
@@ -248,8 +255,8 @@
     pad_r = total_blocks - offsets - pad_l
     band = jnp.pad(own_band.reshape(block_rows, bs, offsets * bs),
                    ((0, 0), (0, 0), (pad_l * bs, pad_r * bs)))
-    moved = jnp.pad(band[:, :, bs:], ((0, 0), (0, 0), (0, bs)))
-    band = jnp.stack([band, moved], axis=0)
+    moved = jnp.pad(own_band.reshape(block_rows, bs, offsets * bs),
+                    ((0, 0), (0, 0), ((pad_l - 1) * bs, (pad_r + 1) * bs)))
     core = lax.rem(layer_id, 2)
 
     below = half
@@ -276,7 +283,7 @@
     pair_steps = ((1, 0), (-1, block_rows))
     plan = (slab_offsets, block_rows, pad_l, width, pair_width, far, below,
             tuple(steps), pair_steps)
-    right, pair_buf = row_exchange(sizes, plan, total_rows, 2 * block_rows, band)
+    right, pair_buf = row_exchange(sizes, plan, total_rows, 2 * block_rows, band, moved)
     pair_part = lax.dynamic_slice_in_dim(pair_buf, core * slab_offsets * bs, width * bs, axis=2)
     right = lax.dynamic_update_slice_in_dim(right, pair_part[:block_rows], lower_start, axis=0)
     right = lax.dynamic_update_slice_in_dim(right, pair_part[block_rows:], upper_start, axis=0)

time: 142 us -> 142 us (level)
  other arithmetic: 9.72 us -> 4.37 us
  local copies, waits for them, and re-layouts: 24.2 us -> 29.3 us
    pad x0 -> x1, local copies, waits for them, and re-layouts: none -> 9.9 us  [body(): jnp.pad(own_band.reshape(block_rows, bs, offsets * bs), ((0, 0), (0, 0),...]
    another operation x1 -> x0, other arithmetic: 5.35 us -> none  [body(): band = jnp.stack([band, moved], axis=0)]
    slice x1 -> x0, local copies, waits for them, and re-layouts: 3.54 us -> none  [body(): moved = jnp.pad(band[:, :, bs:], ((0, 0), (0, 0), (0, bs)))]
where the time goes in v15:
time: 142 us
  Pallas kernels  98.2 us (69%)
  local copies, waits for them, and re-layouts  29.3 us (21%)
  matrix products  9.56 us (7%)
  other arithmetic  4.37 us (3%)
    pallas_call x1, Pallas kernels, row_exchange(): pl.pallas_call(lambda *refs: _row_exchange_kernel(sizes, plan, *refs), ou...  59.3 us
    pallas_call x2, Pallas kernels, layer_gather(): pl.pallas_call(lambda *refs: _layer_gather_kernel(sizes, *refs), out_shap...  38.8 us
    pad x1, local copies, waits for them, and re-layouts, body(): jnp.pad(own_band.reshape(block_rows, bs, offsets * bs), ((0, 0), (0, 0),...  9.9 us
    dot_general x2, matrix products, product(): dense = jnp.dot(left, right, preferred_element_type=jnp.float32)  9.56 us
    unnamed x50, local copies, waits for them, and re-layouts  4.06 us
    mul x2, local copies, waits for them, and re-layouts, product(): return out.reshape(block_rows, bs, slab_offsets, bs) * pattern_f  3.8 us

profile of v15, /device:TPU:1, one launch (start us, length us, event | category | flops | bytes accessed | tf_op | source)
XLA Modules:
  0.0 141.9 jit_solution(7722025370433137915)
XLA Ops:
  0.0 0.8 fusion.6
  0.8 0.1 copy.3
  0.9 0.3 mul.52
  1.1 0.8 mul.53
  1.9 0.0 copy-done.3
  1.9 1.0 mul.54.refs_0_
  2.9 20.0 %layer_gather.2 = bf16[640,2048]{1,0:T(8,128)(2,1)} custom-call(bf16[640,512]{1,0:T(8,128)(2,1)} %mul.54.refs_0_), custom_call_target="tpu_custom_call" | custom-call | tf_op jit(solution)/shard_map/layer_gather/pallas_call | solution.py:198
  23.0 0.0 copy-done.2
  23.0 1.0 constant_dynamic-update-slice_fusion.1
  23.9 9.9 %fusion.4 = (bf16[10,64,5504]{2,1,0:T(8,128)(2,1)}, bf16[10,64,5504]{2,1,0:T(8,128)(2,1)}) fusion(bf16[10,64,2048]{2,1,0:T(8,128)(2,1)} %bitcast.62), kind=kLoop, calls=%fused_computation.50 | loop fusion | bytes 16711680 | tf_op jit(solution)/shard_map/jit(_pad)/pad | solution.py:258
  33.8 59.3 %row_exchange.1 = (bf16[41,64,1152]{2,1,0:T(8,128)(2,1)}, bf16[20,64,1664]{2,1,0:T(8,128)(2,1)}) custom-call(bf16[10,64,5504]{2,1,0:T(8,128)(2,1)} %get-tuple-element.20.refs_0_, bf16[10,64,5504]{2,1,0:T(8,128)(2,1)} %get-tuple-element.19.refs_1_), custom_call_target="tpu_custom_call" | custom-call | tf_op jit(solution)/shard_map/row_exchange/pallas_call | solution.py:123
  93.2 0.0 copy-start
  93.2 2.8 %dynamic-slice_dynamic-update-slice_fusion.1 = bf16[41,64,1152]{2,1,0:T(8,128)(2,1)} fusion(bf16[41,64,1152]{2,1,0:T(8,128)(2,1)} %get-tuple-element.7, bf16[20,64,1664]{2,1,0:T(8,128)(2,1)} %get-tuple-element.8, s32[]{:T(128)S(6)} %select_n.8), kind=kLoop, calls=%fused_computation.1 | loop fusion | bytes 2949124 | tf_op jit(solution)/shard_map/dynamic_update_slice | solution.py:288
  96.0 2.6 %dynamic-slice_dynamic-update-slice_fusion = bf16[41,64,1152]{2,1,0:T(8,128)(2,1)} fusion(bf16[41,64,1152]{2,1,0:T(8,128)(2,1)} %dynamic-slice_dynamic-update-slice_fusion.1, bf16[20,64,1664]{2,1,0:T(8,128)(2,1)} %get-tuple-element.8, s32[]{:T(128)S(6)} %add.53, s32[]{:T(128)S(6)} %select_n.8), kind=kLoop, calls=%fused_computation | loop fusion | bytes 2949128 | tf_op jit(solution)/shard_map/dynamic_update_slice | solution.py:289
  98.6 0.2 fusion.5
  98.8 0.0 copy-start.4
  98.8 0.1 bitcast_dynamic-update-slice_fusion.18
  99.0 0.1 bitcast_dynamic-update-slice_fusion.16
  99.2 0.1 bitcast_dynamic-update-slice_fusion.14
  99.4 0.1 bitcast_dynamic-update-slice_fusion.12
  99.6 0.1 bitcast_dynamic-update-slice_fusion.10
  99.7 1.8 %copy-done.4 = bf16[41,64,1152]{2,1,0:T(8,128)(2,1)S(1)} copy-done((bf16[41,64,1152]{2,1,0:T(8,128)(2,1)S(1)}, bf16[41,64,1152]{2,1,0:T(8,128)(2,1)}, u32[]{:S(2)}) %copy-start.4) | copy-done | bytes 6045720
  101.5 4.8 %fusion.7 = f32[10,64,1152]{2,1,0:T(8,128)S(1)} fusion(bf16[10,64,2624]{2,1,0:T(8,128)(2,1)S(1)} %bitcast_dynamic-update-slice_fusion.10, bf16[2624,1152,1]{1,0,2:T(8,128)(2,1)S(1)} %bitcast.63), kind=kOutput, calls=%fused_computation.53 | convolution fusion | flops 3869245440 | bytes 12353536 | tf_op jit(solution)/shard_map/dot_general | solution.py:297
  106.3 0.1 slice_dynamic-update-slice_fusion.18
  106.4 0.1 slice_dynamic-update-slice_fusion.16
  106.5 0.1 slice_dynamic-update-slice_fusion.14
  106.7 0.1 slice_dynamic-update-slice_fusion.12
  106.8 0.1 slice_dynamic-update-slice_fusion.10
  106.9 0.1 copy.4
  107.0 1.8 %mul.57 = f32[10,64,8,64]{3,2,1,0:T(8,128)} broadcast(f32[10,8]{1,0:T(8,128)S(1)} %copy.4), dimensions={0,2} | broadcast | bytes 1311040 | tf_op jit(solution)/shard_map/mul | solution.py:302
  108.7 2.0 %mul.58 = f32[640,512]{1,0:T(8,128)S(1)} reshape(f32[10,64,8,64]{3,2,1,0:T(8,128)} %mul.57) | data formatting | bytes 2621440 | tf_op jit(solution)/shard_map/mul | solution.py:302
  110.8 1.1 fusion.2.refs_0_
  111.9 18.8 %layer_gather.3 = bf16[640,2048]{1,0:T(8,128)(2,1)} custom-call(bf16[640,512]{1,0:T(8,128)(2,1)} %fusion.2.refs_0_), custom_call_target="tpu_custom_call" | custom-call | tf_op jit(solution)/shard_map/layer_gather/pallas_call | solution.py:198
  130.7 0.0 slice-start
  130.7 0.9 constant_dynamic-update-slice_fusion
  131.7 2.4 %fusion.3 = (bf16[64,2048]{1,0:T(8,128)(2,1)S(1)}, bf16[64,2048]{1,0:T(8,128)(2,1)S(1)}, bf16[64,2048]{1,0:T(8,128)(2,1)S(1)}, bf16[64,2048]{1,0:T(8,128)(2,1)S(...) fusion(bf16[640,2048]{1,0:T(8,128)(2,1)} %constant_dynamic-upda, ...), kind=kLoop, calls=%fused_computation.49 | loop fusion | bytes 5242880 | tf_op jit(solution)/shard_map/slice | solution.py:223
  134.1 0.1 bitcast_dynamic-update-slice_fusion.8
  134.3 0.1 bitcast_dynamic-update-slice_fusion.6
  134.5 0.1 bitcast_dynamic-update-slice_fusion.4
  134.7 0.1 bitcast_dynamic-update-slice_fusion.2
  134.8 0.1 bitcast_dynamic-update-slice_fusion
  135.0 4.8 %fusion.8 = f32[10,64,1152]{2,1,0:T(8,128)S(1)} fusion(bf16[10,64,2624]{2,1,0:T(8,128)(2,1)S(1)} %bitcast_dynamic-update-slice_fusion, bf16[2624,1152,1]{1,0,2:T(8,128)(2,1)S(1)} %bitcast.66), kind=kOutput, calls=%fused_computation.54 | convolution fusion | flops 3869245440 | bytes 12353536 | tf_op jit(solution)/shard_map/dot_general | solution.py:297
  139.8 0.1 slice_dynamic-update-slice_fusion.8
  140.0 0.1 slice_dynamic-update-slice_fusion.6
  140.1 0.1 slice_dynamic-update-slice_fusion.4
  140.2 0.1 slice_dynamic-update-slice_fusion.2
  140.3 0.1 slice_dynamic-update-slice_fusion
  140.4 1.5 %fusion.1 = f32[640,512]{1,0:T(8,128)} fusion(f32[640,512]{1,0:T(8,128)S(1)} %mul.58, f32[10,64,512]{2,1,0:T(8,128)S(1)} %slice_dynamic-update-slice_fusion, bf16[640,512]{1,0:T(8,128)(2,1)S(1)} %copy-done.1), kind=kLoop, calls=%fused_computation.4 | loop fusion | flops 1638400 | bytes 4587520 | tf_op jit(solution)/shard_map/sub | solution.py:307
  (29 shorter events, 0.4 us)
Async XLA Ops:
  0.0 1.9 %copy-start.3 = (bf16[640,512]{1,0:T(8,128)(2,1)S(1)}, bf16[640,512]{1,0:T(8,128)(2,1)}, u32[]{:S(2)}) copy-start(bf16[640,512]{1,0:T(8,128)(2,1)} %param.2) | copy-start | bytes 1966084
  2.9 20.1 %copy-start.2 = (bf16[640,512]{1,0:T(8,128)(2,1)S(1)}, bf16[640,512]{1,0:T(8,128)(2,1)}, u32[]{:S(2)}) copy-start(bf16[640,512]{1,0:T(8,128)(2,1)} %mul.54.refs_0_) | copy-start | bytes 1966084
  93.2 5.4 %copy-start = (bf16[640,2048]{1,0:T(8,128)(2,1)S(1)}, bf16[640,2048]{1,0:T(8,128)(2,1)}, u32[]{:S(2)}) copy-start(bf16[640,2048]{1,0:T(8,128)(2,1)} %constant_dynamic-update-slice_fusion.1) | copy-start | bytes 7864324
  98.8 2.7 %copy-start.4 = (bf16[41,64,1152]{2,1,0:T(8,128)(2,1)S(1)}, bf16[41,64,1152]{2,1,0:T(8,128)(2,1)}, u32[]{:S(2)}) copy-start(bf16[41,64,1152]{2,1,0:T(8,128)(2,1)} %dynamic-slice_dynamic-update-slice_fusion) | copy-start | bytes 18137092
  111.9 18.8 %copy-start.1 = (bf16[640,512]{1,0:T(8,128)(2,1)S(1)}, bf16[640,512]{1,0:T(8,128)(2,1)}, u32[]{:S(2)}) copy-start(bf16[640,512]{1,0:T(8,128)(2,1)} %fusion.2.refs_0_) | copy-start | bytes 1966084
  130.7 4.3 %slice-start = ((s8[6045696]{0:T(1024)(128)(4,1)}), s8[4194304]{0:T(1024)(128)(4,1)S(1)}, s32[]{:S(2)}) async-start(s8[6045696]{0:T(1024)(128)(4,1)} %bitcast.64), calls=%async_computation | async-start | bytes 8388608
  131.7 3.3 %slice-start.1 = ((s8[6045696]{0:T(1024)(128)(4,1)}), s8[1851392]{0:T(1024)(128)(4,1)S(1)}, s32[]{:S(2)}) async-start(s8[6045696]{0:T(1024)(128)(4,1)} %bitcast.64), calls=%async_computation.1 | async-start | bytes 3702784

commit v16 on v15

--- a/solution.py
+++ b/solution.py
@@ -27,9 +27,10 @@
 
 def _row_exchange_kernel(sizes, plan, *refs):
     (slab_offsets, block_rows, pad_l, width, pair_width, far, own_start,
-     steps, pair_steps) = plan
+     steps, pair_steps, pair_dest) = plan
     band_ref, moved_ref, out_ref, pair_ref = refs[:4]
-    send_sem, recv_sem, pair_send, pair_recv, fwd_send, fwd_recv, local_sem, stage = refs[4:]
+    (send_sem, recv_sem, pair_send, pair_recv, fwd_send, fwd_recv, local_sem, stage,
+     pair_stage) = refs[4:]
     me = lax.axis_index("layer")
     core = lax.rem(me, 2)
     core_shift = 1 - 2 * core
@@ -111,12 +112,30 @@
         held = pair_ref.at[pl.ds(pair_start + core * half_rows, half_rows)]
         group(held, pair_width, fwd_send.at[k], fwd_recv.at[k],
               _peer(sizes, core_shift, 0)).wait()
+    cols = pl.ds(pl.multiple_of(core * slab_offsets * bs, 2 * bs), width * bs)
+    pair_count = 2 * half_rows
+    takes = []
+    for k, (shift, pair_start) in enumerate(pair_steps):
+        take = pltpu.make_async_copy(pair_ref.at[pl.ds(pair_start, pair_count), :, cols],
+                                     pair_stage.at[k], local_sem.at[2 + k])
+        take.start()
+        takes.append(take)
+    puts = []
+    for k in range(len(pair_steps)):
+        takes[k].wait()
+        put = pltpu.make_async_copy(pair_stage.at[k],
+                                    out_ref.at[pl.ds(pair_dest[k], pair_count)],
+                                    local_sem.at[2 + k])
+        put.start()
+        puts.append(put)
     own_out.wait()
+    for put in puts:
+        put.wait()
 
 
 def row_exchange(sizes, plan, total_rows, pair_rows, band, moved):
     (slab_offsets, block_rows, pad_l, width, pair_width, far, own_start,
-     steps, pair_steps) = plan
+     steps, pair_steps, pair_dest) = plan
     bs = band.shape[1]
     any_spec = pl.BlockSpec(memory_space=pl.ANY)
     n, m = len(steps), len(pair_steps)
@@ -133,8 +152,9 @@
             pltpu.SemaphoreType.DMA((m * (block_rows // 2),)),
             pltpu.SemaphoreType.DMA((m,)),
             pltpu.SemaphoreType.DMA((m,)),
-            pltpu.SemaphoreType.DMA((2,)),
+            pltpu.SemaphoreType.DMA((2 + m,)),
             pltpu.VMEM((block_rows, bs, width * bs), band.dtype),
+            pltpu.VMEM((m, 2 * (block_rows // 2), bs, width * bs), band.dtype),
         ],
         compiler_params=pltpu.CompilerParams(collective_id=0, has_side_effects=True),
         name="row_exchange",
@@ -282,11 +302,8 @@
         dist += 1
     pair_steps = ((1, 0), (-1, block_rows))
     plan = (slab_offsets, block_rows, pad_l, width, pair_width, far, below,
-            tuple(steps), pair_steps)
+            tuple(steps), pair_steps, (lower_start, upper_start))
     right, pair_buf = row_exchange(sizes, plan, total_rows, 2 * block_rows, band, moved)
-    pair_part = lax.dynamic_slice_in_dim(pair_buf, core * slab_offsets * bs, width * bs, axis=2)
-    right = lax.dynamic_update_slice_in_dim(right, pair_part[:block_rows], lower_start, axis=0)
-    right = lax.dynamic_update_slice_in_dim(right, pair_part[block_rows:], upper_start, axis=0)
     right = right.reshape(total_rows * bs, width * bs)
 
     pattern_f = pattern.astype(jnp.float32)[:, None, :, None]

time: 142 us -> 142 us (level)
  local copies, waits for them, and re-layouts: 29.3 us -> 23.4 us
  Pallas kernels: 98.2 us -> 101 us
  matrix products: 9.56 us -> 12.3 us
    dynamic_update_slice x2 -> x0, local copies, waits for them, and re-layouts: 5.39 us -> none  [the longest x1 2.78 us: body(): lax.dynamic_update_slice_in_dim(right, pair_part[:block_rows], lower_star...]
    pallas_call x1, Pallas kernels: 59.3 us -> 62.3 us  [row_exchange(): pl.pallas_call(lambda *refs: _row_exchange_kernel(sizes, plan, *refs), ou...]
    dot_general x2, matrix products: 9.56 us -> 12.3 us  [product(): dense = jnp.dot(left, right, preferred_element_type=jnp.float32)]
    pad x1, local copies, waits for them, and re-layouts: 9.9 us -> 7.72 us  [body(): jnp.pad(own_band.reshape(block_rows, bs, offsets * bs), ((0, 0), (0, 0),...]
    slice x2, local copies, waits for them, and re-layouts: 2.57 us -> 4.23 us  [skew_rows(): band[i]]
    unnamed x50 -> x52, local copies, waits for them, and re-layouts: 4.06 us -> 4.12 us
where the time goes in v16:
time: 142 us
  Pallas kernels  101 us (71%)
  local copies, waits for them, and re-layouts  23.4 us (16%)
  matrix products  12.3 us (9%)
  other arithmetic  4.39 us (3%)
    pallas_call x1, Pallas kernels, row_exchange(): pl.pallas_call(lambda *refs: _row_exchange_kernel(sizes, plan, *refs), ou...  62.3 us
    pallas_call x2, Pallas kernels, layer_gather(): pl.pallas_call(lambda *refs: _layer_gather_kernel(sizes, *refs), out_shap...  38.8 us
    dot_general x2, matrix products, product(): dense = jnp.dot(left, right, preferred_element_type=jnp.float32)  12.3 us
    pad x1, local copies, waits for them, and re-layouts, body(): jnp.pad(own_band.reshape(block_rows, bs, offsets * bs), ((0, 0), (0, 0),...  7.72 us
    slice x2, local copies, waits for them, and re-layouts, skew_rows(): band[i]  4.23 us
    unnamed x52, local copies, waits for them, and re-layouts  4.12 us
    mul x2, local copies, waits for them, and re-layouts, product(): return out.reshape(block_rows, bs, slab_offsets, bs) * pattern_f  3.79 us

profile of v16, /device:TPU:1, one launch (start us, length us, event | category | flops | bytes accessed | tf_op | source)
XLA Modules:
  0.0 141.7 jit_solution(1484010405891932842)
XLA Ops:
  0.0 0.8 fusion.6
  0.8 0.1 copy.3
  0.9 0.3 mul.48
  1.1 0.8 mul.49
  1.9 0.0 copy-done.3
  1.9 1.0 mul.50.refs_0_
  2.9 20.0 %layer_gather.2 = bf16[640,2048]{1,0:T(8,128)(2,1)} custom-call(bf16[640,512]{1,0:T(8,128)(2,1)} %mul.50.refs_0_), custom_call_target="tpu_custom_call" | custom-call | tf_op jit(solution)/shard_map/layer_gather/pallas_call | solution.py:218
  23.0 0.0 copy-done.2
  23.0 0.9 constant_dynamic-update-slice_fusion.1
  23.9 1.8 %fusion.5 = (bf16[64,2048]{1,0:T(8,128)(2,1)S(1)}, bf16[64,2048]{1,0:T(8,128)(2,1)S(1)}, bf16[64,2048]{1,0:T(8,128)(2,1)S(1)}, bf16[64,2048]{1,0:T(8,128)(2,1)S(...) fusion(bf16[640,2048]{1,0:T(8,128)(2,1)} %constant_dynamic-upda, ...), kind=kLoop, calls=%fused_computation.49 | loop fusion | bytes 5242880 | tf_op jit(solution)/shard_map/slice | solution.py:243
  25.8 0.0 copy-start
  25.8 0.1 bitcast_dynamic-update-slice_fusion.18
  26.0 0.1 bitcast_dynamic-update-slice_fusion.16
  26.2 0.1 bitcast_dynamic-update-slice_fusion.14
  26.4 0.1 bitcast_dynamic-update-slice_fusion.12
  26.6 0.1 bitcast_dynamic-update-slice_fusion.10
  26.7 0.0 copy-start.4
  26.7 1.8 %copy-done.4 = bf16[10,64,2624]{2,1,0:T(8,128)(2,1)} copy-done((bf16[10,64,2624]{2,1,0:T(8,128)(2,1)}, bf16[10,64,2624]{2,1,0:T(8,128)(2,1)S(1)}, u32[]{:S(2)}) %copy-start.4) | copy-done | bytes 3358744
  28.6 7.7 %fusion.4 = (bf16[10,64,5504]{2,1,0:T(8,128)(2,1)}, bf16[10,64,5504]{2,1,0:T(8,128)(2,1)}) fusion(bf16[10,64,2048]{2,1,0:T(8,128)(2,1)S(1)} %bitcast.62), kind=kLoop, calls=%fused_computation.48 | loop fusion | bytes 16711680 | tf_op jit(solution)/shard_map/jit(_pad)/pad | solution.py:278
  36.3 62.3 %row_exchange.1 = (bf16[41,64,1152]{2,1,0:T(8,128)(2,1)}, bf16[20,64,1664]{2,1,0:T(8,128)(2,1)}) custom-call(bf16[10,64,5504]{2,1,0:T(8,128)(2,1)} %get-tuple-element.18.refs_0_, bf16[10,64,5504]{2,1,0:T(8,128)(2,1)} %get-tuple-element.17.refs_1_), custom_call_target="tpu_custom_call" | custom-call | tf_op jit(solution)/shard_map/row_exchange/pallas_call | solution.py:142
  98.6 7.5 %fusion.7 = f32[10,64,1152]{2,1,0:T(8,128)S(1)} fusion(bf16[10,64,2624]{2,1,0:T(8,128)(2,1)S(1)} %copy-done.5, bf16[2624,1152,1]{1,0,2:T(8,128)(2,1)} %bitcast.63), kind=kOutput, calls=%fused_computation.51 | convolution fusion | flops 3869245440 | bytes 12353536 | tf_op jit(solution)/shard_map/dot_general | solution.py:314
  106.1 0.1 slice_dynamic-update-slice_fusion.18
  106.2 0.1 slice_dynamic-update-slice_fusion.16
  106.4 0.1 slice_dynamic-update-slice_fusion.14
  106.5 0.1 slice_dynamic-update-slice_fusion.12
  106.6 0.1 slice_dynamic-update-slice_fusion.10
  106.7 0.1 copy.4
  106.8 1.7 %mul.52 = f32[10,64,8,64]{3,2,1,0:T(8,128)} broadcast(f32[10,8]{1,0:T(8,128)S(1)} %copy.4), dimensions={0,2} | broadcast | bytes 1311040 | tf_op jit(solution)/shard_map/mul | solution.py:319
  108.5 2.0 %mul.53 = f32[640,512]{1,0:T(8,128)S(1)} reshape(f32[10,64,8,64]{3,2,1,0:T(8,128)} %mul.52) | data formatting | bytes 2621440 | tf_op jit(solution)/shard_map/mul | solution.py:319
  110.6 1.1 fusion.2.refs_0_
  111.7 18.8 %layer_gather.3 = bf16[640,2048]{1,0:T(8,128)(2,1)} custom-call(bf16[640,512]{1,0:T(8,128)(2,1)} %fusion.2.refs_0_), custom_call_target="tpu_custom_call" | custom-call | tf_op jit(solution)/shard_map/layer_gather/pallas_call | solution.py:218
  130.5 0.0 slice-start
  130.5 0.9 constant_dynamic-update-slice_fusion
  131.5 2.4 %fusion.3 = (bf16[64,2048]{1,0:T(8,128)(2,1)S(1)}, bf16[64,2048]{1,0:T(8,128)(2,1)S(1)}, bf16[64,2048]{1,0:T(8,128)(2,1)S(1)}, bf16[64,2048]{1,0:T(8,128)(2,1)S(...) fusion(bf16[640,2048]{1,0:T(8,128)(2,1)} %constant_dynamic-upda, ...), kind=kLoop, calls=%fused_computation.47 | loop fusion | bytes 5242880 | tf_op jit(solution)/shard_map/slice | solution.py:243
  133.9 0.1 bitcast_dynamic-update-slice_fusion.8
  134.1 0.1 bitcast_dynamic-update-slice_fusion.6
  134.3 0.1 bitcast_dynamic-update-slice_fusion.4
  134.5 0.1 bitcast_dynamic-update-slice_fusion.2
  134.7 0.1 bitcast_dynamic-update-slice_fusion
  134.8 0.0 slice-done
  134.8 0.0 slice-done.1
  134.8 4.8 %fusion.8 = f32[10,64,1152]{2,1,0:T(8,128)S(1)} fusion(bf16[10,64,2624]{2,1,0:T(8,128)(2,1)S(1)} %bitcast_dynamic-update-slice_fusion, bf16[2624,1152,1]{1,0,2:T(8,128)(2,1)S(1)} %bitcast.66), kind=kOutput, calls=%fused_computation.52 | convolution fusion | flops 3869245440 | bytes 12353536 | tf_op jit(solution)/shard_map/dot_general | solution.py:314
  139.6 0.1 slice_dynamic-update-slice_fusion.8
  139.8 0.1 slice_dynamic-update-slice_fusion.6
  139.9 0.1 slice_dynamic-update-slice_fusion.4
  140.0 0.1 slice_dynamic-update-slice_fusion.2
  140.1 0.1 slice_dynamic-update-slice_fusion
  140.2 1.5 %fusion.1 = f32[640,512]{1,0:T(8,128)} fusion(f32[640,512]{1,0:T(8,128)S(1)} %mul.53, f32[10,64,512]{2,1,0:T(8,128)S(1)} %slice_dynamic-update-slice_fusion, bf16[640,512]{1,0:T(8,128)(2,1)S(1)} %copy-done.1), kind=kLoop, calls=%fused_computation.2 | loop fusion | flops 1638400 | bytes 4587520 | tf_op jit(solution)/shard_map/sub | solution.py:324
  (29 shorter events, 0.4 us)
Async XLA Ops:
  0.0 1.9 %copy-start.3 = (bf16[640,512]{1,0:T(8,128)(2,1)S(1)}, bf16[640,512]{1,0:T(8,128)(2,1)}, u32[]{:S(2)}) copy-start(bf16[640,512]{1,0:T(8,128)(2,1)} %param.2) | copy-start | bytes 1966084
  2.9 20.1 %copy-start.2 = (bf16[640,512]{1,0:T(8,128)(2,1)S(1)}, bf16[640,512]{1,0:T(8,128)(2,1)}, u32[]{:S(2)}) copy-start(bf16[640,512]{1,0:T(8,128)(2,1)} %mul.50.refs_0_) | copy-start | bytes 1966084
  25.8 2.8 %copy-start = (bf16[640,2048]{1,0:T(8,128)(2,1)S(1)}, bf16[640,2048]{1,0:T(8,128)(2,1)}, u32[]{:S(2)}) copy-start(bf16[640,2048]{1,0:T(8,128)(2,1)} %constant_dynamic-update-slice_fusion.1) | copy-start | bytes 7864324
  26.7 1.8 %copy-start.4 = (bf16[10,64,2624]{2,1,0:T(8,128)(2,1)}, bf16[10,64,2624]{2,1,0:T(8,128)(2,1)S(1)}, u32[]{:S(2)}) copy-start(bf16[10,64,2624]{2,1,0:T(8,128)(2,1)S(1)} %bitcast_dynamic-update-slice_fusion.10) | copy-start | bytes 10076164
  36.3 62.3 %copy-start.5 = (bf16[10,64,2624]{2,1,0:T(8,128)(2,1)S(1)}, bf16[10,64,2624]{2,1,0:T(8,128)(2,1)}, u32[]{:S(2)}) copy-start(bf16[10,64,2624]{2,1,0:T(8,128)(2,1)} %copy-done.4) | copy-start | bytes 10076164
  111.7 18.8 %copy-start.1 = (bf16[640,512]{1,0:T(8,128)(2,1)S(1)}, bf16[640,512]{1,0:T(8,128)(2,1)}, u32[]{:S(2)}) copy-start(bf16[640,512]{1,0:T(8,128)(2,1)} %fusion.2.refs_0_) | copy-start | bytes 1966084
  130.5 4.3 %slice-start = ((s8[6045696]{0:T(1024)(128)(4,1)}), s8[4194304]{0:T(1024)(128)(4,1)S(1)}, s32[]{:S(2)}) async-start(s8[6045696]{0:T(1024)(128)(4,1)} %bitcast.64), calls=%async_computation | async-start | bytes 8388608
  131.5 3.3 %slice-start.1 = ((s8[6045696]{0:T(1024)(128)(4,1)}), s8[1851392]{0:T(1024)(128)(4,1)S(1)}, s32[]{:S(2)}) async-start(s8[6045696]{0:T(1024)(128)(4,1)} %bitcast.64), calls=%async_computation.1 | async-start | bytes 3702784

commit v17 on v15

--- a/solution.py
+++ b/solution.py
@@ -292,13 +292,24 @@
     pattern_f = pattern.astype(jnp.float32)[:, None, :, None]
 
     def product(left_band):
-        left = skew_rows(left_band.reshape(block_rows, bs, offsets * bs), block_rows - 1)
-        left = left.reshape(rows_dev, total_rows * bs)
-        dense = jnp.dot(left, right, preferred_element_type=jnp.float32)
-        dense = dense.reshape(block_rows, bs, width * bs)
-        out = jnp.stack(
-            [dense[i, :, i * bs: (i + slab_offsets) * bs] for i in range(block_rows)], axis=0
-        )
+        rows_band = left_band.reshape(block_rows, bs, offsets * bs)
+        group = block_rows // 2
+        k_blocks = group - 1 + offsets
+        n_blocks = group + slab_offsets
+        n_blocks += n_blocks % 2
+        pieces = []
+        for g in range(2):
+            first = g * group
+            col0 = min(first - first % 2, width - n_blocks)
+            left = skew_rows(rows_band[first:first + group], group - 1)
+            left = left.reshape(group * bs, k_blocks * bs)
+            part = right[first * bs:(first + k_blocks) * bs, col0 * bs:(col0 + n_blocks) * bs]
+            dense = jnp.dot(left, part, preferred_element_type=jnp.float32)
+            dense = dense.reshape(group, bs, n_blocks * bs)
+            for ii in range(group):
+                c = first + ii - col0
+                pieces.append(dense[ii, :, c * bs:(c + slab_offsets) * bs])
+        out = jnp.stack(pieces, axis=0)
         return out.reshape(block_rows, bs, slab_offsets, bs) * pattern_f
 
     square = product(own_band).astype(jnp.bfloat16)

time: 142 us -> 141 us (level)
    dot_general x2 -> x4, matrix products: 9.56 us -> 9.04 us  [product(): dense = jnp.dot(left, part, preferred_element_type=jnp.float32)]
    unnamed x50 -> x48, local copies, waits for them, and re-layouts: 4.06 us -> 3.86 us
where the time goes in v17:
time: 141 us; the launch traced here: 140 us
  Pallas kernels  98.1 us (70%)
  local copies, waits for them, and re-layouts  28.5 us (20%)
  matrix products  9.04 us (6%)
  other arithmetic  4.36 us (3%)
    pallas_call x1, Pallas kernels, row_exchange(): pl.pallas_call(lambda *refs: _row_exchange_kernel(sizes, plan, *refs), ou...  59.3 us
    pallas_call x2, Pallas kernels, layer_gather(): pl.pallas_call(lambda *refs: _layer_gather_kernel(sizes, *refs), out_shap...  38.8 us
    pad x1, local copies, waits for them, and re-layouts, body(): jnp.pad(own_band.reshape(block_rows, bs, offsets * bs), ((0, 0), (0, 0),...  9.9 us
    dot_general x4, matrix products, product(): dense = jnp.dot(left, part, preferred_element_type=jnp.float32)  9.04 us
    unnamed x48, local copies, waits for them, and re-layouts  3.86 us
    mul x2, local copies, waits for them, and re-layouts, product(): return out.reshape(block_rows, bs, slab_offsets, bs) * pattern_f  3.79 us

profile of v17, /device:TPU:1, one launch (start us, length us, event | category | flops | bytes accessed | tf_op | source)
XLA Modules:
  0.0 140.4 jit_solution(15621466753996865207)
XLA Ops:
  0.0 0.8 fusion.10
  0.8 0.1 copy.3
  0.9 0.2 mul.52
  1.1 0.8 mul.53
  1.9 0.1 copy-done.3
  2.0 1.0 mul.54.refs_0_
  3.0 20.0 %layer_gather.2 = bf16[640,2048]{1,0:T(8,128)(2,1)} custom-call(bf16[640,512]{1,0:T(8,128)(2,1)} %mul.54.refs_0_), custom_call_target="tpu_custom_call" | custom-call | tf_op jit(solution)/shard_map/layer_gather/pallas_call | solution.py:198
  23.0 0.0 copy-done.2
  23.0 1.0 constant_dynamic-update-slice_fusion.1
  24.0 9.9 %fusion.9 = (bf16[10,64,5504]{2,1,0:T(8,128)(2,1)}, bf16[10,64,5504]{2,1,0:T(8,128)(2,1)}) fusion(bf16[10,64,2048]{2,1,0:T(8,128)(2,1)} %bitcast.68), kind=kLoop, calls=%fused_computation.57 | loop fusion | bytes 16711680 | tf_op jit(solution)/shard_map/jit(_pad)/pad | solution.py:258
  33.9 59.3 %row_exchange.1 = (bf16[41,64,1152]{2,1,0:T(8,128)(2,1)}, bf16[20,64,1664]{2,1,0:T(8,128)(2,1)}) custom-call(bf16[10,64,5504]{2,1,0:T(8,128)(2,1)} %get-tuple-element.30.refs_0_, bf16[10,64,5504]{2,1,0:T(8,128)(2,1)} %get-tuple-element.29.refs_1_), custom_call_target="tpu_custom_call" | custom-call | tf_op jit(solution)/shard_map/row_exchange/pallas_call | solution.py:123
  93.2 2.6 %dynamic-slice_dynamic-update-slice_fusion.1 = bf16[41,64,1152]{2,1,0:T(8,128)(2,1)} fusion(bf16[41,64,1152]{2,1,0:T(8,128)(2,1)} %get-tuple-element.7, bf16[20,64,1664]{2,1,0:T(8,128)(2,1)} %get-tuple-element.8, s32[]{:T(128)S(6)} %select_n.8), kind=kLoop, calls=%fused_computation.7 | loop fusion | bytes 2949124 | tf_op jit(solution)/shard_map/dynamic_update_slice | solution.py:288
  95.8 2.7 %dynamic-slice_dynamic-update-slice_fusion = bf16[41,64,1152]{2,1,0:T(8,128)(2,1)} fusion(bf16[41,64,1152]{2,1,0:T(8,128)(2,1)} %dynamic-slice_dynamic-update-slice_fusion.1, bf16[20,64,1664]{2,1,0:T(8,128)(2,1)} %get-tuple-element.8, s32[]{:T(128)S(6)} %add.53, s32[]{:T(128)S(6)} %select_n.8), kind=kLoop, calls=%fused_computation.6 | loop fusion | bytes 2949128 | tf_op jit(solution)/shard_map/dynamic_update_slice | solution.py:289
  98.6 0.0 copy-done
  98.6 0.3 fusion.8
  98.9 0.1 bitcast_dynamic-update-slice_fusion.18
  99.1 0.1 bitcast_dynamic-update-slice_fusion.16
  99.3 0.1 bitcast_dynamic-update-slice_fusion.13
  99.5 0.1 bitcast_dynamic-update-slice_fusion.11
  99.7 1.6 %copy-done.4 = bf16[41,64,1152]{2,1,0:T(8,128)(2,1)S(1)} copy-done((bf16[41,64,1152]{2,1,0:T(8,128)(2,1)S(1)}, bf16[41,64,1152]{2,1,0:T(8,128)(2,1)}, u32[]{:S(2)}) %copy-start.4) | copy-done | bytes 6045720
  101.3 1.7 %fusion.3 = f32[5,64,896]{2,1,0:T(8,128)S(1)} fusion(bf16[5,64,2304]{2,1,0:T(8,128)(2,1)S(1)} %get-tuple-element.33, bf16[2624,1152]{1,0:T(8,128)(2,1)S(1)} %bitcast.70), kind=kOutput, calls=%fused_computation.5 | convolution fusion | flops 1321205760 | bytes 6750208 | tf_op jit(solution)/shard_map/dot_general | solution.py:307
  103.0 1.7 %fusion.1 = f32[5,64,896]{2,1,0:T(8,128)S(1)} fusion(bf16[5,64,2304]{2,1,0:T(8,128)(2,1)S(1)} %get-tuple-element.34, bf16[2624,1152]{1,0:T(8,128)(2,1)S(1)} %bitcast.71), kind=kOutput, calls=%fused_computation.3 | convolution fusion | flops 1321205760 | bytes 6750208 | tf_op jit(solution)/shard_map/dot_general | solution.py:307
  104.7 0.1 slice_dynamic-update-slice_fusion.18
  104.8 0.1 slice_dynamic-update-slice_fusion.16
  104.9 0.1 slice_dynamic-update-slice_fusion.14
  105.0 0.1 slice_dynamic-update-slice_fusion.12
  105.1 0.1 slice_dynamic-update-slice_fusion.10
  105.2 0.1 copy.4
  105.3 1.7 %mul.57 = f32[10,64,8,64]{3,2,1,0:T(8,128)} broadcast(f32[10,8]{1,0:T(8,128)S(1)} %copy.4), dimensions={0,2} | broadcast | bytes 1311040 | tf_op jit(solution)/shard_map/mul | solution.py:313
  107.1 2.0 %mul.58 = f32[640,512]{1,0:T(8,128)S(1)} reshape(f32[10,64,8,64]{3,2,1,0:T(8,128)} %mul.57) | data formatting | bytes 2621440 | tf_op jit(solution)/shard_map/mul | solution.py:313
  109.1 1.1 fusion.6.refs_0_
  110.3 18.8 %layer_gather.3 = bf16[640,2048]{1,0:T(8,128)(2,1)} custom-call(bf16[640,512]{1,0:T(8,128)(2,1)} %fusion.6.refs_0_), custom_call_target="tpu_custom_call" | custom-call | tf_op jit(solution)/shard_map/layer_gather/pallas_call | solution.py:198
  129.1 0.9 constant_dynamic-update-slice_fusion
  130.0 1.8 %fusion.7 = (bf16[64,2048]{1,0:T(8,128)(2,1)S(1)}, bf16[64,2048]{1,0:T(8,128)(2,1)S(1)}, bf16[64,2048]{1,0:T(8,128)(2,1)S(1)}, bf16[64,2048]{1,0:T(8,128)(2,1)S(...) fusion(bf16[640,2048]{1,0:T(8,128)(2,1)} %constant_dynamic-upda, ...), kind=kLoop, calls=%fused_computation.55 | loop fusion | bytes 5242880 | tf_op jit(solution)/shard_map/slice | solution.py:223
  131.9 0.1 bitcast_dynamic-update-slice_fusion.3
  132.1 0.1 bitcast_dynamic-update-slice_fusion.1
  132.2 0.0 slice-start
  132.3 0.0 slice-start.1
  132.3 4.0 %fusion.2 = f32[5,64,896]{2,1,0:T(8,128)S(1)} fusion(bf16[5,64,2304]{2,1,0:T(8,128)(2,1)S(1)} %bitcast_dynamic-update-slice_fusion, bf16[2624,1152]{1,0:T(8,128)(2,1)} %bitcast.69), kind=kOutput, calls=%fused_computation.4 | convolution fusion | flops 1321205760 | bytes 6750208 | tf_op jit(solution)/shard_map/dot_general | solution.py:307
  136.3 0.1 bitcast_dynamic-update-slice_fusion.8
  136.5 0.1 bitcast_dynamic-update-slice_fusion.6
  136.7 1.7 %fusion = f32[5,64,896]{2,1,0:T(8,128)S(1)} fusion(bf16[5,64,2304]{2,1,0:T(8,128)(2,1)S(1)} %bitcast_dynamic-update-slice_fusion.5, bf16[2624,1152]{1,0:T(8,128)(2,1)S(1)} %bitcast.74), kind=kOutput, calls=%fused_computation.2 | convolution fusion | flops 1321205760 | bytes 6750208 | tf_op jit(solution)/shard_map/dot_general | solution.py:307
  138.4 0.1 slice_dynamic-update-slice_fusion.8
  138.5 0.1 slice_dynamic-update-slice_fusion.6
  138.7 0.1 slice_dynamic-update-slice_fusion.4
  138.8 0.1 slice_dynamic-update-slice_fusion.2
  138.9 0.1 slice_dynamic-update-slice_fusion
  139.0 1.5 %fusion.5 = f32[640,512]{1,0:T(8,128)} fusion(f32[640,512]{1,0:T(8,128)S(1)} %mul.58, f32[10,64,512]{2,1,0:T(8,128)S(1)} %slice_dynamic-update-slice_fusion, bf16[640,512]{1,0:T(8,128)(2,1)S(1)} %copy-done.1), kind=kLoop, calls=%fused_computation.10 | loop fusion | flops 1638400 | bytes 4587520 | tf_op jit(solution)/shard_map/sub | solution.py:318
  (30 shorter events, 0.4 us)
Async XLA Ops:
  0.9 1.1 copy-start.3
  3.0 20.1 %copy-start.2 = (bf16[640,512]{1,0:T(8,128)(2,1)S(1)}, bf16[640,512]{1,0:T(8,128)(2,1)}, u32[]{:S(2)}) copy-start(bf16[640,512]{1,0:T(8,128)(2,1)} %mul.54.refs_0_) | copy-start | bytes 1966084
  95.8 2.8 %copy-start = (bf16[640,2048]{1,0:T(8,128)(2,1)S(1)}, bf16[640,2048]{1,0:T(8,128)(2,1)}, u32[]{:S(2)}) copy-start(bf16[640,2048]{1,0:T(8,128)(2,1)} %constant_dynamic-update-slice_fusion.1) | copy-start | bytes 7864324
  98.6 2.7 %copy-start.4 = (bf16[41,64,1152]{2,1,0:T(8,128)(2,1)S(1)}, bf16[41,64,1152]{2,1,0:T(8,128)(2,1)}, u32[]{:S(2)}) copy-start(bf16[41,64,1152]{2,1,0:T(8,128)(2,1)} %dynamic-slice_dynamic-update-slice_fusion) | copy-start | bytes 18137092
  110.3 18.8 %copy-start.1 = (bf16[640,512]{1,0:T(8,128)(2,1)S(1)}, bf16[640,512]{1,0:T(8,128)(2,1)}, u32[]{:S(2)}) copy-start(bf16[640,512]{1,0:T(8,128)(2,1)} %fusion.6.refs_0_) | copy-start | bytes 1966084
  132.2 4.5 %slice-start = ((s8[6045696]{0:T(1024)(128)(4,1)}), s8[4194304]{0:T(1024)(128)(4,1)S(1)}, s32[]{:S(2)}) async-start(s8[6045696]{0:T(1024)(128)(4,1)} %bitcast.72), calls=%async_computation | async-start | bytes 8388608
  132.3 4.4 %slice-start.1 = ((s8[6045696]{0:T(1024)(128)(4,1)}), s8[1851392]{0:T(1024)(128)(4,1)S(1)}, s32[]{:S(2)}) async-start(s8[6045696]{0:T(1024)(128)(4,1)} %bitcast.72), calls=%async_computation.1 | async-start | bytes 3702784

commit v18 on v17

--- a/solution.py
+++ b/solution.py
@@ -293,12 +293,12 @@
 
     def product(left_band):
         rows_band = left_band.reshape(block_rows, bs, offsets * bs)
-        group = block_rows // 2
+        group = 2 if block_rows % 2 == 0 else block_rows
         k_blocks = group - 1 + offsets
         n_blocks = group + slab_offsets
         n_blocks += n_blocks % 2
         pieces = []
-        for g in range(2):
+        for g in range(block_rows // group):
             first = g * group
             col0 = min(first - first % 2, width - n_blocks)
             left = skew_rows(rows_band[first:first + group], group - 1)

time: 141 us -> 143 us (1.014)
    another operation x3 -> x15, local copies, waits for them, and re-layouts: 0.08 us -> 1.53 us  [skew_rows(): return jnp.stack(pieces, axis=0)]
    dot_general x4 -> x10, matrix products: 9.04 us -> 10.1 us  [product(): dense = jnp.dot(left, part, preferred_element_type=jnp.float32)]
    unnamed x48 -> x32, local copies, waits for them, and re-layouts: 3.86 us -> 3.39 us
where the time goes in v18:
time: 143 us
  Pallas kernels  98.1 us (69%)
  local copies, waits for them, and re-layouts  29.6 us (21%)
  matrix products  10.1 us (7%)
  other arithmetic  4.36 us (3%)
    pallas_call x1, Pallas kernels, row_exchange(): pl.pallas_call(lambda *refs: _row_exchange_kernel(sizes, plan, *refs), ou...  59.3 us
    pallas_call x2, Pallas kernels, layer_gather(): pl.pallas_call(lambda *refs: _layer_gather_kernel(sizes, *refs), out_shap...  38.8 us
    dot_general x10, matrix products, product(): dense = jnp.dot(left, part, preferred_element_type=jnp.float32)  10.1 us
    pad x1, local copies, waits for them, and re-layouts, body(): jnp.pad(own_band.reshape(block_rows, bs, offsets * bs), ((0, 0), (0, 0),...  9.89 us
    mul x2, local copies, waits for them, and re-layouts, product(): return out.reshape(block_rows, bs, slab_offsets, bs) * pattern_f  3.79 us
    unnamed x32, local copies, waits for them, and re-layouts  3.39 us

profile of v18, /device:TPU:1, one launch (start us, length us, event | category | flops | bytes accessed | tf_op | source)
XLA Modules:
  0.0 142.6 jit_solution(16081061790366522969)
XLA Ops:
  0.0 0.8 fusion.56
  0.9 0.3 mul.52
  1.1 0.8 mul.53
  1.9 0.3 copy-done.3
  2.2 1.0 mul.54.refs_0_
  3.2 20.0 %layer_gather.2 = bf16[640,2048]{1,0:T(8,128)(2,1)} custom-call(bf16[640,512]{1,0:T(8,128)(2,1)} %mul.54.refs_0_), custom_call_target="tpu_custom_call" | custom-call | tf_op jit(solution)/shard_map/layer_gather/pallas_call | solution.py:198
  23.3 1.0 constant_dynamic-update-slice_fusion.1
  24.3 9.9 %fusion.55 = (bf16[10,64,5504]{2,1,0:T(8,128)(2,1)}, bf16[10,64,5504]{2,1,0:T(8,128)(2,1)}) fusion(bf16[10,64,2048]{2,1,0:T(8,128)(2,1)} %bitcast.76), kind=kLoop, calls=%fused_computation.106 | loop fusion | bytes 16711680 | tf_op jit(solution)/shard_map/jit(_pad)/pad | solution.py:258
  34.2 59.3 %row_exchange.1 = (bf16[41,64,1152]{2,1,0:T(8,128)(2,1)}, bf16[20,64,1664]{2,1,0:T(8,128)(2,1)}) custom-call(bf16[10,64,5504]{2,1,0:T(8,128)(2,1)} %get-tuple-element.30.refs_0_, bf16[10,64,5504]{2,1,0:T(8,128)(2,1)} %get-tuple-element.29.refs_1_), custom_call_target="tpu_custom_call" | custom-call | tf_op jit(solution)/shard_map/row_exchange/pallas_call | solution.py:123
  93.4 2.6 %dynamic-slice_dynamic-update-slice_fusion.1 = bf16[41,64,1152]{2,1,0:T(8,128)(2,1)} fusion(bf16[41,64,1152]{2,1,0:T(8,128)(2,1)} %get-tuple-element.7, bf16[20,64,1664]{2,1,0:T(8,128)(2,1)} %get-tuple-element.8, s32[]{:T(128)S(6)} %select_n.8), kind=kLoop, calls=%fused_computation.16 | loop fusion | bytes 2949124 | tf_op jit(solution)/shard_map/dynamic_update_slice | solution.py:288
  96.1 2.8 %dynamic-slice_dynamic-update-slice_fusion = bf16[41,64,1152]{2,1,0:T(8,128)(2,1)} fusion(bf16[41,64,1152]{2,1,0:T(8,128)(2,1)} %dynamic-slice_dynamic-update-slice_fusion.1, bf16[20,64,1664]{2,1,0:T(8,128)(2,1)} %get-tuple-element.8, s32[]{:T(128)S(6)} %add.53, s32[]{:T(128)S(6)} %select_n.8), kind=kLoop, calls=%fused_computation.15 | loop fusion | bytes 2949128 | tf_op jit(solution)/shard_map/dynamic_update_slice | solution.py:289
  98.8 0.3 fusion.54
  99.2 0.1 pad_bitcast_fusion.10
  99.3 2.2 %copy-done.4 = bf16[41,64,1152]{2,1,0:T(8,128)(2,1)S(1)} copy-done((bf16[41,64,1152]{2,1,0:T(8,128)(2,1)S(1)}, bf16[41,64,1152]{2,1,0:T(8,128)(2,1)}, u32[]{:S(2)}) %copy-start.4) | copy-done | bytes 6045720
  101.5 0.6 fusion.9
  102.2 0.1 pad_bitcast_fusion.12
  102.3 0.6 fusion.7
  103.0 0.1 pad_bitcast_fusion.14
  103.1 0.6 fusion.5
  103.8 0.1 pad_bitcast_fusion.16
  103.9 0.6 fusion.3
  104.6 0.1 pad_bitcast_fusion.18
  104.7 0.6 fusion.1
  105.4 0.1 slice_dynamic-update-slice_fusion.18
  105.5 0.1 slice_dynamic-update-slice_fusion.16
  105.6 0.1 slice_dynamic-update-slice_fusion.14
  105.8 0.1 slice_dynamic-update-slice_fusion.12
  105.9 0.1 slice_dynamic-update-slice_fusion.10
  106.1 1.7 %mul.57 = f32[10,64,8,64]{3,2,1,0:T(8,128)} broadcast(f32[10,8]{1,0:T(8,128)S(1)} %copy.4), dimensions={0,2} | broadcast | bytes 1311040 | tf_op jit(solution)/shard_map/mul | solution.py:313
  107.8 2.0 %mul.58 = f32[640,512]{1,0:T(8,128)S(1)} reshape(f32[10,64,8,64]{3,2,1,0:T(8,128)} %mul.57) | data formatting | bytes 2621440 | tf_op jit(solution)/shard_map/mul | solution.py:313
  109.9 1.1 fusion.12.refs_0_
  111.0 18.8 %layer_gather.3 = bf16[640,2048]{1,0:T(8,128)(2,1)} custom-call(bf16[640,512]{1,0:T(8,128)(2,1)} %fusion.12.refs_0_), custom_call_target="tpu_custom_call" | custom-call | tf_op jit(solution)/shard_map/layer_gather/pallas_call | solution.py:198
  129.8 0.9 constant_dynamic-update-slice_fusion
  130.8 2.0 %fusion.53 = (bf16[64,2048]{1,0:T(8,128)(2,1)S(1)}, bf16[64,2048]{1,0:T(8,128)(2,1)S(1)}, bf16[64,2048]{1,0:T(8,128)(2,1)S(1)}, bf16[64,2048]{1,0:T(8,128)(2,1)S...) fusion(bf16[640,2048]{1,0:T(8,128)(2,1)} %constant_dynamic-upda, ...), kind=kLoop, calls=%fused_computation.104 | loop fusion | bytes 5242880 | tf_op jit(solution)/shard_map/slice | solution.py:223
  132.7 0.1 pad_bitcast_fusion
  132.9 2.6 %fusion.8 = f32[2,64,640]{2,1,0:T(8,128)S(1)} fusion(bf16[2624,1152]{1,0:T(8,128)(2,1)} %bitcast.77, bf16[1,64,2112]{2,1,0:T(8,128)(2,1)S(1)} %pad_bitcast_fusion, bf16[1,64,2112]{2,1,0:T(8,128)(2,1)S(1)} %pad_bitcast_fusion.1), kind=kOutput, calls=%fused_computation.13 | convolution fusion | flops 346300416 | bytes 3571712 | tf_op jit(solution)/shard_map/dot_general | solution.py:307
  135.5 0.1 pad_bitcast_fusion.2
  135.7 2.4 %fusion.6 = f32[2,64,640]{2,1,0:T(8,128)S(1)} fusion(bf16[2624,1152]{1,0:T(8,128)(2,1)} %bitcast.78, bf16[1,64,2112]{2,1,0:T(8,128)(2,1)S(1)} %pad_bitcast_fusion.2, bf16[1,64,2112]{2,1,0:T(8,128)(2,1)S(1)} %pad_bitcast_fusion.3), kind=kOutput, calls=%fused_computation.11 | convolution fusion | flops 346300416 | bytes 3571712 | tf_op jit(solution)/shard_map/dot_general | solution.py:307
  138.1 0.1 pad_bitcast_fusion.4
  138.3 0.6 fusion.4
  138.9 0.1 pad_bitcast_fusion.6
  139.1 0.6 fusion.2
  139.8 0.1 pad_bitcast_fusion.8
  139.9 0.6 fusion
  140.6 0.1 slice_dynamic-update-slice_fusion.8
  140.7 0.1 slice_dynamic-update-slice_fusion.6
  140.8 0.1 slice_dynamic-update-slice_fusion.4
  141.2 1.5 %fusion.11 = f32[640,512]{1,0:T(8,128)} fusion(f32[640,512]{1,0:T(8,128)S(1)} %mul.58, f32[10,64,512]{2,1,0:T(8,128)S(1)} %slice_dynamic-update-slice_fusion, bf16[640,512]{1,0:T(8,128)(2,1)S(1)} %copy-done.1), kind=kLoop, calls=%fused_computation.19 | loop fusion | flops 1638400 | bytes 4587520 | tf_op jit(solution)/shard_map/sub | solution.py:318
  (32 shorter events, 0.6 us)
Async XLA Ops:
  1.1 1.1 copy-start.3
  3.2 20.1 %copy-start.2 = (bf16[640,512]{1,0:T(8,128)(2,1)S(1)}, bf16[640,512]{1,0:T(8,128)(2,1)}, u32[]{:S(2)}) copy-start(bf16[640,512]{1,0:T(8,128)(2,1)} %mul.54.refs_0_) | copy-start | bytes 1966084
  96.1 2.8 %copy-start = (bf16[640,2048]{1,0:T(8,128)(2,1)S(1)}, bf16[640,2048]{1,0:T(8,128)(2,1)}, u32[]{:S(2)}) copy-start(bf16[640,2048]{1,0:T(8,128)(2,1)} %constant_dynamic-update-slice_fusion.1) | copy-start | bytes 7864324
  98.8 2.7 %copy-start.4 = (bf16[41,64,1152]{2,1,0:T(8,128)(2,1)S(1)}, bf16[41,64,1152]{2,1,0:T(8,128)(2,1)}, u32[]{:S(2)}) copy-start(bf16[41,64,1152]{2,1,0:T(8,128)(2,1)} %dynamic-slice_dynamic-update-slice_fusion) | copy-start | bytes 18137092
  111.0 18.8 %copy-start.1 = (bf16[640,512]{1,0:T(8,128)(2,1)S(1)}, bf16[640,512]{1,0:T(8,128)(2,1)}, u32[]{:S(2)}) copy-start(bf16[640,512]{1,0:T(8,128)(2,1)} %fusion.12.refs_0_) | copy-start | bytes 1966084
  130.7 7.5 %slice-start = ((s8[6045696]{0:T(1024)(128)(4,1)}), s8[1851392]{0:T(1024)(128)(4,1)S(1)}, s32[]{:S(2)}) async-start(s8[6045696]{0:T(1024)(128)(4,1)} %bitcast.84), calls=%async_computation | async-start | bytes 3702784
  132.9 5.4 %slice-start.1 = ((s8[6045696]{0:T(1024)(128)(4,1)}), s8[4194304]{0:T(1024)(128)(4,1)S(1)}, s32[]{:S(2)}) async-start(s8[6045696]{0:T(1024)(128)(4,1)} %bitcast.84), calls=%async_computation.1 | async-start | bytes 8388608
